TPU v7x, 32 devices: a whole 2x2x4 slice. The times are simulated.
32 devices in a mesh: parts: 2 (over x), grp: 2 (over core), row: 8 (over z, y).
Axes of the slice: x: 2, y: 2, z: 4, core: 2. Of those that a mesh axis runs over, the one named last changes fastest.
Arguments:
- design: bfloat16 [8192, 1024], P(('parts', 'grp', 'row')), parts along dimension 0, may hold values from -6 to 6
- target: float32 [8192], P(('parts', 'grp', 'row')), parts along dimension 0, may hold values from -6 to 6
- coeffs: bfloat16 [2048], P('parts'), parts along dimension 0, may hold values from -0.1875 to 0.1875
- tau_level: int32 [64], P(('parts', 'grp', 'row')), parts along dimension 0, may hold values from 0 to 3
- bucket: int32 [8192], P(('parts', 'grp', 'row')), parts along dimension 0, may hold values from 0 to 63
- sign_bit: int32 [8192], P(('parts', 'grp', 'row')), parts along dimension 0, may hold values from 0 to 1
- panel_order: int32 [16], P('parts'), parts along dimension 0, may hold values from 0 to 7, each once
Outputs:
- rotated: float32 [2048, 1024], P(('parts', 'grp'), 'row'), parts along dimension 0
There are 2 independent parts, one for each index of `parts`. A program takes and returns all parts, laid end to end along the dimension named above; each array names one. Nothing has to cross between parts.
Inputs may be any that keep to these rules, and one draw needn't show every extreme that they name: `panel_order`: each of 0 to 7 once.
All inputs are finite; a program needn't handle non-finite values. Where the computation divides by a largest or mean magnitude, that divisor is 1e-20 or more.
Results may differ from a plain program's by a relative error of at most 0.0044.
Values may be sent and summed in bfloat16 or wider, within the bound.
No kernel may reach another device: no remote copies, remote signals or barrier semaphores. Data moves between devices by JAX's collectives and lax.ppermute only.
A program may use at most 64 MiB of HBM per device.

v0:
```python
import functools

import jax
import jax.numpy as jnp
from jax import lax
from jax.experimental import pallas as pl
from jax.experimental.pallas import tpu as pltpu
from jax.sharding import PartitionSpec as P

PANEL = 128
KB = 64
ROUNDS = 5
NS_ITERS = 4
GATHER_BYTES = 12 << 20


def swapped(block, axis, bit):
    count = lax.axis_size(axis)
    route = []
    for low in range(count):
        high = low | 1 << bit
        if high != low and high < count:
            route += [(low, high), (high, low)]
    return lax.ppermute(block, axis, route)


def sketch_kernel(design_hbm, target_hbm, coeffs_hbm, level_ref, bucket_hbm, sign_hbm, out_ref,
                  design_ref, target_ref, coeffs_ref, bucket_ref, sign_ref, arrived):
    copies = [
        pltpu.make_async_copy(source, here, arrived.at[i])
        for i, (source, here) in enumerate(
            [
                (coeffs_hbm, coeffs_ref),
                (design_hbm, design_ref),
                (target_hbm, target_ref),
                (bucket_hbm, bucket_ref),
                (sign_hbm, sign_ref),
            ]
        )
    ]
    for copy in copies:
        copy.start()
    for copy in copies:
        copy.wait()
    rows = design_ref.shape[0]
    design = design_ref[...]
    fitted = lax.dot_general(
        coeffs_ref[...].reshape(1, -1),
        design,
        (((1,), (1,)), ((), ())),
        preferred_element_type=jnp.float32,
    )
    residual = target_ref[...].reshape(1, rows) - fitted
    blocks = level_ref.shape[0]
    lane = lax.broadcasted_iota(jnp.int32, (1, rows), 1)
    level = jnp.full((1, rows), level_ref[0], jnp.int32)
    for block in range(1, blocks):
        level = jnp.where(lane >= block * (rows // blocks), level_ref[block], level)
    quantile = 0.1 + 0.25 * level.astype(jnp.float32)
    upper = jax.nn.sigmoid(residual / 0.2)
    weight = (quantile * upper + (1.0 - quantile) * (1.0 - upper)) / jnp.sqrt(
        residual * residual + 0.25
    )
    sign = 2.0 * sign_ref[...].reshape(1, rows).astype(jnp.float32) - 1.0
    signed = (sign * jnp.sqrt(weight)).astype(jnp.bfloat16).astype(jnp.float32)
    slots = lax.broadcasted_iota(jnp.int32, (KB, rows), 0)
    embed = jnp.where(slots == bucket_ref[...].reshape(1, rows), signed, 0.0).astype(jnp.bfloat16)
    out_ref[...] = jnp.dot(embed, design, preferred_element_type=jnp.float32).astype(jnp.bfloat16)


def sketch_local(design, target, coeffs, tau_level, bucket, sign_bit):
    rows, columns = design.shape
    anywhere = pl.BlockSpec(memory_space=pltpu.HBM)
    return pl.pallas_call(
        sketch_kernel,
        out_shape=jax.ShapeDtypeStruct((KB, columns), jnp.bfloat16),
        in_specs=[anywhere] * 3 + [pl.BlockSpec(memory_space=pltpu.SMEM)] + [anywhere] * 2,
        out_specs=pl.BlockSpec(memory_space=pltpu.VMEM),
        scratch_shapes=[
            pltpu.VMEM((rows, columns), jnp.bfloat16),
            pltpu.VMEM((rows,), jnp.float32),
            pltpu.VMEM((columns,), jnp.bfloat16),
            pltpu.VMEM((rows,), jnp.int32),
            pltpu.VMEM((rows,), jnp.int32),
            pltpu.SemaphoreType.DMA((5,)),
        ],
        compiler_params=pltpu.CompilerParams(vmem_limit_bytes=67043328),
    )(design, target, coeffs, tau_level, bucket, sign_bit)


def half(block):
    return block.astype(jnp.bfloat16)


def mul(left, right):
    return jnp.dot(left, right, preferred_element_type=jnp.float32)


def diagonal_mask(width):
    rows = lax.broadcasted_iota(jnp.int32, (width, width), 0)
    columns = lax.broadcasted_iota(jnp.int32, (width, width), 1)
    return rows == columns


def root_factors(grams, offs):
    w, t, x, z = [], [], [], []
    for gram, off in zip(grams, offs):
        bound = jnp.max(jnp.sum(jnp.abs(gram), axis=0, keepdims=True), axis=1, keepdims=True)
        w.append(1.0 / bound)
        t.append(1.5 - 0.5 * w[-1])
        x.append((-0.5 * w[-1] / t[-1]) * off)
        z.append(t[-1] * lax.rsqrt(bound))
    xs, halves = [x], [[half(a) for a in x]]
    for _ in range(NS_ITERS - 1):
        thin = halves[-1]
        after = [1.5 - 0.5 * a * a * b for a, b in zip(t, w)]
        gain = [a * a * a / b for a, b in zip(t, after)]
        linear = [g * (1.0 - b / a) for g, a, b in zip(gain, t, w)]
        square = [g * (2.0 - 0.5 * b / a) for g, a, b in zip(gain, t, w)]
        inner = [
            half(q * a + g * mul(b, b)) for q, g, a, b in zip(square, gain, x, thin)
        ]
        x = [p * a + mul(r, b) for p, a, b, r in zip(linear, x, thin, inner)]
        w = [a * a * b for a, b in zip(t, w)]
        t = after
        z = [a * b for a, b in zip(z, t)]
        xs.append(x)
        halves.append([half(a) for a in x])
    while len(xs) > 1:
        merged, thinner = [], []
        for k in range(0, len(xs) - 1, 2):
            merged.append(
                [
                    a + b + mul(d, c)
                    for a, b, c, d in zip(xs[k], xs[k + 1], halves[k], halves[k + 1])
                ]
            )
            thinner.append([half(a) for a in merged[-1]])
        if len(xs) % 2:
            merged.append(xs[-1])
            thinner.append(halves[-1])
        xs, halves = merged, thinner
    return list(zip(z, xs[0], halves[0]))


def diagonal_of(block, axis):
    return jnp.sum(jnp.where(diagonal_mask(block.shape[0]), block, 0.0), axis=axis, keepdims=True)


def ring_place(index, count):
    return jnp.where(index % 2 == 0, index // 2, count - 1 - index // 2)


def ring_index(place, count):
    return jnp.where(place < count // 2, 2 * place, 2 * (count - 1 - place) + 1)


def ring_origins(count):
    here = ring_place(lax.axis_index("row"), count)
    turns = [0] + [step for k in range(1, count // 2) for step in (-k, k)] + [count // 2]
    return [ring_index((here + turn + count) % count, count) for turn in turns]


def panel_columns(order_ref, count):
    position = lax.axis_index("row")
    return [
        pl.multiple_of(order_ref[jnp.bitwise_xor(position, j)] * PANEL, PANEL)
        for j in range(count)
    ]


def gather_panels(columns, chunks, ordered_ref, turned_ref):
    start = 0
    for chunk in chunks:
        rows = chunk.shape[0]
        for j, column in enumerate(columns):
            ordered_ref[start : start + rows, j * PANEL : (j + 1) * PANEL] = chunk[
                :, pl.ds(column, PANEL)
            ]
        start += rows
    for p in range(0, len(columns), 2):
        span = slice(p * PANEL, (p + 2) * PANEL)
        turned_ref[span] = ordered_ref[:, span].T


def tall_gram(turned_ref, ordered_ref, b):
    return mul(turned_ref[: (b + 2) * PANEL], ordered_ref[:, b * PANEL : (b + 2) * PANEL])


def gram_kernel(count, pieces, order_ref, *refs):
    chunks, (ordered_ref, *tall_refs), turned_ref = refs[:pieces], refs[pieces:-1], refs[-1]
    gather_panels(panel_columns(order_ref, count), chunks, ordered_ref, turned_ref)
    for k, tall_ref in enumerate(tall_refs):
        tall_ref[...] = tall_gram(turned_ref, ordered_ref, 2 * k)


def rounds_kernel(count, pieces, order_ref, *refs):
    chunks, refs = refs[:pieces], refs[pieces:]
    early_ref, tall_refs = refs[0], refs[1 : 1 + count // 2]
    out_ref, ordered_ref, turned_ref = refs[1 + count // 2 :]
    width = PANEL
    depth = count.bit_length() - 1
    gather_panels(panel_columns(order_ref, count), chunks, ordered_ref, turned_ref)

    live = [None] * (ROUNDS + 1)
    live[ROUNDS] = [0]
    for turn in reversed(range(ROUNDS)):
        bit = 1 << turn % depth
        live[turn] = sorted({a for p in live[turn + 1] for a in (p, p ^ bit)})

    row_scale, column_scale, total, grams = {}, {}, {}, {}
    for b in range(0, count, 2):
        tall = tall_refs[b // 2][...] + tall_gram(turned_ref, ordered_ref, b)
        for i in range(b + 2):
            for j in range(2):
                if i <= b + j:
                    grams[i, b + j] = tall[
                        i * width : (i + 1) * width, j * width : (j + 1) * width
                    ]
    for p in range(count):
        total[p] = diagonal_of(grams[p, p], 0)
        row_scale[p] = lax.rsqrt(total[p])
        column_scale[p] = lax.rsqrt(diagonal_of(grams[p, p], 1))
    first_scale = dict(column_scale)
    blocks = {
        (a, b): column_scale[a] * gram * row_scale[b] for (a, b), gram in grams.items()
    }
    eye = diagonal_mask(width)

    def joined_from(blocks):
        def joined(left, right, corner=lambda block: block):
            def block_of(a, b):
                if a == b:
                    return corner(blocks[a, a])
                return blocks[a, b] if (a, b) in blocks else blocks[b, a].T

            return jnp.concatenate(
                [jnp.concatenate([block_of(a, b) for b in right], axis=1) for a in left], axis=0
            )

        return joined

    history = []
    finish = None
    for turn in range(ROUNDS):
        bit = 1 << turn % depth
        pairs = [(p, p | bit) for p in live[turn] if not p & bit]
        joined = joined_from(blocks)
        whole = [joined(pair, pair) for pair in pairs]
        offs = [
            joined(pair, pair, lambda block: jnp.where(eye, 0.0, block)) for pair in pairs
        ]
        factors = root_factors(whole, offs)
        if finish is not None:
            finish()
        keep = live[turn + 1]
        scales = {}
        if turn + 1 < ROUNDS:
            kept = [[i for i in range(2) if pair[i] in keep] for pair in pairs]
            spans = [
                slice(k[0] * width, (k[-1] + 1) * width) for k in kept
            ]
            fresh, row_scale, column_scale = {}, {}, {}
            for i, pair in enumerate(pairs):
                z, e, thin = factors[i]
                span = spans[i]
                part = offs[i][span] + e[span] + mul(thin[span], half(offs[i]))
                value = part[:, span] + e[span, span] + mul(half(part), thin[:, span])
                for k, at in enumerate(kept[i]):
                    cut = slice(k * width, (k + 1) * width)
                    block = value[cut, cut] + jnp.where(eye, 1.0, 0.0)
                    along = diagonal_of(block, 0)
                    row_scale[pair[at]] = lax.rsqrt(along)
                    column_scale[pair[at]] = lax.rsqrt(diagonal_of(block, 1))
                    total[pair[at]] = total[pair[at]] * along * z * z
                    fresh[pair[at], pair[at]] = block
                    for j, to in list(enumerate(kept[i]))[k + 1 :]:
                        fresh[pair[at], pair[to]] = value[cut, j * width : (j + 1) * width]
            following = 1 << (turn + 1) % depth
            soon, later = [], []
            for j in range(1, len(pairs)):
                near = [
                    i
                    for i in range(j)
                    if any(a ^ following in pairs[j] for a in pairs[i])
                ]
                soon.append((j, near))
                later.append((j, [i for i in range(j) if i not in near]))

            def cross(work, joined, pairs, factors, kept, spans, fresh):
                for j, members in work:
                    if not members:
                        continue
                    tops = []
                    for i in members:
                        source = joined(pairs[i], pairs[j])
                        tops.append(
                            source[spans[i]] + mul(factors[i][2][spans[i]], half(source))
                        )
                    tall = jnp.concatenate(tops, axis=0)
                    tall = tall[:, spans[j]] + mul(half(tall), factors[j][2][:, spans[j]])
                    start = 0
                    for i in members:
                        for at in kept[i]:
                            for k, to in enumerate(kept[j]):
                                fresh[pairs[i][at], pairs[j][to]] = tall[
                                    start : start + width, k * width : (k + 1) * width
                                ]
                            start += width

            def scaled(fresh, column_scale, row_scale):
                return {
                    (a, b): column_scale[a] * value * row_scale[b]
                    for (a, b), value in fresh.items()
                }

            known = (joined_from(blocks), pairs, factors, kept, spans)
            cross(soon, *known, fresh)
            blocks = scaled(fresh, column_scale, row_scale)

            def finish(blocks=blocks, later=later, known=known, down=column_scale, along=row_scale):
                rest = {}
                cross(later, *known, rest)
                blocks.update(scaled(rest, down, along))

            scales = column_scale
        history.append((pairs, factors, scales))

    pairs, factors, _ = history[-1]
    z, e, _ = factors[0]
    combined = {
        pairs[0][0]: jnp.where(eye, 1.0, 0.0) + e[:width, :width],
        pairs[0][1]: e[width:, :width],
    }
    final = z * jnp.sqrt(total[0])
    for pairs, factors, scales in reversed(history[:-1]):
        following = {}
        for pair, (z, e, thin) in zip(pairs, factors):
            parts = [i for i in range(2) if pair[i] in combined]
            tops = {i: scales[pair[i]] * combined[pair[i]] for i in parts}
            stacked = half(jnp.concatenate([tops[i] for i in parts], axis=0))
            moved = mul(thin[:, parts[0] * width : (parts[-1] + 1) * width], stacked)
            for i in range(2):
                rows = moved[i * width : (i + 1) * width]
                following[pair[i]] = tops[i] + rows if i in tops else rows
        combined = following
    weights = jnp.concatenate(
        [first_scale[p] * combined[p] for p in range(count)], axis=0
    ) * final
    high = half(weights)
    low = half(weights - high.astype(jnp.float32))
    own = out_ref.shape[0]
    chunk = own // count
    both = jnp.concatenate([high, low], axis=1)
    origins = ring_origins(count)
    for source_ref, first, rows in ((early_ref, 0, own - chunk), (ordered_ref, count - 1, chunk)):
        product = mul(source_ref[:rows], both)
        result = product[:, :width] + product[:, width:]
        for k in range(rows // chunk):
            start = pl.multiple_of(origins[first + k] * chunk, chunk)
            out_ref[pl.ds(start, chunk), :] = result[k * chunk : (k + 1) * chunk]


def all_rounds(mine, other, panel_order):
    count = panel_order.shape[0]
    total = mine[0].shape[1]
    inside = pl.BlockSpec(memory_space=pltpu.VMEM)
    numbers = pl.BlockSpec(memory_space=pltpu.SMEM)
    early = mine[:-2] + other[:-2]
    last = mine[-2:] + other[-2:]
    early_rows = sum(block.shape[0] for block in early)
    last_rows = sum(block.shape[0] for block in last)
    early_gram = pl.pallas_call(
        functools.partial(gram_kernel, count, len(early)),
        out_shape=[jax.ShapeDtypeStruct((early_rows, total), jnp.bfloat16)]
        + [
            jax.ShapeDtypeStruct(((b + 2) * PANEL, 2 * PANEL), jnp.float32)
            for b in range(0, count, 2)
        ],
        in_specs=[numbers] + [inside] * len(early),
        out_specs=[inside] * (1 + count // 2),
        scratch_shapes=[pltpu.VMEM((total, early_rows), jnp.bfloat16)],
        compiler_params=pltpu.CompilerParams(vmem_limit_bytes=16 << 20),
        cost_estimate=pl.CostEstimate(
            flops=2 * early_rows * total * total,
            bytes_accessed=4 * early_rows * total + 3 * total * total,
            transcendentals=0,
        ),
    )
    ordered, *talls = early_gram(panel_order, *early)
    return pl.pallas_call(
        functools.partial(rounds_kernel, count, len(last)),
        out_shape=jax.ShapeDtypeStruct(((early_rows + last_rows) // 2, PANEL), jnp.float32),
        in_specs=[numbers] + [inside] * (len(last) + 1 + len(talls)),
        out_specs=inside,
        scratch_shapes=[
            pltpu.VMEM((last_rows, total), jnp.bfloat16),
            pltpu.VMEM((total, last_rows), jnp.bfloat16),
        ],
        compiler_params=pltpu.CompilerParams(vmem_limit_bytes=32 << 20),
    )(panel_order, *last, ordered, *talls)


def ring_gather(block, axis):
    count = lax.axis_size(axis)
    ring = list(range(0, count, 2)) + list(range(1, count, 2))[::-1]
    onward = [(ring[i], ring[(i + 1) % count]) for i in range(count)]
    back = [(b, a) for a, b in onward]
    blocks = [block]
    ahead = behind = block
    for _ in range(1, count // 2):
        ahead = lax.ppermute(ahead, axis, onward)
        behind = lax.ppermute(behind, axis, back)
        blocks += [ahead, behind]
    middle = block.shape[0] // 2
    blocks.append(lax.ppermute(ahead[:middle], axis, onward))
    blocks.append(lax.ppermute(behind[middle:], axis, back))
    return blocks


def gathered_rounds(sketch, panel_order):
    mine = ring_gather(sketch, "row")
    other = [lax.ppermute(block, "grp", [(0, 1), (1, 0)]) for block in mine]
    return all_rounds(mine, other, panel_order)


def pair_transform(gram):
    squares = jnp.sum(jnp.where(diagonal_mask(gram.shape[0]), gram, 0.0), axis=0)
    inv_root = lax.rsqrt(squares)
    normed = gram * inv_root[:, None] * inv_root[None, :]
    bound = jnp.max(jnp.sum(jnp.abs(normed), axis=1))
    identity = jnp.eye(gram.shape[0], dtype=jnp.float32)
    current = normed / bound
    inverse = identity
    for _ in range(NS_ITERS):
        middle = 1.5 * identity - 0.5 * jnp.dot(inverse, current, precision=lax.Precision.HIGHEST)
        current_next = jnp.dot(current, middle, precision=lax.Precision.HIGHEST)
        inverse = jnp.dot(middle, inverse, precision=lax.Precision.HIGHEST)
        current = current_next
    return inv_root[:, None] * inverse * (jnp.sqrt(squares) / jnp.sqrt(bound))[None, :]


def cross_product(left, right):
    return lax.dot_general(
        left,
        right,
        (((0,), (0,)), ((), ())),
        precision=lax.Precision.HIGHEST,
        preferred_element_type=jnp.float32,
    )


def gram_blocks(own, partner):
    return (cross_product(own, own), cross_product(own, partner), cross_product(partner, partner))


def pair_update(own, partner, blocks, lower):
    self_gram, cross_gram, other_gram = blocks
    low_low = jnp.where(lower, self_gram, other_gram)
    high_high = jnp.where(lower, other_gram, self_gram)
    low_high = jnp.where(lower, cross_gram, cross_gram.T)
    gram = jnp.concatenate(
        [
            jnp.concatenate([low_low, low_high], axis=1),
            jnp.concatenate([low_high.T, high_high], axis=1),
        ],
        axis=0,
    )
    mixing = pair_transform(gram)
    width = own.shape[1]
    own_own = jnp.where(lower, mixing[:width, :width], mixing[width:, width:])
    other_own = jnp.where(lower, mixing[width:, :width], mixing[:width, width:])
    return jnp.dot(own, own_own, precision=lax.Precision.HIGHEST) + jnp.dot(
        partner, other_own, precision=lax.Precision.HIGHEST
    )


def exchanged_rounds(sketch, panel_order):
    panels = sketch.reshape(KB, -1, PANEL)
    ordered = jnp.take(panels, panel_order, axis=1).reshape(KB, -1)
    regrouped = lax.all_to_all(ordered, "row", split_axis=1, concat_axis=0, tiled=True)
    half_rows = regrouped.shape[0]
    depth = lax.axis_size("row").bit_length() - 1
    position = lax.axis_index("row")
    working = lax.all_gather(regrouped, "grp", axis=0, tiled=True).astype(jnp.float32)
    for turn in range(ROUNDS):
        bit = turn % depth
        partner = swapped(working.astype(jnp.bfloat16), "row", bit).astype(working.dtype)
        lower = position >> bit & 1 == 0
        working = pair_update(working, partner, gram_blocks(working, partner), lower)
    return lax.dynamic_slice_in_dim(working, lax.axis_index("grp") * half_rows, half_rows, 0)


def gathers(devices, columns):
    return 2 * KB * devices * columns + 4 * columns * columns <= GATHER_BYTES


def per_device(design, target, coeffs, tau_level, bucket, sign_bit, panel_order):
    sketch = sketch_local(design, target, coeffs, tau_level, bucket, sign_bit)
    columns = design.shape[1]
    if gathers(lax.axis_size("row") * lax.axis_size("grp"), columns):
        return gathered_rounds(sketch, panel_order)
    return exchanged_rounds(sketch, panel_order)


def solution(mesh):
    placed = (
        P(("parts", "grp", "row"), None),
        P(("parts", "grp", "row")),
        P("parts"),
        P(("parts", "grp", "row")),
        P(("parts", "grp", "row")),
        P(("parts", "grp", "row")),
        P("parts"),
    )
    return jax.shard_map(
        per_device,
        mesh=mesh,
        in_specs=placed,
        out_specs=P(("parts", "grp"), "row"),
        check_vma=False,
    )
```

profile of v0, /device:TPU:0, one launch (start us, length us, event | category | flops | bytes accessed | tf_op | source)
XLA Modules:
  0.0 46.3 jit_solution(11563195686856380071)
XLA Ops:
  0.0 3.0 %shard_map.73.refs_0_ = bf16[64,1024]{1,0:T(8,128)(2,1)} custom-call(bf16[256,1024]{1,0:T(8,128)(2,1)} %design_hbm.1, f32[256]{0:T(256)} %target_hbm.1, bf16[1024]{0:T(1024)(128)(2,1)} %coeffs_hbm.1, s32[2]{0:T(128)} %level_ref.1, s32[256]{0:T(256)} %bucket_hbm.1, s32[256]{0:T(256)} %sign_hbm.1), custom_call_target="tpu_custom_call" | custom-call | tf_op jit(solution)/shard_map/pallas_call | solution.py:74
  3.0 3.1 %collective-permute-start = (bf16[64,1024]{1,0:T(8,128)(2,1)}, bf16[64,1024]{1,0:T(8,128)(2,1)S(1)}, u32[]{:S(2)}, u32[]{:S(2)}) collective-permute-start(bf16[64,1024]{1,0:T(8,128)(2,1)} %shard_map.73.refs_0_), channel_id=1, source_target_pairs={{0,2},{2,4},{4,6},{6,7},{7,5},{5,3},{3,1},{1,0},{8,10},{10,12},{12... | collective-permute-start | bytes 393224 | tf_op jit(solution)/shard_map/ppermute | solution.py:412
  6.1 0.0 collective-permute-start.4
  6.1 3.6 %collective-permute-done.refs_1_ = bf16[64,1024]{1,0:T(8,128)(2,1)S(1)} collective-permute-done((bf16[64,1024]{1,0:T(8,128)(2,1)}, bf16[64,1024]{1,0:T(8,128)(2,1)S(1)}, u32[]{:S(2)}, u32[]{:S(2)}) %collective-permute-start) | collective-permute-done | bytes 131104 | tf_op jit(solution)/shard_map/ppermute | solution.py:412
  9.8 1.8 %collective-permute-start.1 = (bf16[64,1024]{1,0:T(8,128)(2,1)S(1)}, bf16[64,1024]{1,0:T(8,128)(2,1)S(1)}, u32[]{:S(2)}, u32[]{:S(2)}) collective-permute-start(bf16[64,1024]{1,0:T(8,128)(2,1)S(1)} %collective-permute-done.refs_1_), channel_id=1, source_target_pairs={{0,2},{2,4},{4,6},{6,7},{7,5},{5,3},{3,1},{1,0},{8,10},{10,12},{12... | collective-permute-start | bytes 393224 | tf_op jit(solution)/shard_map/ppermute | solution.py:412
  11.6 0.0 collective-permute-done.4.refs_2_
  11.6 0.2 collective-permute-start.5
  11.8 0.0 collective-permute-start.10
  11.8 0.5 %collective-permute-start.11 = (bf16[64,1024]{1,0:T(8,128)(2,1)S(1)}, bf16[64,1024]{1,0:T(8,128)(2,1)S(1)}, u32[]{:S(2)}, u32[]{:S(2)}) collective-permute-start(bf16[64,1024]{1,0:T(8,128)(2,1)S(1)} %collective-permute-done.refs_1_), channel_id=1, source_target_pairs={{0,8},{8,0},{1,9},{9,1},{2,10},{10,2},{3,11},{11,3},{4,12},{12,4},... | collective-permute-start | bytes 393224 | tf_op jit(solution)/shard_map/ppermute | solution.py:423
  12.3 2.4 %collective-permute-done.1.refs_3_ = bf16[64,1024]{1,0:T(8,128)(2,1)S(1)} collective-permute-done((bf16[64,1024]{1,0:T(8,128)(2,1)S(1)}, bf16[64,1024]{1,0:T(8,128)(2,1)S(1)}, u32[]{:S(2)}, u32[]{:S(2)}) %collective-permute-start.1) | collective-permute-done | bytes 131104 | tf_op jit(solution)/shard_map/ppermute | solution.py:412
  14.8 1.8 %collective-permute-start.2 = (bf16[64,1024]{1,0:T(8,128)(2,1)S(1)}, bf16[64,1024]{1,0:T(8,128)(2,1)S(1)}, u32[]{:S(2)}, u32[]{:S(2)}) collective-permute-start(bf16[64,1024]{1,0:T(8,128)(2,1)S(1)} %collective-permute-done.1.refs_3_), channel_id=1, source_target_pairs={{0,2},{2,4},{4,6},{6,7},{7,5},{5,3},{3,1},{1,0},{8,10},{10,12},{12... | collective-permute-start | bytes 393224 | tf_op jit(solution)/shard_map/ppermute | solution.py:412
  16.6 0.0 collective-permute-done.5.refs_4_
  16.6 0.2 collective-permute-start.6
  16.8 0.0 collective-permute-start.12
  16.8 0.0 collective-permute-done.10.refs_7_
  16.8 0.5 %collective-permute-start.13 = (bf16[64,1024]{1,0:T(8,128)(2,1)S(1)}, bf16[64,1024]{1,0:T(8,128)(2,1)S(1)}, u32[]{:S(2)}, u32[]{:S(2)}) collective-permute-start(bf16[64,1024]{1,0:T(8,128)(2,1)S(1)} %collective-permute-done.1.refs_3_), channel_id=1, source_target_pairs={{0,8},{8,0},{1,9},{9,1},{2,10},{10,2},{3,11},{11,3},{4,12},{12,4},... | collective-permute-start | bytes 393224 | tf_op jit(solution)/shard_map/ppermute | solution.py:423
  17.3 0.0 collective-permute-done.11.refs_8_
  17.3 0.1 collective-permute-start.14
  17.4 2.3 %collective-permute-done.2.refs_5_ = bf16[64,1024]{1,0:T(8,128)(2,1)S(1)} collective-permute-done((bf16[64,1024]{1,0:T(8,128)(2,1)S(1)}, bf16[64,1024]{1,0:T(8,128)(2,1)S(1)}, u32[]{:S(2)}, u32[]{:S(2)}) %collective-permute-start.2) | collective-permute-done | bytes 131104 | tf_op jit(solution)/shard_map/ppermute | solution.py:412
  19.7 0.0 collective-permute-start.15
  19.7 1.8 %collective-permute-done.6.refs_6_ = bf16[64,1024]{1,0:T(8,128)(2,1)S(1)} collective-permute-done((bf16[64,1024]{1,0:T(8,128)(2,1)S(1)}, bf16[64,1024]{1,0:T(8,128)(2,1)S(1)}, u32[]{:S(2)}, u32[]{:S(2)}) %collective-permute-start.6) | collective-permute-done | bytes 131104 | tf_op jit(solution)/shard_map/ppermute | solution.py:413
  21.5 0.0 collective-permute-start.16
  21.5 0.0 copy-start.2
  21.6 0.0 collective-permute-done.12.refs_9_
  21.6 1.6 %collective-permute-start.3 = (bf16[32,1024]{1,0:T(8,128)(2,1)S(1)}, bf16[32,1024]{1,0:T(8,128)(2,1)S(1)}, u32[]{:S(2)}, u32[]{:S(2)}) collective-permute-start(bf16[32,1024]{1,0:T(8,128)(2,1)S(1)} %slice.8), channel_id=1, source_target_pairs={{0,2},{2,4},{4,6},{6,7},{7,5},{5,3},{3,1},{1,0},{8,10},{10,12},{12... | collective-permute-start | bytes 196616 | tf_op jit(solution)/shard_map/ppermute | solution.py:416
  23.2 0.0 collective-permute-done.13.refs_10_
  23.2 0.4 collective-permute-start.7
  23.7 2.5 %collective-permute-done.3.refs_0_ = bf16[32,1024]{1,0:T(8,128)(2,1)S(1)} collective-permute-done((bf16[32,1024]{1,0:T(8,128)(2,1)S(1)}, bf16[32,1024]{1,0:T(8,128)(2,1)S(1)}, u32[]{:S(2)}, u32[]{:S(2)}) %collective-permute-start.3) | collective-permute-done | bytes 65568 | tf_op jit(solution)/shard_map/ppermute | solution.py:416
  26.1 0.0 collective-permute-start.8
  26.1 1.4 %collective-permute-done.7.refs_1_ = bf16[32,1024]{1,0:T(8,128)(2,1)S(1)} collective-permute-done((bf16[32,1024]{1,0:T(8,128)(2,1)S(1)}, bf16[32,1024]{1,0:T(8,128)(2,1)S(1)}, u32[]{:S(2)}, u32[]{:S(2)}) %collective-permute-start.7) | collective-permute-done | bytes 65568 | tf_op jit(solution)/shard_map/ppermute | solution.py:417
  27.5 0.0 collective-permute-start.9
  27.5 0.0 collective-permute-done.14.refs_11_
  27.5 0.0 collective-permute-done.15.refs_12_
  27.5 0.0 collective-permute-done.16.refs_13_
  27.5 0.0 copy-start
  27.5 0.9 %copy-done = bf16[64,1024]{1,0:T(8,128)(2,1)S(1)} copy-done((bf16[64,1024]{1,0:T(8,128)(2,1)S(1)}, bf16[64,1024]{1,0:T(8,128)(2,1)}, u32[]{:S(2)}) %copy-start) | copy-done | bytes 131096
  28.4 0.0 copy-start.1
  28.4 0.7 %copy-done.1 = s32[8]{0:T(128)S(1)} copy-done((s32[8]{0:T(128)S(1)}, s32[8]{0:T(128)}, u32[]{:S(2)}) %copy-start.1) | copy-done | bytes 56
  29.1 2.4 %shard_map.74 = (bf16[896,1024]{1,0:T(8,128)(2,1)S(1)}, f32[256,256]{1,0:T(8,128)S(1)}, f32[512,256]{1,0:T(8,128)S(1)}, f32[768,256]{1,0:T(8,128)S(1)}, f32[1024,256]{1,0:T(8,128)S(1)}) custom-call(s32[8]{0:T(128)S(1)} %copy-done.1, bf16[64,1024]{1,0:T(8,128)(2,1)S(1)} %copy-done, bf16[64,1024]{1,0:T(8,128)(2,1)S(1)} %collective-permute-done.refs_1_, ...), custom_call_target="tpu_custom_call" | custom-call | flops 1879048192 | bytes 6815744 | tf_op jit(solution)/shard_map/pallas_call | solution.py:390
  31.5 0.0 collective-permute-done.8.refs_2_
  31.5 0.0 collective-permute-done.9.refs_3_
  31.5 0.0 copy-done.2
  31.5 14.8 %shard_map.75 = f32[512,128]{1,0:T(8,128)} custom-call(s32[8]{0:T(128)S(1)} %copy-done.2, bf16[32,1024]{1,0:T(8,128)(2,1)S(1)} %collective-permute-done.3.refs_0_, bf16[32,1024]{1,0:T(8,128)(2,1)S(1)} %collective-permute-done.7.refs_1_, bf16[32,1024]{1,0:T(8,128)(2,1)S(1)} %collective-permute-done.8.refs_2_, ...), custom_call_target="tpu_custom_call" | custom-call | tf_op jit(solution)/shard_map/pallas_call | solution.py:391
  (2 shorter events, 0.0 us)
Async XLA Ops:
  3.0 6.8 %collective-permute-start = (bf16[64,1024]{1,0:T(8,128)(2,1)}, bf16[64,1024]{1,0:T(8,128)(2,1)S(1)}, u32[]{:S(2)}, u32[]{:S(2)}) collective-permute-start(bf16[64,1024]{1,0:T(8,128)(2,1)} %shard_map.73.refs_0_), channel_id=1, source_target_pairs={{0,2},{2,4},{4,6},{6,7},{7,5},{5,3},{3,1},{1,0},{8,10},{10,12},{12... | collective-permute-start | bytes 393224 | tf_op jit(solution)/shard_map/ppermute | solution.py:412
  6.1 5.5 %collective-permute-start.4 = (bf16[64,1024]{1,0:T(8,128)(2,1)}, bf16[64,1024]{1,0:T(8,128)(2,1)S(1)}, u32[]{:S(2)}, u32[]{:S(2)}) collective-permute-start(bf16[64,1024]{1,0:T(8,128)(2,1)} %shard_map.73.refs_0_), channel_id=1, source_target_pairs={{2,0},{4,2},{6,4},{7,6},{5,7},{3,5},{1,3},{0,1},{10,8},{12,10},{14... | collective-permute-start | bytes 393224 | tf_op jit(solution)/shard_map/ppermute | solution.py:413
  9.8 5.0 %collective-permute-start.1 = (bf16[64,1024]{1,0:T(8,128)(2,1)S(1)}, bf16[64,1024]{1,0:T(8,128)(2,1)S(1)}, u32[]{:S(2)}, u32[]{:S(2)}) collective-permute-start(bf16[64,1024]{1,0:T(8,128)(2,1)S(1)} %collective-permute-done.refs_1_), channel_id=1, source_target_pairs={{0,2},{2,4},{4,6},{6,7},{7,5},{5,3},{3,1},{1,0},{8,10},{10,12},{12... | collective-permute-start | bytes 393224 | tf_op jit(solution)/shard_map/ppermute | solution.py:412
  11.6 5.0 %collective-permute-start.5 = (bf16[64,1024]{1,0:T(8,128)(2,1)S(1)}, bf16[64,1024]{1,0:T(8,128)(2,1)S(1)}, u32[]{:S(2)}, u32[]{:S(2)}) collective-permute-start(bf16[64,1024]{1,0:T(8,128)(2,1)S(1)} %collective-permute-done.4.refs_2_), channel_id=1, source_target_pairs={{2,0},{4,2},{6,4},{7,6},{5,7},{3,5},{1,3},{0,1},{10,8},{12,10},{14... | collective-permute-start | bytes 393224 | tf_op jit(solution)/shard_map/ppermute | solution.py:413
  11.8 5.0 %collective-permute-start.10 = (bf16[64,1024]{1,0:T(8,128)(2,1)}, bf16[64,1024]{1,0:T(8,128)(2,1)S(1)}, u32[]{:S(2)}, u32[]{:S(2)}) collective-permute-start(bf16[64,1024]{1,0:T(8,128)(2,1)} %shard_map.73.refs_0_), channel_id=1, source_target_pairs={{0,8},{8,0},{1,9},{9,1},{2,10},{10,2},{3,11},{11,3},{4,12},{12,4},... | collective-permute-start | bytes 393224 | tf_op jit(solution)/shard_map/ppermute | solution.py:423
  11.8 5.5 %collective-permute-start.11 = (bf16[64,1024]{1,0:T(8,128)(2,1)S(1)}, bf16[64,1024]{1,0:T(8,128)(2,1)S(1)}, u32[]{:S(2)}, u32[]{:S(2)}) collective-permute-start(bf16[64,1024]{1,0:T(8,128)(2,1)S(1)} %collective-permute-done.refs_1_), channel_id=1, source_target_pairs={{0,8},{8,0},{1,9},{9,1},{2,10},{10,2},{3,11},{11,3},{4,12},{12,4},... | collective-permute-start | bytes 393224 | tf_op jit(solution)/shard_map/ppermute | solution.py:423
  14.8 5.0 %collective-permute-start.2 = (bf16[64,1024]{1,0:T(8,128)(2,1)S(1)}, bf16[64,1024]{1,0:T(8,128)(2,1)S(1)}, u32[]{:S(2)}, u32[]{:S(2)}) collective-permute-start(bf16[64,1024]{1,0:T(8,128)(2,1)S(1)} %collective-permute-done.1.refs_3_), channel_id=1, source_target_pairs={{0,2},{2,4},{4,6},{6,7},{7,5},{5,3},{3,1},{1,0},{8,10},{10,12},{12... | collective-permute-start | bytes 393224 | tf_op jit(solution)/shard_map/ppermute | solution.py:412
  16.6 5.0 %collective-permute-start.6 = (bf16[64,1024]{1,0:T(8,128)(2,1)S(1)}, bf16[64,1024]{1,0:T(8,128)(2,1)S(1)}, u32[]{:S(2)}, u32[]{:S(2)}) collective-permute-start(bf16[64,1024]{1,0:T(8,128)(2,1)S(1)} %collective-permute-done.5.refs_4_), channel_id=1, source_target_pairs={{2,0},{4,2},{6,4},{7,6},{5,7},{3,5},{1,3},{0,1},{10,8},{12,10},{14... | collective-permute-start | bytes 393224 | tf_op jit(solution)/shard_map/ppermute | solution.py:413
  16.8 4.8 %collective-permute-start.12 = (bf16[64,1024]{1,0:T(8,128)(2,1)S(1)}, bf16[64,1024]{1,0:T(8,128)(2,1)S(1)}, u32[]{:S(2)}, u32[]{:S(2)}) collective-permute-start(bf16[64,1024]{1,0:T(8,128)(2,1)S(1)} %collective-permute-done.4.refs_2_), channel_id=1, source_target_pairs={{0,8},{8,0},{1,9},{9,1},{2,10},{10,2},{3,11},{11,3},{4,12},{12,4},... | collective-permute-start | bytes 393224 | tf_op jit(solution)/shard_map/ppermute | solution.py:423
  16.8 6.4 %collective-permute-start.13 = (bf16[64,1024]{1,0:T(8,128)(2,1)S(1)}, bf16[64,1024]{1,0:T(8,128)(2,1)S(1)}, u32[]{:S(2)}, u32[]{:S(2)}) collective-permute-start(bf16[64,1024]{1,0:T(8,128)(2,1)S(1)} %collective-permute-done.1.refs_3_), channel_id=1, source_target_pairs={{0,8},{8,0},{1,9},{9,1},{2,10},{10,2},{3,11},{11,3},{4,12},{12,4},... | collective-permute-start | bytes 393224 | tf_op jit(solution)/shard_map/ppermute | solution.py:423
  17.3 10.2 %collective-permute-start.14 = (bf16[64,1024]{1,0:T(8,128)(2,1)S(1)}, bf16[64,1024]{1,0:T(8,128)(2,1)S(1)}, u32[]{:S(2)}, u32[]{:S(2)}) collective-permute-start(bf16[64,1024]{1,0:T(8,128)(2,1)S(1)} %collective-permute-done.5.refs_4_), channel_id=1, source_target_pairs={{0,8},{8,0},{1,9},{9,1},{2,10},{10,2},{3,11},{11,3},{4,12},{12,4},... | collective-permute-start | bytes 393224 | tf_op jit(solution)/shard_map/ppermute | solution.py:423
  19.7 7.8 %collective-permute-start.15 = (bf16[64,1024]{1,0:T(8,128)(2,1)S(1)}, bf16[64,1024]{1,0:T(8,128)(2,1)S(1)}, u32[]{:S(2)}, u32[]{:S(2)}) collective-permute-start(bf16[64,1024]{1,0:T(8,128)(2,1)S(1)} %collective-permute-done.2.refs_5_), channel_id=1, source_target_pairs={{0,8},{8,0},{1,9},{9,1},{2,10},{10,2},{3,11},{11,3},{4,12},{12,4},... | collective-permute-start | bytes 393224 | tf_op jit(solution)/shard_map/ppermute | solution.py:423
  21.5 6.0 %collective-permute-start.16 = (bf16[64,1024]{1,0:T(8,128)(2,1)S(1)}, bf16[64,1024]{1,0:T(8,128)(2,1)S(1)}, u32[]{:S(2)}, u32[]{:S(2)}) collective-permute-start(bf16[64,1024]{1,0:T(8,128)(2,1)S(1)} %collective-permute-done.6.refs_6_), channel_id=1, source_target_pairs={{0,8},{8,0},{1,9},{9,1},{2,10},{10,2},{3,11},{11,3},{4,12},{12,4},... | collective-permute-start | bytes 393224 | tf_op jit(solution)/shard_map/ppermute | solution.py:423
  21.5 10.0 %copy-start.2 = (s32[8]{0:T(128)S(1)}, s32[8]{0:T(128)}, u32[]{:S(2)}) copy-start(s32[8]{0:T(128)} %order_ref.3) | copy-start | bytes 100
  21.6 4.5 %collective-permute-start.3 = (bf16[32,1024]{1,0:T(8,128)(2,1)S(1)}, bf16[32,1024]{1,0:T(8,128)(2,1)S(1)}, u32[]{:S(2)}, u32[]{:S(2)}) collective-permute-start(bf16[32,1024]{1,0:T(8,128)(2,1)S(1)} %slice.8), channel_id=1, source_target_pairs={{0,2},{2,4},{4,6},{6,7},{7,5},{5,3},{3,1},{1,0},{8,10},{10,12},{12... | collective-permute-start | bytes 196616 | tf_op jit(solution)/shard_map/ppermute | solution.py:416
  23.2 4.3 %collective-permute-start.7 = (bf16[32,1024]{1,0:T(8,128)(2,1)S(1)}, bf16[32,1024]{1,0:T(8,128)(2,1)S(1)}, u32[]{:S(2)}, u32[]{:S(2)}) collective-permute-start(bf16[32,1024]{1,0:T(8,128)(2,1)S(1)} %slice.9), channel_id=1, source_target_pairs={{2,0},{4,2},{6,4},{7,6},{5,7},{3,5},{1,3},{0,1},{10,8},{12,10},{14... | collective-permute-start | bytes 196616 | tf_op jit(solution)/shard_map/ppermute | solution.py:417
  26.1 5.4 %collective-permute-start.8 = (bf16[32,1024]{1,0:T(8,128)(2,1)S(1)}, bf16[32,1024]{1,0:T(8,128)(2,1)S(1)}, u32[]{:S(2)}, u32[]{:S(2)}) collective-permute-start(bf16[32,1024]{1,0:T(8,128)(2,1)S(1)} %collective-permute-done.3.refs_0_), channel_id=1, source_target_pairs={{0,8},{8,0},{1,9},{9,1},{2,10},{10,2},{3,11},{11,3},{4,12},{12,4},... | collective-permute-start | bytes 196616 | tf_op jit(solution)/shard_map/ppermute | solution.py:423
  27.5 4.0 %collective-permute-start.9 = (bf16[32,1024]{1,0:T(8,128)(2,1)S(1)}, bf16[32,1024]{1,0:T(8,128)(2,1)S(1)}, u32[]{:S(2)}, u32[]{:S(2)}) collective-permute-start(bf16[32,1024]{1,0:T(8,128)(2,1)S(1)} %collective-permute-done.7.refs_1_), channel_id=1, source_target_pairs={{0,8},{8,0},{1,9},{9,1},{2,10},{10,2},{3,11},{11,3},{4,12},{12,4},... | collective-permute-start | bytes 196616 | tf_op jit(solution)/shard_map/ppermute | solution.py:423
  27.5 0.9 %copy-start = (bf16[64,1024]{1,0:T(8,128)(2,1)S(1)}, bf16[64,1024]{1,0:T(8,128)(2,1)}, u32[]{:S(2)}) copy-start(bf16[64,1024]{1,0:T(8,128)(2,1)} %shard_map.73.refs_0_) | copy-start | bytes 393220
  28.4 0.7 %copy-start.1 = (s32[8]{0:T(128)S(1)}, s32[8]{0:T(128)}, u32[]{:S(2)}) copy-start(s32[8]{0:T(128)} %order_ref.3) | copy-start | bytes 100
where the time goes:
time: 46.5 us; the launch traced here: 46.3 us
  Pallas kernels  20.2 us (43%)
  waiting for transfers between devices  14.1 us (30%)
  starting transfers between devices  10.3 us (22%)
  local copies, waits for them, and re-layouts  1.57 us (3%)
    pallas_call x1, Pallas kernels, all_rounds(): pl.pallas_call(functools.partial(rounds_kernel, count, len(last)), out_sh...  14.8 us
    ppermute x3, waiting for transfers between devices, ring_gather(): ahead = lax.ppermute(ahead, axis, onward)  8.42 us
    ppermute x3, starting transfers between devices, ring_gather(): ahead = lax.ppermute(ahead, axis, onward)  6.7 us
    pallas_call x1, Pallas kernels, sketch_local(): pl.pallas_call(sketch_kernel, out_shape=jax.ShapeDtypeStruct((KB, columns...  3.02 us
    ppermute x1, waiting for transfers between devices, ring_gather(): blocks.append(lax.ppermute(ahead[:middle], axis, onward))  2.46 us
    pallas_call x1, Pallas kernels, all_rounds(): ordered, *talls = early_gram(panel_order, *early)  2.41 us
    ppermute x3, waiting for transfers between devices, ring_gather(): behind = lax.ppermute(behind, axis, back)  1.8 us
    ppermute x1, starting transfers between devices, ring_gather(): blocks.append(lax.ppermute(ahead[:middle], axis, onward))  1.63 us
  transfers between devices with their start and end apart: 17, of which 6 were waited for; matrix products, arithmetic and copies ran while one was open for 0% of the time, Pallas kernels for 5%

commit v1 on v0

--- a/solution.py
+++ b/solution.py
@@ -24,8 +24,8 @@
     return lax.ppermute(block, axis, route)
 
 
-def sketch_kernel(design_hbm, target_hbm, coeffs_hbm, level_ref, bucket_hbm, sign_hbm, out_ref,
-                  design_ref, target_ref, coeffs_ref, bucket_ref, sign_ref, arrived):
+def sketch_kernel(design_hbm, target_hbm, coeffs_hbm, level_ref, bucket_hbm, sign_hbm, order_ref,
+                  out_ref, design_ref, target_ref, coeffs_ref, bucket_ref, sign_ref, arrived):
     copies = [
         pltpu.make_async_copy(source, here, arrived.at[i])
         for i, (source, here) in enumerate(
@@ -65,16 +65,21 @@
     signed = (sign * jnp.sqrt(weight)).astype(jnp.bfloat16).astype(jnp.float32)
     slots = lax.broadcasted_iota(jnp.int32, (KB, rows), 0)
     embed = jnp.where(slots == bucket_ref[...].reshape(1, rows), signed, 0.0).astype(jnp.bfloat16)
-    out_ref[...] = jnp.dot(embed, design, preferred_element_type=jnp.float32).astype(jnp.bfloat16)
-
-
-def sketch_local(design, target, coeffs, tau_level, bucket, sign_bit):
+    for j in range(order_ref.shape[0]):
+        column = pl.multiple_of(order_ref[j] * PANEL, PANEL)
+        out_ref[:, j * PANEL : (j + 1) * PANEL] = jnp.dot(
+            embed, design_ref[:, pl.ds(column, PANEL)], preferred_element_type=jnp.float32
+        ).astype(jnp.bfloat16)
+
+
+def sketch_local(design, target, coeffs, tau_level, bucket, sign_bit, panel_order):
     rows, columns = design.shape
     anywhere = pl.BlockSpec(memory_space=pltpu.HBM)
+    numbers = pl.BlockSpec(memory_space=pltpu.SMEM)
     return pl.pallas_call(
         sketch_kernel,
         out_shape=jax.ShapeDtypeStruct((KB, columns), jnp.bfloat16),
-        in_specs=[anywhere] * 3 + [pl.BlockSpec(memory_space=pltpu.SMEM)] + [anywhere] * 2,
+        in_specs=[anywhere] * 3 + [numbers] + [anywhere] * 2 + [numbers],
         out_specs=pl.BlockSpec(memory_space=pltpu.VMEM),
         scratch_shapes=[
             pltpu.VMEM((rows, columns), jnp.bfloat16),
@@ -85,7 +90,7 @@
             pltpu.SemaphoreType.DMA((5,)),
         ],
         compiler_params=pltpu.CompilerParams(vmem_limit_bytes=67043328),
-    )(design, target, coeffs, tau_level, bucket, sign_bit)
+    )(design, target, coeffs, tau_level, bucket, sign_bit, panel_order)
 
 
 def half(block):
@@ -103,44 +108,61 @@
 
 
 def root_factors(grams, offs):
-    w, t, x, z = [], [], [], []
+    w, t, v, z = [], [], [], []
     for gram, off in zip(grams, offs):
         bound = jnp.max(jnp.sum(jnp.abs(gram), axis=0, keepdims=True), axis=1, keepdims=True)
         w.append(1.0 / bound)
         t.append(1.5 - 0.5 * w[-1])
-        x.append((-0.5 * w[-1] / t[-1]) * off)
-        z.append(t[-1] * lax.rsqrt(bound))
-    xs, halves = [x], [[half(a) for a in x]]
-    for _ in range(NS_ITERS - 1):
-        thin = halves[-1]
+        v.append((-0.5 * w[-1] / t[-1]) * off)
+        z.append(lax.rsqrt(bound))
+    s = [jnp.ones_like(a) for a in w]
+    thin = [half(a) for a in v]
+    doubles = []
+    for step in range(NS_ITERS):
+        z = [a * b for a, b in zip(z, t)]
         after = [1.5 - 0.5 * a * a * b for a, b in zip(t, w)]
         gain = [a * a * a / b for a, b in zip(t, after)]
-        linear = [g * (1.0 - b / a) for g, a, b in zip(gain, t, w)]
-        square = [g * (2.0 - 0.5 * b / a) for g, a, b in zip(gain, t, w)]
-        inner = [
-            half(q * a + g * mul(b, b)) for q, g, a, b in zip(square, gain, x, thin)
-        ]
-        x = [p * a + mul(r, b) for p, a, b, r in zip(linear, x, thin, inner)]
+        linear = [1.0 - b / a for a, b in zip(t, w)]
+        square = [2.0 - 0.5 * b / a for a, b in zip(t, w)]
+        if step % 2 == 0:
+            squared = [mul(a, a) for a in thin]
+        if step % 2 == 0 and step + 2 >= NS_ITERS and step + 1 < NS_ITERS:
+            parts = []
+            for g, a, b, c, x, q in zip(gain, linear, square, s, v, squared):
+                outer = half(q)
+                inner = half((g * (1.0 + b) * c * c * c) * x + (g * c * c * c * c) * q)
+                parts.append(
+                    ((1.0 + g * a) * c) * x + (g * (a + b) * c * c) * q + mul(inner, outer)
+                )
+            doubles.append(parts)
+        elif step % 2 == 0 and step + 1 == NS_ITERS:
+            doubles.append([c * x for c, x in zip(s, v)])
+        if step + 2 < NS_ITERS or step % 2 == 1 and step + 1 < NS_ITERS:
+            if step % 2 == 1:
+                squared = [mul(a, a) for a in thin]
+            inner = [half((b / c) * x + q) for b, c, x, q in zip(square, s, v, squared)]
+            before, flat, size = v, thin, s
+            v = [
+                (a / (c * c)) * x + mul(r, y)
+                for a, c, x, r, y in zip(linear, s, v, inner, thin)
+            ]
+            thin = [half(a) for a in v]
+            s = [g * c * c * c for g, c in zip(gain, s)]
+            if step % 2 == 0:
+                doubles.append(
+                    [
+                        c * x + d * (y + c * mul(a, b))
+                        for c, x, d, y, a, b in zip(size, before, s, v, thin, flat)
+                    ]
+                )
         w = [a * a * b for a, b in zip(t, w)]
         t = after
-        z = [a * b for a, b in zip(z, t)]
-        xs.append(x)
-        halves.append([half(a) for a in x])
-    while len(xs) > 1:
-        merged, thinner = [], []
-        for k in range(0, len(xs) - 1, 2):
-            merged.append(
-                [
-                    a + b + mul(d, c)
-                    for a, b, c, d in zip(xs[k], xs[k + 1], halves[k], halves[k + 1])
-                ]
-            )
-            thinner.append([half(a) for a in merged[-1]])
-        if len(xs) % 2:
-            merged.append(xs[-1])
-            thinner.append(halves[-1])
-        xs, halves = merged, thinner
-    return list(zip(z, xs[0], halves[0]))
+    e = doubles[0]
+    thin = [half(a) for a in e]
+    for parts in doubles[1:]:
+        e = [a + b + mul(half(b), c) for a, b, c in zip(e, parts, thin)]
+        thin = [half(a) for a in e]
+    return list(zip(z, e, thin))
 
 
 def diagonal_of(block, axis):
@@ -161,24 +183,18 @@
     return [ring_index((here + turn + count) % count, count) for turn in turns]
 
 
-def panel_columns(order_ref, count):
+def gather_panels(count, chunks, ordered_ref, turned_ref):
     position = lax.axis_index("row")
-    return [
-        pl.multiple_of(order_ref[jnp.bitwise_xor(position, j)] * PANEL, PANEL)
-        for j in range(count)
-    ]
-
-
-def gather_panels(columns, chunks, ordered_ref, turned_ref):
     start = 0
     for chunk in chunks:
         rows = chunk.shape[0]
-        for j, column in enumerate(columns):
+        for j in range(count):
+            column = pl.multiple_of(jnp.bitwise_xor(position, j) * PANEL, PANEL)
             ordered_ref[start : start + rows, j * PANEL : (j + 1) * PANEL] = chunk[
                 :, pl.ds(column, PANEL)
             ]
         start += rows
-    for p in range(0, len(columns), 2):
+    for p in range(0, count, 2):
         span = slice(p * PANEL, (p + 2) * PANEL)
         turned_ref[span] = ordered_ref[:, span].T
 
@@ -187,20 +203,24 @@
     return mul(turned_ref[: (b + 2) * PANEL], ordered_ref[:, b * PANEL : (b + 2) * PANEL])
 
 
-def gram_kernel(count, pieces, order_ref, *refs):
-    chunks, (ordered_ref, *tall_refs), turned_ref = refs[:pieces], refs[pieces:-1], refs[-1]
-    gather_panels(panel_columns(order_ref, count), chunks, ordered_ref, turned_ref)
+def gram_kernel(count, pieces, first_hbm, *refs):
+    chunks, (ordered_ref, *tall_refs) = refs[:pieces], refs[pieces:-3]
+    turned_ref, first_ref, arrived = refs[-3:]
+    copy = pltpu.make_async_copy(first_hbm, first_ref, arrived)
+    copy.start()
+    copy.wait()
+    gather_panels(count, (first_ref, *chunks), ordered_ref, turned_ref)
     for k, tall_ref in enumerate(tall_refs):
         tall_ref[...] = tall_gram(turned_ref, ordered_ref, 2 * k)
 
 
-def rounds_kernel(count, pieces, order_ref, *refs):
+def rounds_kernel(count, pieces, *refs):
     chunks, refs = refs[:pieces], refs[pieces:]
     early_ref, tall_refs = refs[0], refs[1 : 1 + count // 2]
     out_ref, ordered_ref, turned_ref = refs[1 + count // 2 :]
     width = PANEL
     depth = count.bit_length() - 1
-    gather_panels(panel_columns(order_ref, count), chunks, ordered_ref, turned_ref)
+    gather_panels(count, chunks, ordered_ref, turned_ref)
 
     live = [None] * (ROUNDS + 1)
     live[ROUNDS] = [0]
@@ -361,25 +381,28 @@
             out_ref[pl.ds(start, chunk), :] = result[k * chunk : (k + 1) * chunk]
 
 
-def all_rounds(mine, other, panel_order):
-    count = panel_order.shape[0]
+def all_rounds(mine, other):
     total = mine[0].shape[1]
+    count = total // PANEL
     inside = pl.BlockSpec(memory_space=pltpu.VMEM)
-    numbers = pl.BlockSpec(memory_space=pltpu.SMEM)
     early = mine[:-2] + other[:-2]
     last = mine[-2:] + other[-2:]
     early_rows = sum(block.shape[0] for block in early)
     last_rows = sum(block.shape[0] for block in last)
     early_gram = pl.pallas_call(
-        functools.partial(gram_kernel, count, len(early)),
+        functools.partial(gram_kernel, count, len(early) - 1),
         out_shape=[jax.ShapeDtypeStruct((early_rows, total), jnp.bfloat16)]
         + [
             jax.ShapeDtypeStruct(((b + 2) * PANEL, 2 * PANEL), jnp.float32)
             for b in range(0, count, 2)
         ],
-        in_specs=[numbers] + [inside] * len(early),
+        in_specs=[pl.BlockSpec(memory_space=pltpu.HBM)] + [inside] * (len(early) - 1),
         out_specs=[inside] * (1 + count // 2),
-        scratch_shapes=[pltpu.VMEM((total, early_rows), jnp.bfloat16)],
+        scratch_shapes=[
+            pltpu.VMEM((total, early_rows), jnp.bfloat16),
+            pltpu.VMEM(mine[0].shape, jnp.bfloat16),
+            pltpu.SemaphoreType.DMA,
+        ],
         compiler_params=pltpu.CompilerParams(vmem_limit_bytes=16 << 20),
         cost_estimate=pl.CostEstimate(
             flops=2 * early_rows * total * total,
@@ -387,18 +410,18 @@
             transcendentals=0,
         ),
     )
-    ordered, *talls = early_gram(panel_order, *early)
+    ordered, *talls = early_gram(*early)
     return pl.pallas_call(
         functools.partial(rounds_kernel, count, len(last)),
         out_shape=jax.ShapeDtypeStruct(((early_rows + last_rows) // 2, PANEL), jnp.float32),
-        in_specs=[numbers] + [inside] * (len(last) + 1 + len(talls)),
+        in_specs=[inside] * (len(last) + 1 + len(talls)),
         out_specs=inside,
         scratch_shapes=[
             pltpu.VMEM((last_rows, total), jnp.bfloat16),
             pltpu.VMEM((total, last_rows), jnp.bfloat16),
         ],
         compiler_params=pltpu.CompilerParams(vmem_limit_bytes=32 << 20),
-    )(panel_order, *last, ordered, *talls)
+    )(*last, ordered, *talls)
 
 
 def ring_gather(block, axis):
@@ -418,10 +441,10 @@
     return blocks
 
 
-def gathered_rounds(sketch, panel_order):
+def gathered_rounds(sketch):
     mine = ring_gather(sketch, "row")
     other = [lax.ppermute(block, "grp", [(0, 1), (1, 0)]) for block in mine]
-    return all_rounds(mine, other, panel_order)
+    return all_rounds(mine, other)
 
 
 def pair_transform(gram):
@@ -475,10 +498,8 @@
     )
 
 
-def exchanged_rounds(sketch, panel_order):
-    panels = sketch.reshape(KB, -1, PANEL)
-    ordered = jnp.take(panels, panel_order, axis=1).reshape(KB, -1)
-    regrouped = lax.all_to_all(ordered, "row", split_axis=1, concat_axis=0, tiled=True)
+def exchanged_rounds(sketch):
+    regrouped = lax.all_to_all(sketch, "row", split_axis=1, concat_axis=0, tiled=True)
     half_rows = regrouped.shape[0]
     depth = lax.axis_size("row").bit_length() - 1
     position = lax.axis_index("row")
@@ -496,11 +517,11 @@
 
 
 def per_device(design, target, coeffs, tau_level, bucket, sign_bit, panel_order):
-    sketch = sketch_local(design, target, coeffs, tau_level, bucket, sign_bit)
+    sketch = sketch_local(design, target, coeffs, tau_level, bucket, sign_bit, panel_order)
     columns = design.shape[1]
     if gathers(lax.axis_size("row") * lax.axis_size("grp"), columns):
-        return gathered_rounds(sketch, panel_order)
-    return exchanged_rounds(sketch, panel_order)
+        return gathered_rounds(sketch)
+    return exchanged_rounds(sketch)
 
 
 def solution(mesh):

time: 46.5 us -> 44.2 us (0.951)
  Pallas kernels: 20.2 us -> 18.6 us
  local copies, waits for them, and re-layouts: 1.57 us -> 0.91 us
    pallas_call x1, Pallas kernels: 14.8 us -> 13.5 us  [all_rounds(): pl.pallas_call(functools.partial(rounds_kernel, count, len(last)), out_sh...]
    unnamed x6 -> x2, local copies, waits for them, and re-layouts: 1.56 us -> 0.9 us
where the time goes in v1:
time: 44.2 us; the launch traced here: 44 us
  Pallas kernels  18.6 us (42%)
  waiting for transfers between devices  14.1 us (32%)
  starting transfers between devices  10.3 us (23%)
  local copies, waits for them, and re-layouts  0.91 us (2%)
    pallas_call x1, Pallas kernels, all_rounds(): pl.pallas_call(functools.partial(rounds_kernel, count, len(last)), out_sh...  13.5 us
    ppermute x3, waiting for transfers between devices, ring_gather(): ahead = lax.ppermute(ahead, axis, onward)  8.42 us
    ppermute x3, starting transfers between devices, ring_gather(): ahead = lax.ppermute(ahead, axis, onward)  6.7 us
    pallas_call x1, Pallas kernels, sketch_local(): pl.pallas_call(sketch_kernel, out_shape=jax.ShapeDtypeStruct((KB, columns...  3.04 us
    ppermute x1, waiting for transfers between devices, ring_gather(): blocks.append(lax.ppermute(ahead[:middle], axis, onward))  2.47 us
    pallas_call x1, Pallas kernels, all_rounds(): ordered, *talls = early_gram(*early)  2.04 us
    ppermute x3, waiting for transfers between devices, ring_gather(): behind = lax.ppermute(behind, axis, back)  1.8 us
    ppermute x1, starting transfers between devices, ring_gather(): blocks.append(lax.ppermute(ahead[:middle], axis, onward))  1.63 us
  transfers between devices with their start and end apart: 17, of which 6 were waited for; matrix products, arithmetic and copies ran while one was open for 0% of the time, Pallas kernels for 5%

profile of v1, /device:TPU:0, one launch (start us, length us, event | category | flops | bytes accessed | tf_op | source)
XLA Modules:
  0.0 44.0 jit_solution(5597100305910329479)
XLA Ops:
  0.0 3.0 %shard_map.73.first_hbm = bf16[64,1024]{1,0:T(8,128)(2,1)} custom-call(bf16[256,1024]{1,0:T(8,128)(2,1)} %design_hbm.1, f32[256]{0:T(256)} %target_hbm.1, bf16[1024]{0:T(1024)(128)(2,1)} %coeffs_hbm.1, s32[2]{0:T(128)} %level_ref.1, s32[256]{0:T(256)} %bucket_hbm.1, s32[256]{0:T(256)} %sign_hbm.1, s32[8]{0:T(128)} %order_ref.1), custom_call_target="tpu_custom_call" | custom-call | tf_op jit(solution)/shard_map/pallas_call | solution.py:79
  3.1 3.1 %collective-permute-start = (bf16[64,1024]{1,0:T(8,128)(2,1)}, bf16[64,1024]{1,0:T(8,128)(2,1)S(1)}, u32[]{:S(2)}, u32[]{:S(2)}) collective-permute-start(bf16[64,1024]{1,0:T(8,128)(2,1)} %shard_map.73.first_hbm), channel_id=1, source_target_pairs={{0,2},{2,4},{4,6},{6,7},{7,5},{5,3},{3,1},{1,0},{8,10},{10,12},{12... | collective-permute-start | bytes 393224 | tf_op jit(solution)/shard_map/ppermute | solution.py:435
  6.2 0.0 collective-permute-start.4
  6.2 3.6 %collective-permute-done.refs_0_ = bf16[64,1024]{1,0:T(8,128)(2,1)S(1)} collective-permute-done((bf16[64,1024]{1,0:T(8,128)(2,1)}, bf16[64,1024]{1,0:T(8,128)(2,1)S(1)}, u32[]{:S(2)}, u32[]{:S(2)}) %collective-permute-start) | collective-permute-done | bytes 131104 | tf_op jit(solution)/shard_map/ppermute | solution.py:435
  9.8 1.8 %collective-permute-start.1 = (bf16[64,1024]{1,0:T(8,128)(2,1)S(1)}, bf16[64,1024]{1,0:T(8,128)(2,1)S(1)}, u32[]{:S(2)}, u32[]{:S(2)}) collective-permute-start(bf16[64,1024]{1,0:T(8,128)(2,1)S(1)} %collective-permute-done.refs_0_), channel_id=1, source_target_pairs={{0,2},{2,4},{4,6},{6,7},{7,5},{5,3},{3,1},{1,0},{8,10},{10,12},{12... | collective-permute-start | bytes 393224 | tf_op jit(solution)/shard_map/ppermute | solution.py:435
  11.6 0.0 collective-permute-done.4.refs_1_
  11.6 0.2 collective-permute-start.5
  11.8 0.0 collective-permute-start.10
  11.8 0.5 %collective-permute-start.11 = (bf16[64,1024]{1,0:T(8,128)(2,1)S(1)}, bf16[64,1024]{1,0:T(8,128)(2,1)S(1)}, u32[]{:S(2)}, u32[]{:S(2)}) collective-permute-start(bf16[64,1024]{1,0:T(8,128)(2,1)S(1)} %collective-permute-done.refs_0_), channel_id=1, source_target_pairs={{0,8},{8,0},{1,9},{9,1},{2,10},{10,2},{3,11},{11,3},{4,12},{12,4},... | collective-permute-start | bytes 393224 | tf_op jit(solution)/shard_map/ppermute | solution.py:446
  12.3 2.4 %collective-permute-done.1.refs_2_ = bf16[64,1024]{1,0:T(8,128)(2,1)S(1)} collective-permute-done((bf16[64,1024]{1,0:T(8,128)(2,1)S(1)}, bf16[64,1024]{1,0:T(8,128)(2,1)S(1)}, u32[]{:S(2)}, u32[]{:S(2)}) %collective-permute-start.1) | collective-permute-done | bytes 131104 | tf_op jit(solution)/shard_map/ppermute | solution.py:435
  14.8 1.8 %collective-permute-start.2 = (bf16[64,1024]{1,0:T(8,128)(2,1)S(1)}, bf16[64,1024]{1,0:T(8,128)(2,1)S(1)}, u32[]{:S(2)}, u32[]{:S(2)}) collective-permute-start(bf16[64,1024]{1,0:T(8,128)(2,1)S(1)} %collective-permute-done.1.refs_2_), channel_id=1, source_target_pairs={{0,2},{2,4},{4,6},{6,7},{7,5},{5,3},{3,1},{1,0},{8,10},{10,12},{12... | collective-permute-start | bytes 393224 | tf_op jit(solution)/shard_map/ppermute | solution.py:435
  16.6 0.0 collective-permute-done.5.refs_3_
  16.6 0.2 collective-permute-start.6
  16.8 0.0 collective-permute-start.12
  16.8 0.0 collective-permute-done.10.refs_6_
  16.8 0.5 %collective-permute-start.13 = (bf16[64,1024]{1,0:T(8,128)(2,1)S(1)}, bf16[64,1024]{1,0:T(8,128)(2,1)S(1)}, u32[]{:S(2)}, u32[]{:S(2)}) collective-permute-start(bf16[64,1024]{1,0:T(8,128)(2,1)S(1)} %collective-permute-done.1.refs_2_), channel_id=1, source_target_pairs={{0,8},{8,0},{1,9},{9,1},{2,10},{10,2},{3,11},{11,3},{4,12},{12,4},... | collective-permute-start | bytes 393224 | tf_op jit(solution)/shard_map/ppermute | solution.py:446
  17.3 0.0 collective-permute-done.11.refs_7_
  17.3 0.1 collective-permute-start.14
  17.4 2.3 %collective-permute-done.2.refs_4_ = bf16[64,1024]{1,0:T(8,128)(2,1)S(1)} collective-permute-done((bf16[64,1024]{1,0:T(8,128)(2,1)S(1)}, bf16[64,1024]{1,0:T(8,128)(2,1)S(1)}, u32[]{:S(2)}, u32[]{:S(2)}) %collective-permute-start.2) | collective-permute-done | bytes 131104 | tf_op jit(solution)/shard_map/ppermute | solution.py:435
  19.7 0.0 collective-permute-start.15
  19.7 1.8 %collective-permute-done.6.refs_5_ = bf16[64,1024]{1,0:T(8,128)(2,1)S(1)} collective-permute-done((bf16[64,1024]{1,0:T(8,128)(2,1)S(1)}, bf16[64,1024]{1,0:T(8,128)(2,1)S(1)}, u32[]{:S(2)}, u32[]{:S(2)}) %collective-permute-start.6) | collective-permute-done | bytes 131104 | tf_op jit(solution)/shard_map/ppermute | solution.py:436
  21.5 0.0 collective-permute-start.16
  21.6 0.0 collective-permute-done.12.refs_8_
  21.6 1.6 %collective-permute-start.3 = (bf16[32,1024]{1,0:T(8,128)(2,1)S(1)}, bf16[32,1024]{1,0:T(8,128)(2,1)S(1)}, u32[]{:S(2)}, u32[]{:S(2)}) collective-permute-start(bf16[32,1024]{1,0:T(8,128)(2,1)S(1)} %slice.8), channel_id=1, source_target_pairs={{0,2},{2,4},{4,6},{6,7},{7,5},{5,3},{3,1},{1,0},{8,10},{10,12},{12... | collective-permute-start | bytes 196616 | tf_op jit(solution)/shard_map/ppermute | solution.py:439
  23.2 0.0 collective-permute-done.13.refs_9_
  23.2 0.4 %collective-permute-start.7 = (bf16[32,1024]{1,0:T(8,128)(2,1)S(1)}, bf16[32,1024]{1,0:T(8,128)(2,1)S(1)}, u32[]{:S(2)}, u32[]{:S(2)}) collective-permute-start(bf16[32,1024]{1,0:T(8,128)(2,1)S(1)} %slice.9), channel_id=1, source_target_pairs={{2,0},{4,2},{6,4},{7,6},{5,7},{3,5},{1,3},{0,1},{10,8},{12,10},{14... | collective-permute-start | bytes 196616 | tf_op jit(solution)/shard_map/ppermute | solution.py:440
  23.7 2.5 %collective-permute-done.3.refs_0_ = bf16[32,1024]{1,0:T(8,128)(2,1)S(1)} collective-permute-done((bf16[32,1024]{1,0:T(8,128)(2,1)S(1)}, bf16[32,1024]{1,0:T(8,128)(2,1)S(1)}, u32[]{:S(2)}, u32[]{:S(2)}) %collective-permute-start.3) | collective-permute-done | bytes 65568 | tf_op jit(solution)/shard_map/ppermute | solution.py:439
  26.1 0.0 collective-permute-start.8
  26.1 1.3 %collective-permute-done.7.refs_1_ = bf16[32,1024]{1,0:T(8,128)(2,1)S(1)} collective-permute-done((bf16[32,1024]{1,0:T(8,128)(2,1)S(1)}, bf16[32,1024]{1,0:T(8,128)(2,1)S(1)}, u32[]{:S(2)}, u32[]{:S(2)}) %collective-permute-start.7) | collective-permute-done | bytes 65568 | tf_op jit(solution)/shard_map/ppermute | solution.py:440
  27.5 0.0 collective-permute-start.9
  27.5 0.0 collective-permute-done.14.refs_10_
  27.5 0.0 collective-permute-done.15.refs_11_
  27.5 0.0 collective-permute-done.16.refs_12_
  27.5 0.0 copy-start
  27.5 0.9 %copy-done = bf16[64,1024]{1,0:T(8,128)(2,1)S(1)} copy-done((bf16[64,1024]{1,0:T(8,128)(2,1)S(1)}, bf16[64,1024]{1,0:T(8,128)(2,1)}, u32[]{:S(2)}) %copy-start) | copy-done | bytes 131096
  28.4 2.0 %shard_map.74 = (bf16[896,1024]{1,0:T(8,128)(2,1)S(1)}, f32[256,256]{1,0:T(8,128)S(1)}, f32[512,256]{1,0:T(8,128)S(1)}, f32[768,256]{1,0:T(8,128)S(1)}, f32[1024,256]{1,0:T(8,128)S(1)}) custom-call(bf16[64,1024]{1,0:T(8,128)(2,1)S(1)} %copy-done, bf16[64,1024]{1,0:T(8,128)(2,1)S(1)} %collective-permute-done.refs_0_, ...), custom_call_target="tpu_custom_call" | custom-call | flops 1879048192 | bytes 6815744 | tf_op jit(solution)/shard_map/pallas_call | solution.py:413
  30.5 0.0 collective-permute-done.8.refs_2_
  30.5 0.0 collective-permute-done.9.refs_3_
  30.5 13.5 %shard_map.75 = f32[512,128]{1,0:T(8,128)} custom-call(bf16[32,1024]{1,0:T(8,128)(2,1)S(1)} %collective-permute-done.3.refs_0_, bf16[32,1024]{1,0:T(8,128)(2,1)S(1)} %collective-permute-done.7.refs_1_, bf16[32,1024]{1,0:T(8,128)(2,1)S(1)} %collective-permute-done.8.refs_2_, bf16[32,1024]{1,0:T(8,128)(2,1)S(1)} %collective-permute-done.9.refs_3_, ...), custom_call_target="tpu_custom_call" | custom-call | tf_op jit(solution)/shard_map/pallas_call | solution.py:414
  (2 shorter events, 0.0 us)
Async XLA Ops:
  3.1 6.8 %collective-permute-start = (bf16[64,1024]{1,0:T(8,128)(2,1)}, bf16[64,1024]{1,0:T(8,128)(2,1)S(1)}, u32[]{:S(2)}, u32[]{:S(2)}) collective-permute-start(bf16[64,1024]{1,0:T(8,128)(2,1)} %shard_map.73.first_hbm), channel_id=1, source_target_pairs={{0,2},{2,4},{4,6},{6,7},{7,5},{5,3},{3,1},{1,0},{8,10},{10,12},{12... | collective-permute-start | bytes 393224 | tf_op jit(solution)/shard_map/ppermute | solution.py:435
  6.2 5.5 %collective-permute-start.4 = (bf16[64,1024]{1,0:T(8,128)(2,1)}, bf16[64,1024]{1,0:T(8,128)(2,1)S(1)}, u32[]{:S(2)}, u32[]{:S(2)}) collective-permute-start(bf16[64,1024]{1,0:T(8,128)(2,1)} %shard_map.73.first_hbm), channel_id=1, source_target_pairs={{2,0},{4,2},{6,4},{7,6},{5,7},{3,5},{1,3},{0,1},{10,8},{12,10},{14... | collective-permute-start | bytes 393224 | tf_op jit(solution)/shard_map/ppermute | solution.py:436
  9.8 5.0 %collective-permute-start.1 = (bf16[64,1024]{1,0:T(8,128)(2,1)S(1)}, bf16[64,1024]{1,0:T(8,128)(2,1)S(1)}, u32[]{:S(2)}, u32[]{:S(2)}) collective-permute-start(bf16[64,1024]{1,0:T(8,128)(2,1)S(1)} %collective-permute-done.refs_0_), channel_id=1, source_target_pairs={{0,2},{2,4},{4,6},{6,7},{7,5},{5,3},{3,1},{1,0},{8,10},{10,12},{12... | collective-permute-start | bytes 393224 | tf_op jit(solution)/shard_map/ppermute | solution.py:435
  11.6 5.0 %collective-permute-start.5 = (bf16[64,1024]{1,0:T(8,128)(2,1)S(1)}, bf16[64,1024]{1,0:T(8,128)(2,1)S(1)}, u32[]{:S(2)}, u32[]{:S(2)}) collective-permute-start(bf16[64,1024]{1,0:T(8,128)(2,1)S(1)} %collective-permute-done.4.refs_1_), channel_id=1, source_target_pairs={{2,0},{4,2},{6,4},{7,6},{5,7},{3,5},{1,3},{0,1},{10,8},{12,10},{14... | collective-permute-start | bytes 393224 | tf_op jit(solution)/shard_map/ppermute | solution.py:436
  11.8 5.0 %collective-permute-start.10 = (bf16[64,1024]{1,0:T(8,128)(2,1)}, bf16[64,1024]{1,0:T(8,128)(2,1)S(1)}, u32[]{:S(2)}, u32[]{:S(2)}) collective-permute-start(bf16[64,1024]{1,0:T(8,128)(2,1)} %shard_map.73.first_hbm), channel_id=1, source_target_pairs={{0,8},{8,0},{1,9},{9,1},{2,10},{10,2},{3,11},{11,3},{4,12},{12,4},... | collective-permute-start | bytes 393224 | tf_op jit(solution)/shard_map/ppermute | solution.py:446
  11.8 5.5 %collective-permute-start.11 = (bf16[64,1024]{1,0:T(8,128)(2,1)S(1)}, bf16[64,1024]{1,0:T(8,128)(2,1)S(1)}, u32[]{:S(2)}, u32[]{:S(2)}) collective-permute-start(bf16[64,1024]{1,0:T(8,128)(2,1)S(1)} %collective-permute-done.refs_0_), channel_id=1, source_target_pairs={{0,8},{8,0},{1,9},{9,1},{2,10},{10,2},{3,11},{11,3},{4,12},{12,4},... | collective-permute-start | bytes 393224 | tf_op jit(solution)/shard_map/ppermute | solution.py:446
  14.8 5.0 %collective-permute-start.2 = (bf16[64,1024]{1,0:T(8,128)(2,1)S(1)}, bf16[64,1024]{1,0:T(8,128)(2,1)S(1)}, u32[]{:S(2)}, u32[]{:S(2)}) collective-permute-start(bf16[64,1024]{1,0:T(8,128)(2,1)S(1)} %collective-permute-done.1.refs_2_), channel_id=1, source_target_pairs={{0,2},{2,4},{4,6},{6,7},{7,5},{5,3},{3,1},{1,0},{8,10},{10,12},{12... | collective-permute-start | bytes 393224 | tf_op jit(solution)/shard_map/ppermute | solution.py:435
  16.6 5.0 %collective-permute-start.6 = (bf16[64,1024]{1,0:T(8,128)(2,1)S(1)}, bf16[64,1024]{1,0:T(8,128)(2,1)S(1)}, u32[]{:S(2)}, u32[]{:S(2)}) collective-permute-start(bf16[64,1024]{1,0:T(8,128)(2,1)S(1)} %collective-permute-done.5.refs_3_), channel_id=1, source_target_pairs={{2,0},{4,2},{6,4},{7,6},{5,7},{3,5},{1,3},{0,1},{10,8},{12,10},{14... | collective-permute-start | bytes 393224 | tf_op jit(solution)/shard_map/ppermute | solution.py:436
  16.8 4.8 %collective-permute-start.12 = (bf16[64,1024]{1,0:T(8,128)(2,1)S(1)}, bf16[64,1024]{1,0:T(8,128)(2,1)S(1)}, u32[]{:S(2)}, u32[]{:S(2)}) collective-permute-start(bf16[64,1024]{1,0:T(8,128)(2,1)S(1)} %collective-permute-done.4.refs_1_), channel_id=1, source_target_pairs={{0,8},{8,0},{1,9},{9,1},{2,10},{10,2},{3,11},{11,3},{4,12},{12,4},... | collective-permute-start | bytes 393224 | tf_op jit(solution)/shard_map/ppermute | solution.py:446
  16.8 6.4 %collective-permute-start.13 = (bf16[64,1024]{1,0:T(8,128)(2,1)S(1)}, bf16[64,1024]{1,0:T(8,128)(2,1)S(1)}, u32[]{:S(2)}, u32[]{:S(2)}) collective-permute-start(bf16[64,1024]{1,0:T(8,128)(2,1)S(1)} %collective-permute-done.1.refs_2_), channel_id=1, source_target_pairs={{0,8},{8,0},{1,9},{9,1},{2,10},{10,2},{3,11},{11,3},{4,12},{12,4},... | collective-permute-start | bytes 393224 | tf_op jit(solution)/shard_map/ppermute | solution.py:446
  17.3 10.2 %collective-permute-start.14 = (bf16[64,1024]{1,0:T(8,128)(2,1)S(1)}, bf16[64,1024]{1,0:T(8,128)(2,1)S(1)}, u32[]{:S(2)}, u32[]{:S(2)}) collective-permute-start(bf16[64,1024]{1,0:T(8,128)(2,1)S(1)} %collective-permute-done.5.refs_3_), channel_id=1, source_target_pairs={{0,8},{8,0},{1,9},{9,1},{2,10},{10,2},{3,11},{11,3},{4,12},{12,4},... | collective-permute-start | bytes 393224 | tf_op jit(solution)/shard_map/ppermute | solution.py:446
  19.7 7.7 %collective-permute-start.15 = (bf16[64,1024]{1,0:T(8,128)(2,1)S(1)}, bf16[64,1024]{1,0:T(8,128)(2,1)S(1)}, u32[]{:S(2)}, u32[]{:S(2)}) collective-permute-start(bf16[64,1024]{1,0:T(8,128)(2,1)S(1)} %collective-permute-done.2.refs_4_), channel_id=1, source_target_pairs={{0,8},{8,0},{1,9},{9,1},{2,10},{10,2},{3,11},{11,3},{4,12},{12,4},... | collective-permute-start | bytes 393224 | tf_op jit(solution)/shard_map/ppermute | solution.py:446
  21.5 6.0 %collective-permute-start.16 = (bf16[64,1024]{1,0:T(8,128)(2,1)S(1)}, bf16[64,1024]{1,0:T(8,128)(2,1)S(1)}, u32[]{:S(2)}, u32[]{:S(2)}) collective-permute-start(bf16[64,1024]{1,0:T(8,128)(2,1)S(1)} %collective-permute-done.6.refs_5_), channel_id=1, source_target_pairs={{0,8},{8,0},{1,9},{9,1},{2,10},{10,2},{3,11},{11,3},{4,12},{12,4},... | collective-permute-start | bytes 393224 | tf_op jit(solution)/shard_map/ppermute | solution.py:446
  21.6 4.5 %collective-permute-start.3 = (bf16[32,1024]{1,0:T(8,128)(2,1)S(1)}, bf16[32,1024]{1,0:T(8,128)(2,1)S(1)}, u32[]{:S(2)}, u32[]{:S(2)}) collective-permute-start(bf16[32,1024]{1,0:T(8,128)(2,1)S(1)} %slice.8), channel_id=1, source_target_pairs={{0,2},{2,4},{4,6},{6,7},{7,5},{5,3},{3,1},{1,0},{8,10},{10,12},{12... | collective-permute-start | bytes 196616 | tf_op jit(solution)/shard_map/ppermute | solution.py:439
  23.2 4.3 %collective-permute-start.7 = (bf16[32,1024]{1,0:T(8,128)(2,1)S(1)}, bf16[32,1024]{1,0:T(8,128)(2,1)S(1)}, u32[]{:S(2)}, u32[]{:S(2)}) collective-permute-start(bf16[32,1024]{1,0:T(8,128)(2,1)S(1)} %slice.9), channel_id=1, source_target_pairs={{2,0},{4,2},{6,4},{7,6},{5,7},{3,5},{1,3},{0,1},{10,8},{12,10},{14... | collective-permute-start | bytes 196616 | tf_op jit(solution)/shard_map/ppermute | solution.py:440
  26.1 4.3 %collective-permute-start.8 = (bf16[32,1024]{1,0:T(8,128)(2,1)S(1)}, bf16[32,1024]{1,0:T(8,128)(2,1)S(1)}, u32[]{:S(2)}, u32[]{:S(2)}) collective-permute-start(bf16[32,1024]{1,0:T(8,128)(2,1)S(1)} %collective-permute-done.3.refs_0_), channel_id=1, source_target_pairs={{0,8},{8,0},{1,9},{9,1},{2,10},{10,2},{3,11},{11,3},{4,12},{12,4},... | collective-permute-start | bytes 196616 | tf_op jit(solution)/shard_map/ppermute | solution.py:446
  27.5 3.0 %collective-permute-start.9 = (bf16[32,1024]{1,0:T(8,128)(2,1)S(1)}, bf16[32,1024]{1,0:T(8,128)(2,1)S(1)}, u32[]{:S(2)}, u32[]{:S(2)}) collective-permute-start(bf16[32,1024]{1,0:T(8,128)(2,1)S(1)} %collective-permute-done.7.refs_1_), channel_id=1, source_target_pairs={{0,8},{8,0},{1,9},{9,1},{2,10},{10,2},{3,11},{11,3},{4,12},{12,4},... | collective-permute-start | bytes 196616 | tf_op jit(solution)/shard_map/ppermute | solution.py:446
  27.5 0.9 %copy-start = (bf16[64,1024]{1,0:T(8,128)(2,1)S(1)}, bf16[64,1024]{1,0:T(8,128)(2,1)}, u32[]{:S(2)}) copy-start(bf16[64,1024]{1,0:T(8,128)(2,1)} %shard_map.73.first_hbm) | copy-start | bytes 393220

commit v2 on v1

--- a/solution.py
+++ b/solution.py
@@ -203,21 +203,19 @@
     return mul(turned_ref[: (b + 2) * PANEL], ordered_ref[:, b * PANEL : (b + 2) * PANEL])
 
 
-def gram_kernel(count, pieces, first_hbm, *refs):
-    chunks, (ordered_ref, *tall_refs) = refs[:pieces], refs[pieces:-3]
-    turned_ref, first_ref, arrived = refs[-3:]
-    copy = pltpu.make_async_copy(first_hbm, first_ref, arrived)
-    copy.start()
-    copy.wait()
-    gather_panels(count, (first_ref, *chunks), ordered_ref, turned_ref)
+def gram_kernel(count, pieces, *refs):
+    chunks, before, after = refs[:pieces], refs[pieces : -2 - count // 2], refs[-2 - count // 2 :]
+    ordered_ref, *tall_refs, turned_ref = after
+    gather_panels(count, chunks, ordered_ref, turned_ref)
     for k, tall_ref in enumerate(tall_refs):
-        tall_ref[...] = tall_gram(turned_ref, ordered_ref, 2 * k)
+        tall = tall_gram(turned_ref, ordered_ref, 2 * k)
+        tall_ref[...] = tall + before[k][...] if before else tall
 
 
 def rounds_kernel(count, pieces, *refs):
     chunks, refs = refs[:pieces], refs[pieces:]
-    early_ref, tall_refs = refs[0], refs[1 : 1 + count // 2]
-    out_ref, ordered_ref, turned_ref = refs[1 + count // 2 :]
+    *earlier, out_ref, ordered_ref, turned_ref = refs
+    early_refs, tall_refs = earlier[: -(count // 2)], earlier[-(count // 2) :]
     width = PANEL
     depth = count.bit_length() - 1
     gather_panels(count, chunks, ordered_ref, turned_ref)
@@ -373,55 +371,65 @@
     chunk = own // count
     both = jnp.concatenate([high, low], axis=1)
     origins = ring_origins(count)
-    for source_ref, first, rows in ((early_ref, 0, own - chunk), (ordered_ref, count - 1, chunk)):
+    first = 0
+    for source_ref in (*early_refs, ordered_ref):
+        rows = source_ref.shape[0] // 2
         product = mul(source_ref[:rows], both)
         result = product[:, :width] + product[:, width:]
         for k in range(rows // chunk):
             start = pl.multiple_of(origins[first + k] * chunk, chunk)
             out_ref[pl.ds(start, chunk), :] = result[k * chunk : (k + 1) * chunk]
+        first += rows // chunk
+
+
+def add_gram(blocks, talls):
+    rows, total = sum(block.shape[0] for block in blocks), blocks[0].shape[1]
+    count = total // PANEL
+    inside = pl.BlockSpec(memory_space=pltpu.VMEM)
+    ordered, *talls = pl.pallas_call(
+        functools.partial(gram_kernel, count, len(blocks)),
+        out_shape=[jax.ShapeDtypeStruct((rows, total), jnp.bfloat16)]
+        + [
+            jax.ShapeDtypeStruct(((b + 2) * PANEL, 2 * PANEL), jnp.float32)
+            for b in range(0, count, 2)
+        ],
+        in_specs=[inside] * (len(blocks) + len(talls)),
+        out_specs=[inside] * (1 + count // 2),
+        input_output_aliases={len(blocks) + k: 1 + k for k in range(len(talls))},
+        scratch_shapes=[pltpu.VMEM((total, rows), jnp.bfloat16)],
+        compiler_params=pltpu.CompilerParams(vmem_limit_bytes=16 << 20),
+        cost_estimate=pl.CostEstimate(
+            flops=2 * rows * total * total,
+            bytes_accessed=4 * rows * total + 3 * total * total,
+            transcendentals=0,
+        ),
+    )(*blocks, *talls)
+    return ordered, talls
 
 
 def all_rounds(mine, other):
     total = mine[0].shape[1]
     count = total // PANEL
     inside = pl.BlockSpec(memory_space=pltpu.VMEM)
-    early = mine[:-2] + other[:-2]
+    talls, early = [], []
+    near = len(mine) // 3
+    for span in (slice(0, near), slice(near, -2)):
+        ordered, talls = add_gram(mine[span] + other[span], talls)
+        early.append(ordered)
     last = mine[-2:] + other[-2:]
-    early_rows = sum(block.shape[0] for block in early)
     last_rows = sum(block.shape[0] for block in last)
-    early_gram = pl.pallas_call(
-        functools.partial(gram_kernel, count, len(early) - 1),
-        out_shape=[jax.ShapeDtypeStruct((early_rows, total), jnp.bfloat16)]
-        + [
-            jax.ShapeDtypeStruct(((b + 2) * PANEL, 2 * PANEL), jnp.float32)
-            for b in range(0, count, 2)
-        ],
-        in_specs=[pl.BlockSpec(memory_space=pltpu.HBM)] + [inside] * (len(early) - 1),
-        out_specs=[inside] * (1 + count // 2),
-        scratch_shapes=[
-            pltpu.VMEM((total, early_rows), jnp.bfloat16),
-            pltpu.VMEM(mine[0].shape, jnp.bfloat16),
-            pltpu.SemaphoreType.DMA,
-        ],
-        compiler_params=pltpu.CompilerParams(vmem_limit_bytes=16 << 20),
-        cost_estimate=pl.CostEstimate(
-            flops=2 * early_rows * total * total,
-            bytes_accessed=4 * early_rows * total + 3 * total * total,
-            transcendentals=0,
-        ),
-    )
-    ordered, *talls = early_gram(*early)
+    own_rows = sum(block.shape[0] for block in mine)
     return pl.pallas_call(
         functools.partial(rounds_kernel, count, len(last)),
-        out_shape=jax.ShapeDtypeStruct(((early_rows + last_rows) // 2, PANEL), jnp.float32),
-        in_specs=[inside] * (len(last) + 1 + len(talls)),
+        out_shape=jax.ShapeDtypeStruct((own_rows, PANEL), jnp.float32),
+        in_specs=[inside] * (len(last) + len(early) + len(talls)),
         out_specs=inside,
         scratch_shapes=[
             pltpu.VMEM((last_rows, total), jnp.bfloat16),
             pltpu.VMEM((total, last_rows), jnp.bfloat16),
         ],
         compiler_params=pltpu.CompilerParams(vmem_limit_bytes=32 << 20),
-    )(*last, ordered, *talls)
+    )(*last, *early, *talls)
 
 
 def ring_gather(block, axis):
@@ -443,7 +451,9 @@
 
 def gathered_rounds(sketch):
     mine = ring_gather(sketch, "row")
-    other = [lax.ppermute(block, "grp", [(0, 1), (1, 0)]) for block in mine]
+    other = []
+    for block in mine:
+        other.append(lax.ppermute(block, "grp", [(0, 1), (1, 0)]))
     return all_rounds(mine, other)
 
 

time: 44.2 us -> 42.3 us (0.957)
  waiting for transfers between devices: 14.1 us -> 13 us
  local copies, waits for them, and re-layouts: 0.91 us -> 0.02 us
    ppermute x1, waiting for transfers between devices: 2.47 us -> 1.45 us  [ring_gather(): blocks.append(lax.ppermute(ahead[:middle], axis, onward))]
    unnamed x2, local copies, waits for them, and re-layouts: 0.9 us -> 0.01 us
    pallas_call x1 -> x2, Pallas kernels: 2.04 us -> 2.31 us  [add_gram(): pl.pallas_call(functools.partial(gram_kernel, count, len(blocks)), out_sh...]
where the time goes in v2:
time: 42.3 us; the launch traced here: 42.1 us
  Pallas kernels  18.6 us (44%)
  waiting for transfers between devices  13 us (31%)
  starting transfers between devices  10.3 us (24%)
    pallas_call x1, Pallas kernels, all_rounds(): pl.pallas_call(functools.partial(rounds_kernel, count, len(last)), out_sh...  13.3 us
    ppermute x3, waiting for transfers between devices, ring_gather(): ahead = lax.ppermute(ahead, axis, onward)  8.43 us
    ppermute x3, starting transfers between devices, ring_gather(): ahead = lax.ppermute(ahead, axis, onward)  6.68 us
    pallas_call x1, Pallas kernels, sketch_local(): pl.pallas_call(sketch_kernel, out_shape=jax.ShapeDtypeStruct((KB, columns...  3.04 us
    pallas_call x2, Pallas kernels, add_gram(): pl.pallas_call(functools.partial(gram_kernel, count, len(blocks)), out_sh...  2.31 us
    ppermute x3, waiting for transfers between devices, ring_gather(): behind = lax.ppermute(behind, axis, back)  1.79 us
    ppermute x1, starting transfers between devices, ring_gather(): blocks.append(lax.ppermute(ahead[:middle], axis, onward))  1.63 us
    ppermute x1, waiting for transfers between devices, ring_gather(): blocks.append(lax.ppermute(ahead[:middle], axis, onward))  1.45 us
  transfers between devices with their start and end apart: 17, of which 6 were waited for; matrix products, arithmetic and copies ran while one was open for 0% of the time, Pallas kernels for 5%

profile of v2, /device:TPU:0, one launch (start us, length us, event | category | flops | bytes accessed | tf_op | source)
XLA Modules:
  0.0 42.1 jit_solution(8637398956961159994)
XLA Ops:
  0.0 3.0 %shard_map.73.refs_0_ = bf16[64,1024]{1,0:T(8,128)(2,1)} custom-call(bf16[256,1024]{1,0:T(8,128)(2,1)} %design_hbm.1, f32[256]{0:T(256)} %target_hbm.1, bf16[1024]{0:T(1024)(128)(2,1)} %coeffs_hbm.1, s32[2]{0:T(128)} %level_ref.1, s32[256]{0:T(256)} %bucket_hbm.1, s32[256]{0:T(256)} %sign_hbm.1, s32[8]{0:T(128)} %order_ref.1), custom_call_target="tpu_custom_call" | custom-call | tf_op jit(solution)/shard_map/pallas_call | solution.py:79
  3.1 0.0 copy-start
  3.1 3.1 %collective-permute-start = (bf16[64,1024]{1,0:T(8,128)(2,1)}, bf16[64,1024]{1,0:T(8,128)(2,1)S(1)}, u32[]{:S(2)}, u32[]{:S(2)}) collective-permute-start(bf16[64,1024]{1,0:T(8,128)(2,1)} %shard_map.73.refs_0_), channel_id=1, source_target_pairs={{0,2},{2,4},{4,6},{6,7},{7,5},{5,3},{3,1},{1,0},{8,10},{10,12},{12... | collective-permute-start | bytes 393224 | tf_op jit(solution)/shard_map/ppermute | solution.py:443
  6.2 0.0 collective-permute-start.4
  6.2 3.6 %collective-permute-done.refs_1_ = bf16[64,1024]{1,0:T(8,128)(2,1)S(1)} collective-permute-done((bf16[64,1024]{1,0:T(8,128)(2,1)}, bf16[64,1024]{1,0:T(8,128)(2,1)S(1)}, u32[]{:S(2)}, u32[]{:S(2)}) %collective-permute-start) | collective-permute-done | bytes 131104 | tf_op jit(solution)/shard_map/ppermute | solution.py:443
  9.8 1.8 %collective-permute-start.1 = (bf16[64,1024]{1,0:T(8,128)(2,1)S(1)}, bf16[64,1024]{1,0:T(8,128)(2,1)S(1)}, u32[]{:S(2)}, u32[]{:S(2)}) collective-permute-start(bf16[64,1024]{1,0:T(8,128)(2,1)S(1)} %collective-permute-done.refs_1_), channel_id=1, source_target_pairs={{0,2},{2,4},{4,6},{6,7},{7,5},{5,3},{3,1},{1,0},{8,10},{10,12},{12... | collective-permute-start | bytes 393224 | tf_op jit(solution)/shard_map/ppermute | solution.py:443
  11.6 0.0 collective-permute-done.4.refs_2_
  11.6 0.2 collective-permute-start.5
  11.9 0.0 collective-permute-start.10
  11.9 0.5 %collective-permute-start.11 = (bf16[64,1024]{1,0:T(8,128)(2,1)S(1)}, bf16[64,1024]{1,0:T(8,128)(2,1)S(1)}, u32[]{:S(2)}, u32[]{:S(2)}) collective-permute-start(bf16[64,1024]{1,0:T(8,128)(2,1)S(1)} %collective-permute-done.refs_1_), channel_id=1, source_target_pairs={{0,8},{8,0},{1,9},{9,1},{2,10},{10,2},{3,11},{11,3},{4,12},{12,4},... | collective-permute-start | bytes 393224 | tf_op jit(solution)/shard_map/ppermute | solution.py:456
  12.4 2.4 %collective-permute-done.1.refs_0_ = bf16[64,1024]{1,0:T(8,128)(2,1)S(1)} collective-permute-done((bf16[64,1024]{1,0:T(8,128)(2,1)S(1)}, bf16[64,1024]{1,0:T(8,128)(2,1)S(1)}, u32[]{:S(2)}, u32[]{:S(2)}) %collective-permute-start.1) | collective-permute-done | bytes 131104 | tf_op jit(solution)/shard_map/ppermute | solution.py:443
  14.8 1.8 %collective-permute-start.2 = (bf16[64,1024]{1,0:T(8,128)(2,1)S(1)}, bf16[64,1024]{1,0:T(8,128)(2,1)S(1)}, u32[]{:S(2)}, u32[]{:S(2)}) collective-permute-start(bf16[64,1024]{1,0:T(8,128)(2,1)S(1)} %collective-permute-done.1.refs_0_), channel_id=1, source_target_pairs={{0,2},{2,4},{4,6},{6,7},{7,5},{5,3},{3,1},{1,0},{8,10},{10,12},{12... | collective-permute-start | bytes 393224 | tf_op jit(solution)/shard_map/ppermute | solution.py:443
  16.6 0.0 collective-permute-done.5.refs_1_
  16.6 0.2 collective-permute-start.6
  16.8 0.0 collective-permute-start.12
  16.8 0.0 collective-permute-done.10.refs_3_
  16.8 0.5 %collective-permute-start.13 = (bf16[64,1024]{1,0:T(8,128)(2,1)S(1)}, bf16[64,1024]{1,0:T(8,128)(2,1)S(1)}, u32[]{:S(2)}, u32[]{:S(2)}) collective-permute-start(bf16[64,1024]{1,0:T(8,128)(2,1)S(1)} %collective-permute-done.1.refs_0_), channel_id=1, source_target_pairs={{0,8},{8,0},{1,9},{9,1},{2,10},{10,2},{3,11},{11,3},{4,12},{12,4},... | collective-permute-start | bytes 393224 | tf_op jit(solution)/shard_map/ppermute | solution.py:456
  17.3 0.0 collective-permute-done.11.refs_4_
  17.3 0.1 collective-permute-start.14
  17.4 2.3 %collective-permute-done.2.refs_2_ = bf16[64,1024]{1,0:T(8,128)(2,1)S(1)} collective-permute-done((bf16[64,1024]{1,0:T(8,128)(2,1)S(1)}, bf16[64,1024]{1,0:T(8,128)(2,1)S(1)}, u32[]{:S(2)}, u32[]{:S(2)}) %collective-permute-start.2) | collective-permute-done | bytes 131104 | tf_op jit(solution)/shard_map/ppermute | solution.py:443
  19.8 0.0 collective-permute-start.15
  19.8 1.8 %collective-permute-done.6.refs_3_ = bf16[64,1024]{1,0:T(8,128)(2,1)S(1)} collective-permute-done((bf16[64,1024]{1,0:T(8,128)(2,1)S(1)}, bf16[64,1024]{1,0:T(8,128)(2,1)S(1)}, u32[]{:S(2)}, u32[]{:S(2)}) %collective-permute-start.6) | collective-permute-done | bytes 131104 | tf_op jit(solution)/shard_map/ppermute | solution.py:444
  21.6 0.0 collective-permute-start.16
  21.6 0.0 collective-permute-done.12.refs_5_
  21.6 1.6 %collective-permute-start.3 = (bf16[32,1024]{1,0:T(8,128)(2,1)S(1)}, bf16[32,1024]{1,0:T(8,128)(2,1)S(1)}, u32[]{:S(2)}, u32[]{:S(2)}) collective-permute-start(bf16[32,1024]{1,0:T(8,128)(2,1)S(1)} %slice.8), channel_id=1, source_target_pairs={{0,2},{2,4},{4,6},{6,7},{7,5},{5,3},{3,1},{1,0},{8,10},{10,12},{12... | collective-permute-start | bytes 196616 | tf_op jit(solution)/shard_map/ppermute | solution.py:447
  23.2 0.0 collective-permute-done.13.refs_4_
  23.2 0.4 %collective-permute-start.7 = (bf16[32,1024]{1,0:T(8,128)(2,1)S(1)}, bf16[32,1024]{1,0:T(8,128)(2,1)S(1)}, u32[]{:S(2)}, u32[]{:S(2)}) collective-permute-start(bf16[32,1024]{1,0:T(8,128)(2,1)S(1)} %slice.9), channel_id=1, source_target_pairs={{2,0},{4,2},{6,4},{7,6},{5,7},{3,5},{1,3},{0,1},{10,8},{12,10},{14... | collective-permute-start | bytes 196616 | tf_op jit(solution)/shard_map/ppermute | solution.py:448
  23.7 0.0 copy-done
  23.7 1.0 %shard_map.74 = (bf16[384,1024]{1,0:T(8,128)(2,1)S(1)}, f32[256,256]{1,0:T(8,128)S(1)}, f32[512,256]{1,0:T(8,128)S(1)}, f32[768,256]{1,0:T(8,128)S(1)}, f32[1024,256]{1,0:T(8,128)S(1)}) custom-call(bf16[64,1024]{1,0:T(8,128)(2,1)S(1)} %copy-done, bf16[64,1024]{1,0:T(8,128)(2,1)S(1)} %collective-permute-done.refs_1_, ...), custom_call_target="tpu_custom_call" | custom-call | flops 805306368 | bytes 4718592 | tf_op jit(solution)/shard_map/pallas_call | solution.py:389
  24.7 1.4 %collective-permute-done.3.refs_0_ = bf16[32,1024]{1,0:T(8,128)(2,1)S(1)} collective-permute-done((bf16[32,1024]{1,0:T(8,128)(2,1)S(1)}, bf16[32,1024]{1,0:T(8,128)(2,1)S(1)}, u32[]{:S(2)}, u32[]{:S(2)}) %collective-permute-start.3) | collective-permute-done | bytes 65568 | tf_op jit(solution)/shard_map/ppermute | solution.py:447
  26.1 0.0 collective-permute-start.8
  26.1 1.3 %collective-permute-done.7.refs_1_ = bf16[32,1024]{1,0:T(8,128)(2,1)S(1)} collective-permute-done((bf16[32,1024]{1,0:T(8,128)(2,1)S(1)}, bf16[32,1024]{1,0:T(8,128)(2,1)S(1)}, u32[]{:S(2)}, u32[]{:S(2)}) %collective-permute-start.7) | collective-permute-done | bytes 65568 | tf_op jit(solution)/shard_map/ppermute | solution.py:448
  27.5 0.0 collective-permute-start.9
  27.5 0.0 collective-permute-done.14.refs_5_
  27.5 0.0 collective-permute-done.15.refs_6_
  27.5 0.0 collective-permute-done.16.refs_7_
  27.5 1.3 %shard_map.75 = (bf16[512,1024]{1,0:T(8,128)(2,1)S(1)}, f32[256,256]{1,0:T(8,128)S(1)}, f32[512,256]{1,0:T(8,128)S(1)}, f32[768,256]{1,0:T(8,128)S(1)}, f32[1024,256]{1,0:T(8,128)S(1)}) custom-call(bf16[64,1024]{1,0:T(8,128)(2,1)S(1)} %collective-permute-done.1.refs_0_, ...), custom_call_target="tpu_custom_call", output_to_operand_aliasing={{1}: (8, {}), {2}: (9, {}), {3}: (10, {}), {4}: (11, {})} | custom-call | flops 1073741824 | bytes 5242880 | tf_op jit(solution)/shard_map/pallas_call | solution.py:389
  28.8 0.0 collective-permute-done.8.refs_2_
  28.8 0.0 collective-permute-done.9.refs_3_
  28.8 13.3 %shard_map.76 = f32[512,128]{1,0:T(8,128)} custom-call(bf16[32,1024]{1,0:T(8,128)(2,1)S(1)} %collective-permute-done.3.refs_0_, bf16[32,1024]{1,0:T(8,128)(2,1)S(1)} %collective-permute-done.7.refs_1_, bf16[32,1024]{1,0:T(8,128)(2,1)S(1)} %collective-permute-done.8.refs_2_, bf16[32,1024]{1,0:T(8,128)(2,1)S(1)} %collective-permute-done.9.refs_3_, ...), custom_call_target="tpu_custom_call" | custom-call | tf_op jit(solution)/shard_map/pallas_call | solution.py:422
  (2 shorter events, 0.0 us)
Async XLA Ops:
  3.1 20.6 %copy-start = (bf16[64,1024]{1,0:T(8,128)(2,1)S(1)}, bf16[64,1024]{1,0:T(8,128)(2,1)}, u32[]{:S(2)}) copy-start(bf16[64,1024]{1,0:T(8,128)(2,1)} %shard_map.73.refs_0_) | copy-start | bytes 393220
  3.1 6.8 %collective-permute-start = (bf16[64,1024]{1,0:T(8,128)(2,1)}, bf16[64,1024]{1,0:T(8,128)(2,1)S(1)}, u32[]{:S(2)}, u32[]{:S(2)}) collective-permute-start(bf16[64,1024]{1,0:T(8,128)(2,1)} %shard_map.73.refs_0_), channel_id=1, source_target_pairs={{0,2},{2,4},{4,6},{6,7},{7,5},{5,3},{3,1},{1,0},{8,10},{10,12},{12... | collective-permute-start | bytes 393224 | tf_op jit(solution)/shard_map/ppermute | solution.py:443
  6.2 5.5 %collective-permute-start.4 = (bf16[64,1024]{1,0:T(8,128)(2,1)}, bf16[64,1024]{1,0:T(8,128)(2,1)S(1)}, u32[]{:S(2)}, u32[]{:S(2)}) collective-permute-start(bf16[64,1024]{1,0:T(8,128)(2,1)} %shard_map.73.refs_0_), channel_id=1, source_target_pairs={{2,0},{4,2},{6,4},{7,6},{5,7},{3,5},{1,3},{0,1},{10,8},{12,10},{14... | collective-permute-start | bytes 393224 | tf_op jit(solution)/shard_map/ppermute | solution.py:444
  9.8 5.0 %collective-permute-start.1 = (bf16[64,1024]{1,0:T(8,128)(2,1)S(1)}, bf16[64,1024]{1,0:T(8,128)(2,1)S(1)}, u32[]{:S(2)}, u32[]{:S(2)}) collective-permute-start(bf16[64,1024]{1,0:T(8,128)(2,1)S(1)} %collective-permute-done.refs_1_), channel_id=1, source_target_pairs={{0,2},{2,4},{4,6},{6,7},{7,5},{5,3},{3,1},{1,0},{8,10},{10,12},{12... | collective-permute-start | bytes 393224 | tf_op jit(solution)/shard_map/ppermute | solution.py:443
  11.6 5.0 %collective-permute-start.5 = (bf16[64,1024]{1,0:T(8,128)(2,1)S(1)}, bf16[64,1024]{1,0:T(8,128)(2,1)S(1)}, u32[]{:S(2)}, u32[]{:S(2)}) collective-permute-start(bf16[64,1024]{1,0:T(8,128)(2,1)S(1)} %collective-permute-done.4.refs_2_), channel_id=1, source_target_pairs={{2,0},{4,2},{6,4},{7,6},{5,7},{3,5},{1,3},{0,1},{10,8},{12,10},{14... | collective-permute-start | bytes 393224 | tf_op jit(solution)/shard_map/ppermute | solution.py:444
  11.9 5.0 %collective-permute-start.10 = (bf16[64,1024]{1,0:T(8,128)(2,1)}, bf16[64,1024]{1,0:T(8,128)(2,1)S(1)}, u32[]{:S(2)}, u32[]{:S(2)}) collective-permute-start(bf16[64,1024]{1,0:T(8,128)(2,1)} %shard_map.73.refs_0_), channel_id=1, source_target_pairs={{0,8},{8,0},{1,9},{9,1},{2,10},{10,2},{3,11},{11,3},{4,12},{12,4},... | collective-permute-start | bytes 393224 | tf_op jit(solution)/shard_map/ppermute | solution.py:456
  11.9 5.5 %collective-permute-start.11 = (bf16[64,1024]{1,0:T(8,128)(2,1)S(1)}, bf16[64,1024]{1,0:T(8,128)(2,1)S(1)}, u32[]{:S(2)}, u32[]{:S(2)}) collective-permute-start(bf16[64,1024]{1,0:T(8,128)(2,1)S(1)} %collective-permute-done.refs_1_), channel_id=1, source_target_pairs={{0,8},{8,0},{1,9},{9,1},{2,10},{10,2},{3,11},{11,3},{4,12},{12,4},... | collective-permute-start | bytes 393224 | tf_op jit(solution)/shard_map/ppermute | solution.py:456
  14.8 5.0 %collective-permute-start.2 = (bf16[64,1024]{1,0:T(8,128)(2,1)S(1)}, bf16[64,1024]{1,0:T(8,128)(2,1)S(1)}, u32[]{:S(2)}, u32[]{:S(2)}) collective-permute-start(bf16[64,1024]{1,0:T(8,128)(2,1)S(1)} %collective-permute-done.1.refs_0_), channel_id=1, source_target_pairs={{0,2},{2,4},{4,6},{6,7},{7,5},{5,3},{3,1},{1,0},{8,10},{10,12},{12... | collective-permute-start | bytes 393224 | tf_op jit(solution)/shard_map/ppermute | solution.py:443
  16.6 5.0 %collective-permute-start.6 = (bf16[64,1024]{1,0:T(8,128)(2,1)S(1)}, bf16[64,1024]{1,0:T(8,128)(2,1)S(1)}, u32[]{:S(2)}, u32[]{:S(2)}) collective-permute-start(bf16[64,1024]{1,0:T(8,128)(2,1)S(1)} %collective-permute-done.5.refs_1_), channel_id=1, source_target_pairs={{2,0},{4,2},{6,4},{7,6},{5,7},{3,5},{1,3},{0,1},{10,8},{12,10},{14... | collective-permute-start | bytes 393224 | tf_op jit(solution)/shard_map/ppermute | solution.py:444
  16.8 4.8 %collective-permute-start.12 = (bf16[64,1024]{1,0:T(8,128)(2,1)S(1)}, bf16[64,1024]{1,0:T(8,128)(2,1)S(1)}, u32[]{:S(2)}, u32[]{:S(2)}) collective-permute-start(bf16[64,1024]{1,0:T(8,128)(2,1)S(1)} %collective-permute-done.4.refs_2_), channel_id=1, source_target_pairs={{0,8},{8,0},{1,9},{9,1},{2,10},{10,2},{3,11},{11,3},{4,12},{12,4},... | collective-permute-start | bytes 393224 | tf_op jit(solution)/shard_map/ppermute | solution.py:456
  16.8 6.4 %collective-permute-start.13 = (bf16[64,1024]{1,0:T(8,128)(2,1)S(1)}, bf16[64,1024]{1,0:T(8,128)(2,1)S(1)}, u32[]{:S(2)}, u32[]{:S(2)}) collective-permute-start(bf16[64,1024]{1,0:T(8,128)(2,1)S(1)} %collective-permute-done.1.refs_0_), channel_id=1, source_target_pairs={{0,8},{8,0},{1,9},{9,1},{2,10},{10,2},{3,11},{11,3},{4,12},{12,4},... | collective-permute-start | bytes 393224 | tf_op jit(solution)/shard_map/ppermute | solution.py:456
  17.3 10.2 %collective-permute-start.14 = (bf16[64,1024]{1,0:T(8,128)(2,1)S(1)}, bf16[64,1024]{1,0:T(8,128)(2,1)S(1)}, u32[]{:S(2)}, u32[]{:S(2)}) collective-permute-start(bf16[64,1024]{1,0:T(8,128)(2,1)S(1)} %collective-permute-done.5.refs_1_), channel_id=1, source_target_pairs={{0,8},{8,0},{1,9},{9,1},{2,10},{10,2},{3,11},{11,3},{4,12},{12,4},... | collective-permute-start | bytes 393224 | tf_op jit(solution)/shard_map/ppermute | solution.py:456
  19.8 7.7 %collective-permute-start.15 = (bf16[64,1024]{1,0:T(8,128)(2,1)S(1)}, bf16[64,1024]{1,0:T(8,128)(2,1)S(1)}, u32[]{:S(2)}, u32[]{:S(2)}) collective-permute-start(bf16[64,1024]{1,0:T(8,128)(2,1)S(1)} %collective-permute-done.2.refs_2_), channel_id=1, source_target_pairs={{0,8},{8,0},{1,9},{9,1},{2,10},{10,2},{3,11},{11,3},{4,12},{12,4},... | collective-permute-start | bytes 393224 | tf_op jit(solution)/shard_map/ppermute | solution.py:456
  21.6 6.0 %collective-permute-start.16 = (bf16[64,1024]{1,0:T(8,128)(2,1)S(1)}, bf16[64,1024]{1,0:T(8,128)(2,1)S(1)}, u32[]{:S(2)}, u32[]{:S(2)}) collective-permute-start(bf16[64,1024]{1,0:T(8,128)(2,1)S(1)} %collective-permute-done.6.refs_3_), channel_id=1, source_target_pairs={{0,8},{8,0},{1,9},{9,1},{2,10},{10,2},{3,11},{11,3},{4,12},{12,4},... | collective-permute-start | bytes 393224 | tf_op jit(solution)/shard_map/ppermute | solution.py:456
  21.6 4.5 %collective-permute-start.3 = (bf16[32,1024]{1,0:T(8,128)(2,1)S(1)}, bf16[32,1024]{1,0:T(8,128)(2,1)S(1)}, u32[]{:S(2)}, u32[]{:S(2)}) collective-permute-start(bf16[32,1024]{1,0:T(8,128)(2,1)S(1)} %slice.8), channel_id=1, source_target_pairs={{0,2},{2,4},{4,6},{6,7},{7,5},{5,3},{3,1},{1,0},{8,10},{10,12},{12... | collective-permute-start | bytes 196616 | tf_op jit(solution)/shard_map/ppermute | solution.py:447
  23.2 4.3 %collective-permute-start.7 = (bf16[32,1024]{1,0:T(8,128)(2,1)S(1)}, bf16[32,1024]{1,0:T(8,128)(2,1)S(1)}, u32[]{:S(2)}, u32[]{:S(2)}) collective-permute-start(bf16[32,1024]{1,0:T(8,128)(2,1)S(1)} %slice.9), channel_id=1, source_target_pairs={{2,0},{4,2},{6,4},{7,6},{5,7},{3,5},{1,3},{0,1},{10,8},{12,10},{14... | collective-permute-start | bytes 196616 | tf_op jit(solution)/shard_map/ppermute | solution.py:448
  26.1 2.7 %collective-permute-start.8 = (bf16[32,1024]{1,0:T(8,128)(2,1)S(1)}, bf16[32,1024]{1,0:T(8,128)(2,1)S(1)}, u32[]{:S(2)}, u32[]{:S(2)}) collective-permute-start(bf16[32,1024]{1,0:T(8,128)(2,1)S(1)} %collective-permute-done.3.refs_0_), channel_id=1, source_target_pairs={{0,8},{8,0},{1,9},{9,1},{2,10},{10,2},{3,11},{11,3},{4,12},{12,4},... | collective-permute-start | bytes 196616 | tf_op jit(solution)/shard_map/ppermute | solution.py:456
  27.5 1.3 %collective-permute-start.9 = (bf16[32,1024]{1,0:T(8,128)(2,1)S(1)}, bf16[32,1024]{1,0:T(8,128)(2,1)S(1)}, u32[]{:S(2)}, u32[]{:S(2)}) collective-permute-start(bf16[32,1024]{1,0:T(8,128)(2,1)S(1)} %collective-permute-done.7.refs_1_), channel_id=1, source_target_pairs={{0,8},{8,0},{1,9},{9,1},{2,10},{10,2},{3,11},{11,3},{4,12},{12,4},... | collective-permute-start | bytes 196616 | tf_op jit(solution)/shard_map/ppermute | solution.py:456

commit v3 on v2

--- a/solution.py
+++ b/solution.py
@@ -24,19 +24,12 @@
     return lax.ppermute(block, axis, route)
 
 
-def sketch_kernel(design_hbm, target_hbm, coeffs_hbm, level_ref, bucket_hbm, sign_hbm, order_ref,
-                  out_ref, design_ref, target_ref, coeffs_ref, bucket_ref, sign_ref, arrived):
+def sketch_kernel(*refs):
+    sources, out_ref, places, arrived = refs[:7], refs[7], refs[8:15], refs[15]
+    design_ref, target_ref, coeffs_ref, level_ref, bucket_ref, sign_ref, order_ref = places
     copies = [
         pltpu.make_async_copy(source, here, arrived.at[i])
-        for i, (source, here) in enumerate(
-            [
-                (coeffs_hbm, coeffs_ref),
-                (design_hbm, design_ref),
-                (target_hbm, target_ref),
-                (bucket_hbm, bucket_ref),
-                (sign_hbm, sign_ref),
-            ]
-        )
+        for i, (source, here) in enumerate(zip(sources, places))
     ]
     for copy in copies:
         copy.start()
@@ -75,19 +68,20 @@
 def sketch_local(design, target, coeffs, tau_level, bucket, sign_bit, panel_order):
     rows, columns = design.shape
     anywhere = pl.BlockSpec(memory_space=pltpu.HBM)
-    numbers = pl.BlockSpec(memory_space=pltpu.SMEM)
     return pl.pallas_call(
         sketch_kernel,
         out_shape=jax.ShapeDtypeStruct((KB, columns), jnp.bfloat16),
-        in_specs=[anywhere] * 3 + [numbers] + [anywhere] * 2 + [numbers],
+        in_specs=[anywhere] * 7,
         out_specs=pl.BlockSpec(memory_space=pltpu.VMEM),
         scratch_shapes=[
             pltpu.VMEM((rows, columns), jnp.bfloat16),
             pltpu.VMEM((rows,), jnp.float32),
             pltpu.VMEM((columns,), jnp.bfloat16),
+            pltpu.SMEM(tau_level.shape, jnp.int32),
             pltpu.VMEM((rows,), jnp.int32),
             pltpu.VMEM((rows,), jnp.int32),
-            pltpu.SemaphoreType.DMA((5,)),
+            pltpu.SMEM(panel_order.shape, jnp.int32),
+            pltpu.SemaphoreType.DMA((7,)),
         ],
         compiler_params=pltpu.CompilerParams(vmem_limit_bytes=67043328),
     )(design, target, coeffs, tau_level, bucket, sign_bit, panel_order)

time: 42.3 us -> 41.6 us (0.983)
  Pallas kernels: 18.6 us -> 18 us
    pallas_call x1, Pallas kernels: 3.04 us -> 2.39 us  [sketch_local(): pl.pallas_call(sketch_kernel, out_shape=jax.ShapeDtypeStruct((KB, columns...]
  transfers between devices with their start and end apart: 17 -> 17, of which waited for: 6 -> 6; matrix products, arithmetic and copies ran while one was open for 0% -> 0% of each run, Pallas kernels for 5% -> 6%
where the time goes in v3:
time: 41.6 us; the launch traced here: 41.5 us
  Pallas kernels  18 us (43%)
  waiting for transfers between devices  13 us (31%)
  starting transfers between devices  10.3 us (25%)
    pallas_call x1, Pallas kernels, all_rounds(): pl.pallas_call(functools.partial(rounds_kernel, count, len(last)), out_sh...  13.3 us
    ppermute x3, waiting for transfers between devices, ring_gather(): ahead = lax.ppermute(ahead, axis, onward)  8.43 us
    ppermute x3, starting transfers between devices, ring_gather(): ahead = lax.ppermute(ahead, axis, onward)  6.68 us
    pallas_call x1, Pallas kernels, sketch_local(): pl.pallas_call(sketch_kernel, out_shape=jax.ShapeDtypeStruct((KB, columns...  2.39 us
    pallas_call x2, Pallas kernels, add_gram(): pl.pallas_call(functools.partial(gram_kernel, count, len(blocks)), out_sh...  2.32 us
    ppermute x3, waiting for transfers between devices, ring_gather(): behind = lax.ppermute(behind, axis, back)  1.79 us
    ppermute x1, starting transfers between devices, ring_gather(): blocks.append(lax.ppermute(ahead[:middle], axis, onward))  1.63 us
    ppermute x1, waiting for transfers between devices, ring_gather(): blocks.append(lax.ppermute(ahead[:middle], axis, onward))  1.45 us
  transfers between devices with their start and end apart: 17, of which 6 were waited for; matrix products, arithmetic and copies ran while one was open for 0% of the time, Pallas kernels for 6%

profile of v3, /device:TPU:0, one launch (start us, length us, event | category | flops | bytes accessed | tf_op | source)
XLA Modules:
  0.0 41.5 jit_solution(4974495398075357794)
XLA Ops:
  0.0 2.4 %shard_map.73.refs_0_ = bf16[64,1024]{1,0:T(8,128)(2,1)} custom-call(bf16[256,1024]{1,0:T(8,128)(2,1)} %refs_0_.1, f32[256]{0:T(256)} %refs_1_.1, bf16[1024]{0:T(1024)(128)(2,1)} %refs_2_.1, s32[2]{0:T(128)} %refs_3_.1, s32[256]{0:T(256)} %refs_4_.1, s32[256]{0:T(256)} %refs_5_.1, s32[8]{0:T(128)} %refs_6_.1), custom_call_target="tpu_custom_call" | custom-call | tf_op jit(solution)/shard_map/pallas_call | solution.py:71
  2.4 0.0 copy-start
  2.4 3.1 %collective-permute-start = (bf16[64,1024]{1,0:T(8,128)(2,1)}, bf16[64,1024]{1,0:T(8,128)(2,1)S(1)}, u32[]{:S(2)}, u32[]{:S(2)}) collective-permute-start(bf16[64,1024]{1,0:T(8,128)(2,1)} %shard_map.73.refs_0_), channel_id=1, source_target_pairs={{0,2},{2,4},{4,6},{6,7},{7,5},{5,3},{3,1},{1,0},{8,10},{10,12},{12... | collective-permute-start | bytes 393224 | tf_op jit(solution)/shard_map/ppermute | solution.py:437
  5.5 0.0 collective-permute-start.4
  5.5 3.7 %collective-permute-done.refs_1_ = bf16[64,1024]{1,0:T(8,128)(2,1)S(1)} collective-permute-done((bf16[64,1024]{1,0:T(8,128)(2,1)}, bf16[64,1024]{1,0:T(8,128)(2,1)S(1)}, u32[]{:S(2)}, u32[]{:S(2)}) %collective-permute-start) | collective-permute-done | bytes 131104 | tf_op jit(solution)/shard_map/ppermute | solution.py:437
  9.2 1.8 %collective-permute-start.1 = (bf16[64,1024]{1,0:T(8,128)(2,1)S(1)}, bf16[64,1024]{1,0:T(8,128)(2,1)S(1)}, u32[]{:S(2)}, u32[]{:S(2)}) collective-permute-start(bf16[64,1024]{1,0:T(8,128)(2,1)S(1)} %collective-permute-done.refs_1_), channel_id=1, source_target_pairs={{0,2},{2,4},{4,6},{6,7},{7,5},{5,3},{3,1},{1,0},{8,10},{10,12},{12... | collective-permute-start | bytes 393224 | tf_op jit(solution)/shard_map/ppermute | solution.py:437
  11.0 0.0 collective-permute-done.4.refs_2_
  11.0 0.2 collective-permute-start.5
  11.2 0.0 collective-permute-start.10
  11.2 0.5 %collective-permute-start.11 = (bf16[64,1024]{1,0:T(8,128)(2,1)S(1)}, bf16[64,1024]{1,0:T(8,128)(2,1)S(1)}, u32[]{:S(2)}, u32[]{:S(2)}) collective-permute-start(bf16[64,1024]{1,0:T(8,128)(2,1)S(1)} %collective-permute-done.refs_1_), channel_id=1, source_target_pairs={{0,8},{8,0},{1,9},{9,1},{2,10},{10,2},{3,11},{11,3},{4,12},{12,4},... | collective-permute-start | bytes 393224 | tf_op jit(solution)/shard_map/ppermute | solution.py:450
  11.7 2.4 %collective-permute-done.1.refs_0_ = bf16[64,1024]{1,0:T(8,128)(2,1)S(1)} collective-permute-done((bf16[64,1024]{1,0:T(8,128)(2,1)S(1)}, bf16[64,1024]{1,0:T(8,128)(2,1)S(1)}, u32[]{:S(2)}, u32[]{:S(2)}) %collective-permute-start.1) | collective-permute-done | bytes 131104 | tf_op jit(solution)/shard_map/ppermute | solution.py:437
  14.1 1.8 %collective-permute-start.2 = (bf16[64,1024]{1,0:T(8,128)(2,1)S(1)}, bf16[64,1024]{1,0:T(8,128)(2,1)S(1)}, u32[]{:S(2)}, u32[]{:S(2)}) collective-permute-start(bf16[64,1024]{1,0:T(8,128)(2,1)S(1)} %collective-permute-done.1.refs_0_), channel_id=1, source_target_pairs={{0,2},{2,4},{4,6},{6,7},{7,5},{5,3},{3,1},{1,0},{8,10},{10,12},{12... | collective-permute-start | bytes 393224 | tf_op jit(solution)/shard_map/ppermute | solution.py:437
  15.9 0.0 collective-permute-done.5.refs_1_
  15.9 0.2 collective-permute-start.6
  16.2 0.0 collective-permute-start.12
  16.2 0.0 collective-permute-done.10.refs_3_
  16.2 0.5 %collective-permute-start.13 = (bf16[64,1024]{1,0:T(8,128)(2,1)S(1)}, bf16[64,1024]{1,0:T(8,128)(2,1)S(1)}, u32[]{:S(2)}, u32[]{:S(2)}) collective-permute-start(bf16[64,1024]{1,0:T(8,128)(2,1)S(1)} %collective-permute-done.1.refs_0_), channel_id=1, source_target_pairs={{0,8},{8,0},{1,9},{9,1},{2,10},{10,2},{3,11},{11,3},{4,12},{12,4},... | collective-permute-start | bytes 393224 | tf_op jit(solution)/shard_map/ppermute | solution.py:450
  16.7 0.0 collective-permute-done.11.refs_4_
  16.7 0.1 collective-permute-start.14
  16.8 2.3 %collective-permute-done.2.refs_2_ = bf16[64,1024]{1,0:T(8,128)(2,1)S(1)} collective-permute-done((bf16[64,1024]{1,0:T(8,128)(2,1)S(1)}, bf16[64,1024]{1,0:T(8,128)(2,1)S(1)}, u32[]{:S(2)}, u32[]{:S(2)}) %collective-permute-start.2) | collective-permute-done | bytes 131104 | tf_op jit(solution)/shard_map/ppermute | solution.py:437
  19.1 0.0 collective-permute-start.15
  19.1 1.8 %collective-permute-done.6.refs_3_ = bf16[64,1024]{1,0:T(8,128)(2,1)S(1)} collective-permute-done((bf16[64,1024]{1,0:T(8,128)(2,1)S(1)}, bf16[64,1024]{1,0:T(8,128)(2,1)S(1)}, u32[]{:S(2)}, u32[]{:S(2)}) %collective-permute-start.6) | collective-permute-done | bytes 131104 | tf_op jit(solution)/shard_map/ppermute | solution.py:438
  20.9 0.0 collective-permute-start.16
  20.9 0.0 collective-permute-done.12.refs_5_
  20.9 1.6 %collective-permute-start.3 = (bf16[32,1024]{1,0:T(8,128)(2,1)S(1)}, bf16[32,1024]{1,0:T(8,128)(2,1)S(1)}, u32[]{:S(2)}, u32[]{:S(2)}) collective-permute-start(bf16[32,1024]{1,0:T(8,128)(2,1)S(1)} %slice.8), channel_id=1, source_target_pairs={{0,2},{2,4},{4,6},{6,7},{7,5},{5,3},{3,1},{1,0},{8,10},{10,12},{12... | collective-permute-start | bytes 196616 | tf_op jit(solution)/shard_map/ppermute | solution.py:441
  22.6 0.0 collective-permute-done.13.refs_4_
  22.6 0.4 %collective-permute-start.7 = (bf16[32,1024]{1,0:T(8,128)(2,1)S(1)}, bf16[32,1024]{1,0:T(8,128)(2,1)S(1)}, u32[]{:S(2)}, u32[]{:S(2)}) collective-permute-start(bf16[32,1024]{1,0:T(8,128)(2,1)S(1)} %slice.9), channel_id=1, source_target_pairs={{2,0},{4,2},{6,4},{7,6},{5,7},{3,5},{1,3},{0,1},{10,8},{12,10},{14... | collective-permute-start | bytes 196616 | tf_op jit(solution)/shard_map/ppermute | solution.py:442
  23.0 0.0 copy-done
  23.0 1.0 %shard_map.74 = (bf16[384,1024]{1,0:T(8,128)(2,1)S(1)}, f32[256,256]{1,0:T(8,128)S(1)}, f32[512,256]{1,0:T(8,128)S(1)}, f32[768,256]{1,0:T(8,128)S(1)}, f32[1024,256]{1,0:T(8,128)S(1)}) custom-call(bf16[64,1024]{1,0:T(8,128)(2,1)S(1)} %copy-done, bf16[64,1024]{1,0:T(8,128)(2,1)S(1)} %collective-permute-done.refs_1_, ...), custom_call_target="tpu_custom_call" | custom-call | flops 805306368 | bytes 4718592 | tf_op jit(solution)/shard_map/pallas_call | solution.py:383
  24.0 1.4 %collective-permute-done.3.refs_0_ = bf16[32,1024]{1,0:T(8,128)(2,1)S(1)} collective-permute-done((bf16[32,1024]{1,0:T(8,128)(2,1)S(1)}, bf16[32,1024]{1,0:T(8,128)(2,1)S(1)}, u32[]{:S(2)}, u32[]{:S(2)}) %collective-permute-start.3) | collective-permute-done | bytes 65568 | tf_op jit(solution)/shard_map/ppermute | solution.py:441
  25.5 0.0 collective-permute-start.8
  25.5 1.3 %collective-permute-done.7.refs_1_ = bf16[32,1024]{1,0:T(8,128)(2,1)S(1)} collective-permute-done((bf16[32,1024]{1,0:T(8,128)(2,1)S(1)}, bf16[32,1024]{1,0:T(8,128)(2,1)S(1)}, u32[]{:S(2)}, u32[]{:S(2)}) %collective-permute-start.7) | collective-permute-done | bytes 65568 | tf_op jit(solution)/shard_map/ppermute | solution.py:442
  26.8 0.0 collective-permute-start.9
  26.8 0.0 collective-permute-done.14.refs_5_
  26.8 0.0 collective-permute-done.15.refs_6_
  26.9 0.0 collective-permute-done.16.refs_7_
  26.9 1.3 %shard_map.75 = (bf16[512,1024]{1,0:T(8,128)(2,1)S(1)}, f32[256,256]{1,0:T(8,128)S(1)}, f32[512,256]{1,0:T(8,128)S(1)}, f32[768,256]{1,0:T(8,128)S(1)}, f32[1024,256]{1,0:T(8,128)S(1)}) custom-call(bf16[64,1024]{1,0:T(8,128)(2,1)S(1)} %collective-permute-done.1.refs_0_, ...), custom_call_target="tpu_custom_call", output_to_operand_aliasing={{1}: (8, {}), {2}: (9, {}), {3}: (10, {}), {4}: (11, {})} | custom-call | flops 1073741824 | bytes 5242880 | tf_op jit(solution)/shard_map/pallas_call | solution.py:383
  28.2 0.0 collective-permute-done.8.refs_2_
  28.2 0.0 collective-permute-done.9.refs_3_
  28.2 13.3 %shard_map.76 = f32[512,128]{1,0:T(8,128)} custom-call(bf16[32,1024]{1,0:T(8,128)(2,1)S(1)} %collective-permute-done.3.refs_0_, bf16[32,1024]{1,0:T(8,128)(2,1)S(1)} %collective-permute-done.7.refs_1_, bf16[32,1024]{1,0:T(8,128)(2,1)S(1)} %collective-permute-done.8.refs_2_, bf16[32,1024]{1,0:T(8,128)(2,1)S(1)} %collective-permute-done.9.refs_3_, ...), custom_call_target="tpu_custom_call" | custom-call | tf_op jit(solution)/shard_map/pallas_call | solution.py:416
  (2 shorter events, 0.0 us)
Async XLA Ops:
  2.4 20.6 %copy-start = (bf16[64,1024]{1,0:T(8,128)(2,1)S(1)}, bf16[64,1024]{1,0:T(8,128)(2,1)}, u32[]{:S(2)}) copy-start(bf16[64,1024]{1,0:T(8,128)(2,1)} %shard_map.73.refs_0_) | copy-start | bytes 393220
  2.4 6.8 %collective-permute-start = (bf16[64,1024]{1,0:T(8,128)(2,1)}, bf16[64,1024]{1,0:T(8,128)(2,1)S(1)}, u32[]{:S(2)}, u32[]{:S(2)}) collective-permute-start(bf16[64,1024]{1,0:T(8,128)(2,1)} %shard_map.73.refs_0_), channel_id=1, source_target_pairs={{0,2},{2,4},{4,6},{6,7},{7,5},{5,3},{3,1},{1,0},{8,10},{10,12},{12... | collective-permute-start | bytes 393224 | tf_op jit(solution)/shard_map/ppermute | solution.py:437
  5.5 5.5 %collective-permute-start.4 = (bf16[64,1024]{1,0:T(8,128)(2,1)}, bf16[64,1024]{1,0:T(8,128)(2,1)S(1)}, u32[]{:S(2)}, u32[]{:S(2)}) collective-permute-start(bf16[64,1024]{1,0:T(8,128)(2,1)} %shard_map.73.refs_0_), channel_id=1, source_target_pairs={{2,0},{4,2},{6,4},{7,6},{5,7},{3,5},{1,3},{0,1},{10,8},{12,10},{14... | collective-permute-start | bytes 393224 | tf_op jit(solution)/shard_map/ppermute | solution.py:438
  9.2 5.0 %collective-permute-start.1 = (bf16[64,1024]{1,0:T(8,128)(2,1)S(1)}, bf16[64,1024]{1,0:T(8,128)(2,1)S(1)}, u32[]{:S(2)}, u32[]{:S(2)}) collective-permute-start(bf16[64,1024]{1,0:T(8,128)(2,1)S(1)} %collective-permute-done.refs_1_), channel_id=1, source_target_pairs={{0,2},{2,4},{4,6},{6,7},{7,5},{5,3},{3,1},{1,0},{8,10},{10,12},{12... | collective-permute-start | bytes 393224 | tf_op jit(solution)/shard_map/ppermute | solution.py:437
  11.0 5.0 %collective-permute-start.5 = (bf16[64,1024]{1,0:T(8,128)(2,1)S(1)}, bf16[64,1024]{1,0:T(8,128)(2,1)S(1)}, u32[]{:S(2)}, u32[]{:S(2)}) collective-permute-start(bf16[64,1024]{1,0:T(8,128)(2,1)S(1)} %collective-permute-done.4.refs_2_), channel_id=1, source_target_pairs={{2,0},{4,2},{6,4},{7,6},{5,7},{3,5},{1,3},{0,1},{10,8},{12,10},{14... | collective-permute-start | bytes 393224 | tf_op jit(solution)/shard_map/ppermute | solution.py:438
  11.2 5.0 %collective-permute-start.10 = (bf16[64,1024]{1,0:T(8,128)(2,1)}, bf16[64,1024]{1,0:T(8,128)(2,1)S(1)}, u32[]{:S(2)}, u32[]{:S(2)}) collective-permute-start(bf16[64,1024]{1,0:T(8,128)(2,1)} %shard_map.73.refs_0_), channel_id=1, source_target_pairs={{0,8},{8,0},{1,9},{9,1},{2,10},{10,2},{3,11},{11,3},{4,12},{12,4},... | collective-permute-start | bytes 393224 | tf_op jit(solution)/shard_map/ppermute | solution.py:450
  11.2 5.5 %collective-permute-start.11 = (bf16[64,1024]{1,0:T(8,128)(2,1)S(1)}, bf16[64,1024]{1,0:T(8,128)(2,1)S(1)}, u32[]{:S(2)}, u32[]{:S(2)}) collective-permute-start(bf16[64,1024]{1,0:T(8,128)(2,1)S(1)} %collective-permute-done.refs_1_), channel_id=1, source_target_pairs={{0,8},{8,0},{1,9},{9,1},{2,10},{10,2},{3,11},{11,3},{4,12},{12,4},... | collective-permute-start | bytes 393224 | tf_op jit(solution)/shard_map/ppermute | solution.py:450
  14.1 5.0 %collective-permute-start.2 = (bf16[64,1024]{1,0:T(8,128)(2,1)S(1)}, bf16[64,1024]{1,0:T(8,128)(2,1)S(1)}, u32[]{:S(2)}, u32[]{:S(2)}) collective-permute-start(bf16[64,1024]{1,0:T(8,128)(2,1)S(1)} %collective-permute-done.1.refs_0_), channel_id=1, source_target_pairs={{0,2},{2,4},{4,6},{6,7},{7,5},{5,3},{3,1},{1,0},{8,10},{10,12},{12... | collective-permute-start | bytes 393224 | tf_op jit(solution)/shard_map/ppermute | solution.py:437
  15.9 5.0 %collective-permute-start.6 = (bf16[64,1024]{1,0:T(8,128)(2,1)S(1)}, bf16[64,1024]{1,0:T(8,128)(2,1)S(1)}, u32[]{:S(2)}, u32[]{:S(2)}) collective-permute-start(bf16[64,1024]{1,0:T(8,128)(2,1)S(1)} %collective-permute-done.5.refs_1_), channel_id=1, source_target_pairs={{2,0},{4,2},{6,4},{7,6},{5,7},{3,5},{1,3},{0,1},{10,8},{12,10},{14... | collective-permute-start | bytes 393224 | tf_op jit(solution)/shard_map/ppermute | solution.py:438
  16.2 4.8 %collective-permute-start.12 = (bf16[64,1024]{1,0:T(8,128)(2,1)S(1)}, bf16[64,1024]{1,0:T(8,128)(2,1)S(1)}, u32[]{:S(2)}, u32[]{:S(2)}) collective-permute-start(bf16[64,1024]{1,0:T(8,128)(2,1)S(1)} %collective-permute-done.4.refs_2_), channel_id=1, source_target_pairs={{0,8},{8,0},{1,9},{9,1},{2,10},{10,2},{3,11},{11,3},{4,12},{12,4},... | collective-permute-start | bytes 393224 | tf_op jit(solution)/shard_map/ppermute | solution.py:450
  16.2 6.4 %collective-permute-start.13 = (bf16[64,1024]{1,0:T(8,128)(2,1)S(1)}, bf16[64,1024]{1,0:T(8,128)(2,1)S(1)}, u32[]{:S(2)}, u32[]{:S(2)}) collective-permute-start(bf16[64,1024]{1,0:T(8,128)(2,1)S(1)} %collective-permute-done.1.refs_0_), channel_id=1, source_target_pairs={{0,8},{8,0},{1,9},{9,1},{2,10},{10,2},{3,11},{11,3},{4,12},{12,4},... | collective-permute-start | bytes 393224 | tf_op jit(solution)/shard_map/ppermute | solution.py:450
  16.7 10.2 %collective-permute-start.14 = (bf16[64,1024]{1,0:T(8,128)(2,1)S(1)}, bf16[64,1024]{1,0:T(8,128)(2,1)S(1)}, u32[]{:S(2)}, u32[]{:S(2)}) collective-permute-start(bf16[64,1024]{1,0:T(8,128)(2,1)S(1)} %collective-permute-done.5.refs_1_), channel_id=1, source_target_pairs={{0,8},{8,0},{1,9},{9,1},{2,10},{10,2},{3,11},{11,3},{4,12},{12,4},... | collective-permute-start | bytes 393224 | tf_op jit(solution)/shard_map/ppermute | solution.py:450
  19.1 7.7 %collective-permute-start.15 = (bf16[64,1024]{1,0:T(8,128)(2,1)S(1)}, bf16[64,1024]{1,0:T(8,128)(2,1)S(1)}, u32[]{:S(2)}, u32[]{:S(2)}) collective-permute-start(bf16[64,1024]{1,0:T(8,128)(2,1)S(1)} %collective-permute-done.2.refs_2_), channel_id=1, source_target_pairs={{0,8},{8,0},{1,9},{9,1},{2,10},{10,2},{3,11},{11,3},{4,12},{12,4},... | collective-permute-start | bytes 393224 | tf_op jit(solution)/shard_map/ppermute | solution.py:450
  20.9 6.0 %collective-permute-start.16 = (bf16[64,1024]{1,0:T(8,128)(2,1)S(1)}, bf16[64,1024]{1,0:T(8,128)(2,1)S(1)}, u32[]{:S(2)}, u32[]{:S(2)}) collective-permute-start(bf16[64,1024]{1,0:T(8,128)(2,1)S(1)} %collective-permute-done.6.refs_3_), channel_id=1, source_target_pairs={{0,8},{8,0},{1,9},{9,1},{2,10},{10,2},{3,11},{11,3},{4,12},{12,4},... | collective-permute-start | bytes 393224 | tf_op jit(solution)/shard_map/ppermute | solution.py:450
  20.9 4.5 %collective-permute-start.3 = (bf16[32,1024]{1,0:T(8,128)(2,1)S(1)}, bf16[32,1024]{1,0:T(8,128)(2,1)S(1)}, u32[]{:S(2)}, u32[]{:S(2)}) collective-permute-start(bf16[32,1024]{1,0:T(8,128)(2,1)S(1)} %slice.8), channel_id=1, source_target_pairs={{0,2},{2,4},{4,6},{6,7},{7,5},{5,3},{3,1},{1,0},{8,10},{10,12},{12... | collective-permute-start | bytes 196616 | tf_op jit(solution)/shard_map/ppermute | solution.py:441
  22.6 4.3 %collective-permute-start.7 = (bf16[32,1024]{1,0:T(8,128)(2,1)S(1)}, bf16[32,1024]{1,0:T(8,128)(2,1)S(1)}, u32[]{:S(2)}, u32[]{:S(2)}) collective-permute-start(bf16[32,1024]{1,0:T(8,128)(2,1)S(1)} %slice.9), channel_id=1, source_target_pairs={{2,0},{4,2},{6,4},{7,6},{5,7},{3,5},{1,3},{0,1},{10,8},{12,10},{14... | collective-permute-start | bytes 196616 | tf_op jit(solution)/shard_map/ppermute | solution.py:442
  25.5 2.7 %collective-permute-start.8 = (bf16[32,1024]{1,0:T(8,128)(2,1)S(1)}, bf16[32,1024]{1,0:T(8,128)(2,1)S(1)}, u32[]{:S(2)}, u32[]{:S(2)}) collective-permute-start(bf16[32,1024]{1,0:T(8,128)(2,1)S(1)} %collective-permute-done.3.refs_0_), channel_id=1, source_target_pairs={{0,8},{8,0},{1,9},{9,1},{2,10},{10,2},{3,11},{11,3},{4,12},{12,4},... | collective-permute-start | bytes 196616 | tf_op jit(solution)/shard_map/ppermute | solution.py:450
  26.8 1.3 %collective-permute-start.9 = (bf16[32,1024]{1,0:T(8,128)(2,1)S(1)}, bf16[32,1024]{1,0:T(8,128)(2,1)S(1)}, u32[]{:S(2)}, u32[]{:S(2)}) collective-permute-start(bf16[32,1024]{1,0:T(8,128)(2,1)S(1)} %collective-permute-done.7.refs_1_), channel_id=1, source_target_pairs={{0,8},{8,0},{1,9},{9,1},{2,10},{10,2},{3,11},{11,3},{4,12},{12,4},... | collective-permute-start | bytes 196616 | tf_op jit(solution)/shard_map/ppermute | solution.py:450

commit v4 on v3

--- a/solution.py
+++ b/solution.py
@@ -102,15 +102,16 @@
 
 
 def root_factors(grams, offs):
-    w, t, v, z = [], [], [], []
-    for gram, off in zip(grams, offs):
+    thin = [half(a) for a in offs]
+    squared = [mul(a, a) for a in thin]
+    w, t, s, z = [], [], [], []
+    for gram in grams:
         bound = jnp.max(jnp.sum(jnp.abs(gram), axis=0, keepdims=True), axis=1, keepdims=True)
         w.append(1.0 / bound)
         t.append(1.5 - 0.5 * w[-1])
-        v.append((-0.5 * w[-1] / t[-1]) * off)
+        s.append(-0.5 * w[-1] / t[-1])
         z.append(lax.rsqrt(bound))
-    s = [jnp.ones_like(a) for a in w]
-    thin = [half(a) for a in v]
+    v = offs
     doubles = []
     for step in range(NS_ITERS):
         z = [a * b for a, b in zip(z, t)]
@@ -118,7 +119,7 @@
         gain = [a * a * a / b for a, b in zip(t, after)]
         linear = [1.0 - b / a for a, b in zip(t, w)]
         square = [2.0 - 0.5 * b / a for a, b in zip(t, w)]
-        if step % 2 == 0:
+        if step:
             squared = [mul(a, a) for a in thin]
         if step % 2 == 0 and step + 2 >= NS_ITERS and step + 1 < NS_ITERS:
             parts = []
@@ -132,16 +133,22 @@
         elif step % 2 == 0 and step + 1 == NS_ITERS:
             doubles.append([c * x for c, x in zip(s, v)])
         if step + 2 < NS_ITERS or step % 2 == 1 and step + 1 < NS_ITERS:
-            if step % 2 == 1:
-                squared = [mul(a, a) for a in thin]
-            inner = [half((b / c) * x + q) for b, c, x, q in zip(square, s, v, squared)]
             before, flat, size = v, thin, s
+            if step:
+                s = [g * c * c * c for g, c in zip(gain, s)]
+                share = [jnp.ones_like(a) for a in s]
+            else:
+                s = [jnp.ones_like(a) for a in s]
+                share = [g * c * c * c for g, c in zip(gain, size)]
+            inner = [
+                half((d * b / c) * x + (d * q if step == 0 else q))
+                for d, b, c, x, q in zip(share, square, size, v, squared)
+            ]
             v = [
-                (a / (c * c)) * x + mul(r, y)
-                for a, c, x, r, y in zip(linear, s, v, inner, thin)
+                (d * a / (c * c)) * x + mul(r, y)
+                for d, a, c, x, r, y in zip(share, linear, size, v, inner, thin)
             ]
             thin = [half(a) for a in v]
-            s = [g * c * c * c for g, c in zip(gain, s)]
             if step % 2 == 0:
                 doubles.append(
                     [
@@ -159,8 +166,12 @@
     return list(zip(z, e, thin))
 
 
-def diagonal_of(block, axis):
-    return jnp.sum(jnp.where(diagonal_mask(block.shape[0]), block, 0.0), axis=axis, keepdims=True)
+def diagonal_of(block):
+    return jnp.sum(jnp.where(diagonal_mask(block.shape[0]), block, 0.0), axis=0, keepdims=True)
+
+
+def turned_rows(row):
+    return jnp.broadcast_to(row, (row.shape[1], row.shape[1])).T
 
 
 def ring_place(index, count):
@@ -230,9 +241,9 @@
                         i * width : (i + 1) * width, j * width : (j + 1) * width
                     ]
     for p in range(count):
-        total[p] = diagonal_of(grams[p, p], 0)
+        total[p] = diagonal_of(grams[p, p])
         row_scale[p] = lax.rsqrt(total[p])
-        column_scale[p] = lax.rsqrt(diagonal_of(grams[p, p], 1))
+        column_scale[p] = turned_rows(row_scale[p])
     first_scale = dict(column_scale)
     blocks = {
         (a, b): column_scale[a] * gram * row_scale[b] for (a, b), gram in grams.items()
@@ -281,9 +292,9 @@
                 for k, at in enumerate(kept[i]):
                     cut = slice(k * width, (k + 1) * width)
                     block = value[cut, cut] + jnp.where(eye, 1.0, 0.0)
-                    along = diagonal_of(block, 0)
+                    along = diagonal_of(block)
                     row_scale[pair[at]] = lax.rsqrt(along)
-                    column_scale[pair[at]] = lax.rsqrt(diagonal_of(block, 1))
+                    column_scale[pair[at]] = turned_rows(row_scale[pair[at]])
                     total[pair[at]] = total[pair[at]] * along * z * z
                     fresh[pair[at], pair[at]] = block
                     for j, to in list(enumerate(kept[i]))[k + 1 :]:

time: 41.6 us -> 40.9 us (0.983)
  Pallas kernels: 18 us -> 17.2 us
    pallas_call x1, Pallas kernels: 13.3 us -> 12.5 us  [all_rounds(): pl.pallas_call(functools.partial(rounds_kernel, count, len(last)), out_sh...]
where the time goes in v4:
time: 40.9 us; the launch traced here: 40.7 us
  Pallas kernels  17.2 us (42%)
  waiting for transfers between devices  13 us (32%)
  starting transfers between devices  10.3 us (25%)
    pallas_call x1, Pallas kernels, all_rounds(): pl.pallas_call(functools.partial(rounds_kernel, count, len(last)), out_sh...  12.5 us
    ppermute x3, waiting for transfers between devices, ring_gather(): ahead = lax.ppermute(ahead, axis, onward)  8.43 us
    ppermute x3, starting transfers between devices, ring_gather(): ahead = lax.ppermute(ahead, axis, onward)  6.68 us
    pallas_call x1, Pallas kernels, sketch_local(): pl.pallas_call(sketch_kernel, out_shape=jax.ShapeDtypeStruct((KB, columns...  2.39 us
    pallas_call x2, Pallas kernels, add_gram(): pl.pallas_call(functools.partial(gram_kernel, count, len(blocks)), out_sh...  2.32 us
    ppermute x3, waiting for transfers between devices, ring_gather(): behind = lax.ppermute(behind, axis, back)  1.79 us
    ppermute x1, starting transfers between devices, ring_gather(): blocks.append(lax.ppermute(ahead[:middle], axis, onward))  1.63 us
    ppermute x1, waiting for transfers between devices, ring_gather(): blocks.append(lax.ppermute(ahead[:middle], axis, onward))  1.45 us
  transfers between devices with their start and end apart: 17, of which 6 were waited for; matrix products, arithmetic and copies ran while one was open for 0% of the time, Pallas kernels for 6%

profile of v4, /device:TPU:0, one launch (start us, length us, event | category | flops | bytes accessed | tf_op | source)
XLA Modules:
  0.0 40.7 jit_solution(6296595320425517413)
XLA Ops:
  0.0 2.4 %shard_map.73.refs_0_ = bf16[64,1024]{1,0:T(8,128)(2,1)} custom-call(bf16[256,1024]{1,0:T(8,128)(2,1)} %refs_0_.1, f32[256]{0:T(256)} %refs_1_.1, bf16[1024]{0:T(1024)(128)(2,1)} %refs_2_.1, s32[2]{0:T(128)} %refs_3_.1, s32[256]{0:T(256)} %refs_4_.1, s32[256]{0:T(256)} %refs_5_.1, s32[8]{0:T(128)} %refs_6_.1), custom_call_target="tpu_custom_call" | custom-call | tf_op jit(solution)/shard_map/pallas_call | solution.py:71
  2.4 0.0 copy-start
  2.4 3.1 %collective-permute-start = (bf16[64,1024]{1,0:T(8,128)(2,1)}, bf16[64,1024]{1,0:T(8,128)(2,1)S(1)}, u32[]{:S(2)}, u32[]{:S(2)}) collective-permute-start(bf16[64,1024]{1,0:T(8,128)(2,1)} %shard_map.73.refs_0_), channel_id=1, source_target_pairs={{0,2},{2,4},{4,6},{6,7},{7,5},{5,3},{3,1},{1,0},{8,10},{10,12},{12... | collective-permute-start | bytes 393224 | tf_op jit(solution)/shard_map/ppermute | solution.py:448
  5.5 0.0 collective-permute-start.4
  5.5 3.7 %collective-permute-done.refs_1_ = bf16[64,1024]{1,0:T(8,128)(2,1)S(1)} collective-permute-done((bf16[64,1024]{1,0:T(8,128)(2,1)}, bf16[64,1024]{1,0:T(8,128)(2,1)S(1)}, u32[]{:S(2)}, u32[]{:S(2)}) %collective-permute-start) | collective-permute-done | bytes 131104 | tf_op jit(solution)/shard_map/ppermute | solution.py:448
  9.2 1.8 %collective-permute-start.1 = (bf16[64,1024]{1,0:T(8,128)(2,1)S(1)}, bf16[64,1024]{1,0:T(8,128)(2,1)S(1)}, u32[]{:S(2)}, u32[]{:S(2)}) collective-permute-start(bf16[64,1024]{1,0:T(8,128)(2,1)S(1)} %collective-permute-done.refs_1_), channel_id=1, source_target_pairs={{0,2},{2,4},{4,6},{6,7},{7,5},{5,3},{3,1},{1,0},{8,10},{10,12},{12... | collective-permute-start | bytes 393224 | tf_op jit(solution)/shard_map/ppermute | solution.py:448
  11.0 0.0 collective-permute-done.4.refs_2_
  11.0 0.2 collective-permute-start.5
  11.2 0.0 collective-permute-start.10
  11.2 0.5 %collective-permute-start.11 = (bf16[64,1024]{1,0:T(8,128)(2,1)S(1)}, bf16[64,1024]{1,0:T(8,128)(2,1)S(1)}, u32[]{:S(2)}, u32[]{:S(2)}) collective-permute-start(bf16[64,1024]{1,0:T(8,128)(2,1)S(1)} %collective-permute-done.refs_1_), channel_id=1, source_target_pairs={{0,8},{8,0},{1,9},{9,1},{2,10},{10,2},{3,11},{11,3},{4,12},{12,4},... | collective-permute-start | bytes 393224 | tf_op jit(solution)/shard_map/ppermute | solution.py:461
  11.7 2.4 %collective-permute-done.1.refs_0_ = bf16[64,1024]{1,0:T(8,128)(2,1)S(1)} collective-permute-done((bf16[64,1024]{1,0:T(8,128)(2,1)S(1)}, bf16[64,1024]{1,0:T(8,128)(2,1)S(1)}, u32[]{:S(2)}, u32[]{:S(2)}) %collective-permute-start.1) | collective-permute-done | bytes 131104 | tf_op jit(solution)/shard_map/ppermute | solution.py:448
  14.1 1.8 %collective-permute-start.2 = (bf16[64,1024]{1,0:T(8,128)(2,1)S(1)}, bf16[64,1024]{1,0:T(8,128)(2,1)S(1)}, u32[]{:S(2)}, u32[]{:S(2)}) collective-permute-start(bf16[64,1024]{1,0:T(8,128)(2,1)S(1)} %collective-permute-done.1.refs_0_), channel_id=1, source_target_pairs={{0,2},{2,4},{4,6},{6,7},{7,5},{5,3},{3,1},{1,0},{8,10},{10,12},{12... | collective-permute-start | bytes 393224 | tf_op jit(solution)/shard_map/ppermute | solution.py:448
  15.9 0.0 collective-permute-done.5.refs_1_
  15.9 0.2 collective-permute-start.6
  16.2 0.0 collective-permute-start.12
  16.2 0.0 collective-permute-done.10.refs_3_
  16.2 0.5 %collective-permute-start.13 = (bf16[64,1024]{1,0:T(8,128)(2,1)S(1)}, bf16[64,1024]{1,0:T(8,128)(2,1)S(1)}, u32[]{:S(2)}, u32[]{:S(2)}) collective-permute-start(bf16[64,1024]{1,0:T(8,128)(2,1)S(1)} %collective-permute-done.1.refs_0_), channel_id=1, source_target_pairs={{0,8},{8,0},{1,9},{9,1},{2,10},{10,2},{3,11},{11,3},{4,12},{12,4},... | collective-permute-start | bytes 393224 | tf_op jit(solution)/shard_map/ppermute | solution.py:461
  16.7 0.0 collective-permute-done.11.refs_4_
  16.7 0.1 collective-permute-start.14
  16.8 2.3 %collective-permute-done.2.refs_2_ = bf16[64,1024]{1,0:T(8,128)(2,1)S(1)} collective-permute-done((bf16[64,1024]{1,0:T(8,128)(2,1)S(1)}, bf16[64,1024]{1,0:T(8,128)(2,1)S(1)}, u32[]{:S(2)}, u32[]{:S(2)}) %collective-permute-start.2) | collective-permute-done | bytes 131104 | tf_op jit(solution)/shard_map/ppermute | solution.py:448
  19.1 0.0 collective-permute-start.15
  19.1 1.8 %collective-permute-done.6.refs_3_ = bf16[64,1024]{1,0:T(8,128)(2,1)S(1)} collective-permute-done((bf16[64,1024]{1,0:T(8,128)(2,1)S(1)}, bf16[64,1024]{1,0:T(8,128)(2,1)S(1)}, u32[]{:S(2)}, u32[]{:S(2)}) %collective-permute-start.6) | collective-permute-done | bytes 131104 | tf_op jit(solution)/shard_map/ppermute | solution.py:449
  20.9 0.0 collective-permute-start.16
  20.9 0.0 collective-permute-done.12.refs_5_
  20.9 1.6 %collective-permute-start.3 = (bf16[32,1024]{1,0:T(8,128)(2,1)S(1)}, bf16[32,1024]{1,0:T(8,128)(2,1)S(1)}, u32[]{:S(2)}, u32[]{:S(2)}) collective-permute-start(bf16[32,1024]{1,0:T(8,128)(2,1)S(1)} %slice.8), channel_id=1, source_target_pairs={{0,2},{2,4},{4,6},{6,7},{7,5},{5,3},{3,1},{1,0},{8,10},{10,12},{12... | collective-permute-start | bytes 196616 | tf_op jit(solution)/shard_map/ppermute | solution.py:452
  22.6 0.0 collective-permute-done.13.refs_4_
  22.6 0.4 %collective-permute-start.7 = (bf16[32,1024]{1,0:T(8,128)(2,1)S(1)}, bf16[32,1024]{1,0:T(8,128)(2,1)S(1)}, u32[]{:S(2)}, u32[]{:S(2)}) collective-permute-start(bf16[32,1024]{1,0:T(8,128)(2,1)S(1)} %slice.9), channel_id=1, source_target_pairs={{2,0},{4,2},{6,4},{7,6},{5,7},{3,5},{1,3},{0,1},{10,8},{12,10},{14... | collective-permute-start | bytes 196616 | tf_op jit(solution)/shard_map/ppermute | solution.py:453
  23.0 0.0 copy-done
  23.0 1.0 %shard_map.74 = (bf16[384,1024]{1,0:T(8,128)(2,1)S(1)}, f32[256,256]{1,0:T(8,128)S(1)}, f32[512,256]{1,0:T(8,128)S(1)}, f32[768,256]{1,0:T(8,128)S(1)}, f32[1024,256]{1,0:T(8,128)S(1)}) custom-call(bf16[64,1024]{1,0:T(8,128)(2,1)S(1)} %copy-done, bf16[64,1024]{1,0:T(8,128)(2,1)S(1)} %collective-permute-done.refs_1_, ...), custom_call_target="tpu_custom_call" | custom-call | flops 805306368 | bytes 4718592 | tf_op jit(solution)/shard_map/pallas_call | solution.py:394
  24.0 1.4 %collective-permute-done.3.refs_0_ = bf16[32,1024]{1,0:T(8,128)(2,1)S(1)} collective-permute-done((bf16[32,1024]{1,0:T(8,128)(2,1)S(1)}, bf16[32,1024]{1,0:T(8,128)(2,1)S(1)}, u32[]{:S(2)}, u32[]{:S(2)}) %collective-permute-start.3) | collective-permute-done | bytes 65568 | tf_op jit(solution)/shard_map/ppermute | solution.py:452
  25.5 0.0 collective-permute-start.8
  25.5 1.3 %collective-permute-done.7.refs_1_ = bf16[32,1024]{1,0:T(8,128)(2,1)S(1)} collective-permute-done((bf16[32,1024]{1,0:T(8,128)(2,1)S(1)}, bf16[32,1024]{1,0:T(8,128)(2,1)S(1)}, u32[]{:S(2)}, u32[]{:S(2)}) %collective-permute-start.7) | collective-permute-done | bytes 65568 | tf_op jit(solution)/shard_map/ppermute | solution.py:453
  26.8 0.0 collective-permute-start.9
  26.8 0.0 collective-permute-done.14.refs_5_
  26.8 0.0 collective-permute-done.15.refs_6_
  26.9 0.0 collective-permute-done.16.refs_7_
  26.9 1.3 %shard_map.75 = (bf16[512,1024]{1,0:T(8,128)(2,1)S(1)}, f32[256,256]{1,0:T(8,128)S(1)}, f32[512,256]{1,0:T(8,128)S(1)}, f32[768,256]{1,0:T(8,128)S(1)}, f32[1024,256]{1,0:T(8,128)S(1)}) custom-call(bf16[64,1024]{1,0:T(8,128)(2,1)S(1)} %collective-permute-done.1.refs_0_, ...), custom_call_target="tpu_custom_call", output_to_operand_aliasing={{1}: (8, {}), {2}: (9, {}), {3}: (10, {}), {4}: (11, {})} | custom-call | flops 1073741824 | bytes 5242880 | tf_op jit(solution)/shard_map/pallas_call | solution.py:394
  28.2 0.0 collective-permute-done.8.refs_2_
  28.2 0.0 collective-permute-done.9.refs_3_
  28.2 12.5 %shard_map.76 = f32[512,128]{1,0:T(8,128)} custom-call(bf16[32,1024]{1,0:T(8,128)(2,1)S(1)} %collective-permute-done.3.refs_0_, bf16[32,1024]{1,0:T(8,128)(2,1)S(1)} %collective-permute-done.7.refs_1_, bf16[32,1024]{1,0:T(8,128)(2,1)S(1)} %collective-permute-done.8.refs_2_, bf16[32,1024]{1,0:T(8,128)(2,1)S(1)} %collective-permute-done.9.refs_3_, ...), custom_call_target="tpu_custom_call" | custom-call | tf_op jit(solution)/shard_map/pallas_call | solution.py:427
  (2 shorter events, 0.0 us)
Async XLA Ops:
  2.4 20.6 %copy-start = (bf16[64,1024]{1,0:T(8,128)(2,1)S(1)}, bf16[64,1024]{1,0:T(8,128)(2,1)}, u32[]{:S(2)}) copy-start(bf16[64,1024]{1,0:T(8,128)(2,1)} %shard_map.73.refs_0_) | copy-start | bytes 393220
  2.4 6.8 %collective-permute-start = (bf16[64,1024]{1,0:T(8,128)(2,1)}, bf16[64,1024]{1,0:T(8,128)(2,1)S(1)}, u32[]{:S(2)}, u32[]{:S(2)}) collective-permute-start(bf16[64,1024]{1,0:T(8,128)(2,1)} %shard_map.73.refs_0_), channel_id=1, source_target_pairs={{0,2},{2,4},{4,6},{6,7},{7,5},{5,3},{3,1},{1,0},{8,10},{10,12},{12... | collective-permute-start | bytes 393224 | tf_op jit(solution)/shard_map/ppermute | solution.py:448
  5.5 5.5 %collective-permute-start.4 = (bf16[64,1024]{1,0:T(8,128)(2,1)}, bf16[64,1024]{1,0:T(8,128)(2,1)S(1)}, u32[]{:S(2)}, u32[]{:S(2)}) collective-permute-start(bf16[64,1024]{1,0:T(8,128)(2,1)} %shard_map.73.refs_0_), channel_id=1, source_target_pairs={{2,0},{4,2},{6,4},{7,6},{5,7},{3,5},{1,3},{0,1},{10,8},{12,10},{14... | collective-permute-start | bytes 393224 | tf_op jit(solution)/shard_map/ppermute | solution.py:449
  9.2 5.0 %collective-permute-start.1 = (bf16[64,1024]{1,0:T(8,128)(2,1)S(1)}, bf16[64,1024]{1,0:T(8,128)(2,1)S(1)}, u32[]{:S(2)}, u32[]{:S(2)}) collective-permute-start(bf16[64,1024]{1,0:T(8,128)(2,1)S(1)} %collective-permute-done.refs_1_), channel_id=1, source_target_pairs={{0,2},{2,4},{4,6},{6,7},{7,5},{5,3},{3,1},{1,0},{8,10},{10,12},{12... | collective-permute-start | bytes 393224 | tf_op jit(solution)/shard_map/ppermute | solution.py:448
  11.0 5.0 %collective-permute-start.5 = (bf16[64,1024]{1,0:T(8,128)(2,1)S(1)}, bf16[64,1024]{1,0:T(8,128)(2,1)S(1)}, u32[]{:S(2)}, u32[]{:S(2)}) collective-permute-start(bf16[64,1024]{1,0:T(8,128)(2,1)S(1)} %collective-permute-done.4.refs_2_), channel_id=1, source_target_pairs={{2,0},{4,2},{6,4},{7,6},{5,7},{3,5},{1,3},{0,1},{10,8},{12,10},{14... | collective-permute-start | bytes 393224 | tf_op jit(solution)/shard_map/ppermute | solution.py:449
  11.2 5.0 %collective-permute-start.10 = (bf16[64,1024]{1,0:T(8,128)(2,1)}, bf16[64,1024]{1,0:T(8,128)(2,1)S(1)}, u32[]{:S(2)}, u32[]{:S(2)}) collective-permute-start(bf16[64,1024]{1,0:T(8,128)(2,1)} %shard_map.73.refs_0_), channel_id=1, source_target_pairs={{0,8},{8,0},{1,9},{9,1},{2,10},{10,2},{3,11},{11,3},{4,12},{12,4},... | collective-permute-start | bytes 393224 | tf_op jit(solution)/shard_map/ppermute | solution.py:461
  11.2 5.5 %collective-permute-start.11 = (bf16[64,1024]{1,0:T(8,128)(2,1)S(1)}, bf16[64,1024]{1,0:T(8,128)(2,1)S(1)}, u32[]{:S(2)}, u32[]{:S(2)}) collective-permute-start(bf16[64,1024]{1,0:T(8,128)(2,1)S(1)} %collective-permute-done.refs_1_), channel_id=1, source_target_pairs={{0,8},{8,0},{1,9},{9,1},{2,10},{10,2},{3,11},{11,3},{4,12},{12,4},... | collective-permute-start | bytes 393224 | tf_op jit(solution)/shard_map/ppermute | solution.py:461
  14.1 5.0 %collective-permute-start.2 = (bf16[64,1024]{1,0:T(8,128)(2,1)S(1)}, bf16[64,1024]{1,0:T(8,128)(2,1)S(1)}, u32[]{:S(2)}, u32[]{:S(2)}) collective-permute-start(bf16[64,1024]{1,0:T(8,128)(2,1)S(1)} %collective-permute-done.1.refs_0_), channel_id=1, source_target_pairs={{0,2},{2,4},{4,6},{6,7},{7,5},{5,3},{3,1},{1,0},{8,10},{10,12},{12... | collective-permute-start | bytes 393224 | tf_op jit(solution)/shard_map/ppermute | solution.py:448
  15.9 5.0 %collective-permute-start.6 = (bf16[64,1024]{1,0:T(8,128)(2,1)S(1)}, bf16[64,1024]{1,0:T(8,128)(2,1)S(1)}, u32[]{:S(2)}, u32[]{:S(2)}) collective-permute-start(bf16[64,1024]{1,0:T(8,128)(2,1)S(1)} %collective-permute-done.5.refs_1_), channel_id=1, source_target_pairs={{2,0},{4,2},{6,4},{7,6},{5,7},{3,5},{1,3},{0,1},{10,8},{12,10},{14... | collective-permute-start | bytes 393224 | tf_op jit(solution)/shard_map/ppermute | solution.py:449
  16.2 4.8 %collective-permute-start.12 = (bf16[64,1024]{1,0:T(8,128)(2,1)S(1)}, bf16[64,1024]{1,0:T(8,128)(2,1)S(1)}, u32[]{:S(2)}, u32[]{:S(2)}) collective-permute-start(bf16[64,1024]{1,0:T(8,128)(2,1)S(1)} %collective-permute-done.4.refs_2_), channel_id=1, source_target_pairs={{0,8},{8,0},{1,9},{9,1},{2,10},{10,2},{3,11},{11,3},{4,12},{12,4},... | collective-permute-start | bytes 393224 | tf_op jit(solution)/shard_map/ppermute | solution.py:461
  16.2 6.4 %collective-permute-start.13 = (bf16[64,1024]{1,0:T(8,128)(2,1)S(1)}, bf16[64,1024]{1,0:T(8,128)(2,1)S(1)}, u32[]{:S(2)}, u32[]{:S(2)}) collective-permute-start(bf16[64,1024]{1,0:T(8,128)(2,1)S(1)} %collective-permute-done.1.refs_0_), channel_id=1, source_target_pairs={{0,8},{8,0},{1,9},{9,1},{2,10},{10,2},{3,11},{11,3},{4,12},{12,4},... | collective-permute-start | bytes 393224 | tf_op jit(solution)/shard_map/ppermute | solution.py:461
  16.7 10.2 %collective-permute-start.14 = (bf16[64,1024]{1,0:T(8,128)(2,1)S(1)}, bf16[64,1024]{1,0:T(8,128)(2,1)S(1)}, u32[]{:S(2)}, u32[]{:S(2)}) collective-permute-start(bf16[64,1024]{1,0:T(8,128)(2,1)S(1)} %collective-permute-done.5.refs_1_), channel_id=1, source_target_pairs={{0,8},{8,0},{1,9},{9,1},{2,10},{10,2},{3,11},{11,3},{4,12},{12,4},... | collective-permute-start | bytes 393224 | tf_op jit(solution)/shard_map/ppermute | solution.py:461
  19.1 7.7 %collective-permute-start.15 = (bf16[64,1024]{1,0:T(8,128)(2,1)S(1)}, bf16[64,1024]{1,0:T(8,128)(2,1)S(1)}, u32[]{:S(2)}, u32[]{:S(2)}) collective-permute-start(bf16[64,1024]{1,0:T(8,128)(2,1)S(1)} %collective-permute-done.2.refs_2_), channel_id=1, source_target_pairs={{0,8},{8,0},{1,9},{9,1},{2,10},{10,2},{3,11},{11,3},{4,12},{12,4},... | collective-permute-start | bytes 393224 | tf_op jit(solution)/shard_map/ppermute | solution.py:461
  20.9 6.0 %collective-permute-start.16 = (bf16[64,1024]{1,0:T(8,128)(2,1)S(1)}, bf16[64,1024]{1,0:T(8,128)(2,1)S(1)}, u32[]{:S(2)}, u32[]{:S(2)}) collective-permute-start(bf16[64,1024]{1,0:T(8,128)(2,1)S(1)} %collective-permute-done.6.refs_3_), channel_id=1, source_target_pairs={{0,8},{8,0},{1,9},{9,1},{2,10},{10,2},{3,11},{11,3},{4,12},{12,4},... | collective-permute-start | bytes 393224 | tf_op jit(solution)/shard_map/ppermute | solution.py:461
  20.9 4.5 %collective-permute-start.3 = (bf16[32,1024]{1,0:T(8,128)(2,1)S(1)}, bf16[32,1024]{1,0:T(8,128)(2,1)S(1)}, u32[]{:S(2)}, u32[]{:S(2)}) collective-permute-start(bf16[32,1024]{1,0:T(8,128)(2,1)S(1)} %slice.8), channel_id=1, source_target_pairs={{0,2},{2,4},{4,6},{6,7},{7,5},{5,3},{3,1},{1,0},{8,10},{10,12},{12... | collective-permute-start | bytes 196616 | tf_op jit(solution)/shard_map/ppermute | solution.py:452
  22.6 4.3 %collective-permute-start.7 = (bf16[32,1024]{1,0:T(8,128)(2,1)S(1)}, bf16[32,1024]{1,0:T(8,128)(2,1)S(1)}, u32[]{:S(2)}, u32[]{:S(2)}) collective-permute-start(bf16[32,1024]{1,0:T(8,128)(2,1)S(1)} %slice.9), channel_id=1, source_target_pairs={{2,0},{4,2},{6,4},{7,6},{5,7},{3,5},{1,3},{0,1},{10,8},{12,10},{14... | collective-permute-start | bytes 196616 | tf_op jit(solution)/shard_map/ppermute | solution.py:453
  25.5 2.7 %collective-permute-start.8 = (bf16[32,1024]{1,0:T(8,128)(2,1)S(1)}, bf16[32,1024]{1,0:T(8,128)(2,1)S(1)}, u32[]{:S(2)}, u32[]{:S(2)}) collective-permute-start(bf16[32,1024]{1,0:T(8,128)(2,1)S(1)} %collective-permute-done.3.refs_0_), channel_id=1, source_target_pairs={{0,8},{8,0},{1,9},{9,1},{2,10},{10,2},{3,11},{11,3},{4,12},{12,4},... | collective-permute-start | bytes 196616 | tf_op jit(solution)/shard_map/ppermute | solution.py:461
  26.8 1.3 %collective-permute-start.9 = (bf16[32,1024]{1,0:T(8,128)(2,1)S(1)}, bf16[32,1024]{1,0:T(8,128)(2,1)S(1)}, u32[]{:S(2)}, u32[]{:S(2)}) collective-permute-start(bf16[32,1024]{1,0:T(8,128)(2,1)S(1)} %collective-permute-done.7.refs_1_), channel_id=1, source_target_pairs={{0,8},{8,0},{1,9},{9,1},{2,10},{10,2},{3,11},{11,3},{4,12},{12,4},... | collective-permute-start | bytes 196616 | tf_op jit(solution)/shard_map/ppermute | solution.py:461

commit v5 on v4

--- a/solution.py
+++ b/solution.py
@@ -417,11 +417,11 @@
     count = total // PANEL
     inside = pl.BlockSpec(memory_space=pltpu.VMEM)
     talls, early = [], []
-    near = len(mine) // 3
-    for span in (slice(0, near), slice(near, -2)):
+    near = count // 2 - 1
+    for span in (slice(0, near), slice(near, -1)):
         ordered, talls = add_gram(mine[span] + other[span], talls)
         early.append(ordered)
-    last = mine[-2:] + other[-2:]
+    last = mine[-1:] + other[-1:]
     last_rows = sum(block.shape[0] for block in last)
     own_rows = sum(block.shape[0] for block in mine)
     return pl.pallas_call(
@@ -448,9 +448,7 @@
         ahead = lax.ppermute(ahead, axis, onward)
         behind = lax.ppermute(behind, axis, back)
         blocks += [ahead, behind]
-    middle = block.shape[0] // 2
-    blocks.append(lax.ppermute(ahead[:middle], axis, onward))
-    blocks.append(lax.ppermute(behind[middle:], axis, back))
+    blocks.append(lax.ppermute(ahead, axis, onward))
     return blocks
 
 

time: 40.9 us -> 40 us (0.978)
  waiting for transfers between devices: 13 us -> 11.6 us
  local copies, waits for them, and re-layouts: 0.02 us -> 0.9 us
    ppermute x2 -> x1, waiting for transfers between devices: 2.79 us -> 1.71 us  [ring_gather(): blocks.append(lax.ppermute(ahead, axis, onward))]
    ppermute x3, waiting for transfers between devices: 1.79 us -> 0.87 us  [ring_gather(): behind = lax.ppermute(behind, axis, back)]
    unnamed x2, local copies, waits for them, and re-layouts: 0.01 us -> 0.9 us
    ppermute x3, waiting for transfers between devices: 8.43 us -> 9 us  [ring_gather(): ahead = lax.ppermute(ahead, axis, onward)]
    ppermute x2 -> x1, starting transfers between devices: 2.08 us -> 1.8 us  [ring_gather(): blocks.append(lax.ppermute(ahead, axis, onward))]
    ppermute x9 -> x8, starting transfers between devices: 1.1 us -> 1.1 us  [gathered_rounds(): other.append(lax.ppermute(block, 'grp', [(0, 1), (1, 0)]))]
  transfers between devices with their start and end apart: 17 -> 15, of which waited for: 6 -> 5; matrix products, arithmetic and copies ran while one was open for 0% -> 0% of each run, Pallas kernels for 6% -> 6%
where the time goes in v5:
time: 40 us; the launch traced here: 39.9 us
  Pallas kernels  17.3 us (43%)
  waiting for transfers between devices  11.6 us (29%)
  starting transfers between devices  10.1 us (25%)
  local copies, waits for them, and re-layouts  0.9 us (2%)
    pallas_call x1, Pallas kernels, all_rounds(): pl.pallas_call(functools.partial(rounds_kernel, count, len(last)), out_sh...  12.6 us
    ppermute x3, waiting for transfers between devices, ring_gather(): ahead = lax.ppermute(ahead, axis, onward)  9 us
    ppermute x3, starting transfers between devices, ring_gather(): ahead = lax.ppermute(ahead, axis, onward)  6.7 us
    pallas_call x1, Pallas kernels, sketch_local(): pl.pallas_call(sketch_kernel, out_shape=jax.ShapeDtypeStruct((KB, columns...  2.39 us
    pallas_call x2, Pallas kernels, add_gram(): pl.pallas_call(functools.partial(gram_kernel, count, len(blocks)), out_sh...  2.31 us
    ppermute x1, starting transfers between devices, ring_gather(): blocks.append(lax.ppermute(ahead, axis, onward))  1.8 us
    ppermute x1, waiting for transfers between devices, ring_gather(): blocks.append(lax.ppermute(ahead, axis, onward))  1.71 us
    ppermute x8, starting transfers between devices, gathered_rounds(): other.append(lax.ppermute(block, 'grp', [(0, 1), (1, 0)]))  1.1 us
  transfers between devices with their start and end apart: 15, of which 5 were waited for; matrix products, arithmetic and copies ran while one was open for 0% of the time, Pallas kernels for 6%

profile of v5, /device:TPU:0, one launch (start us, length us, event | category | flops | bytes accessed | tf_op | source)
XLA Modules:
  0.0 39.9 jit_solution(4404631006380828830)
XLA Ops:
  0.0 2.4 %shard_map.73.refs_0_ = bf16[64,1024]{1,0:T(8,128)(2,1)} custom-call(bf16[256,1024]{1,0:T(8,128)(2,1)} %refs_0_.1, f32[256]{0:T(256)} %refs_1_.1, bf16[1024]{0:T(1024)(128)(2,1)} %refs_2_.1, s32[2]{0:T(128)} %refs_3_.1, s32[256]{0:T(256)} %refs_4_.1, s32[256]{0:T(256)} %refs_5_.1, s32[8]{0:T(128)} %refs_6_.1), custom_call_target="tpu_custom_call" | custom-call | tf_op jit(solution)/shard_map/pallas_call | solution.py:71
  2.4 3.1 %collective-permute-start = (bf16[64,1024]{1,0:T(8,128)(2,1)}, bf16[64,1024]{1,0:T(8,128)(2,1)S(1)}, u32[]{:S(2)}, u32[]{:S(2)}) collective-permute-start(bf16[64,1024]{1,0:T(8,128)(2,1)} %shard_map.73.refs_0_), channel_id=1, source_target_pairs={{0,2},{2,4},{4,6},{6,7},{7,5},{5,3},{3,1},{1,0},{8,10},{10,12},{12... | collective-permute-start | bytes 393224 | tf_op jit(solution)/shard_map/ppermute | solution.py:448
  5.5 0.0 collective-permute-start.5
  5.5 3.6 %collective-permute-done.refs_1_ = bf16[64,1024]{1,0:T(8,128)(2,1)S(1)} collective-permute-done((bf16[64,1024]{1,0:T(8,128)(2,1)}, bf16[64,1024]{1,0:T(8,128)(2,1)S(1)}, u32[]{:S(2)}, u32[]{:S(2)}) %collective-permute-start) | collective-permute-done | bytes 131104 | tf_op jit(solution)/shard_map/ppermute | solution.py:448
  9.2 1.8 %collective-permute-start.1 = (bf16[64,1024]{1,0:T(8,128)(2,1)S(1)}, bf16[64,1024]{1,0:T(8,128)(2,1)S(1)}, u32[]{:S(2)}, u32[]{:S(2)}) collective-permute-start(bf16[64,1024]{1,0:T(8,128)(2,1)S(1)} %collective-permute-done.refs_1_), channel_id=1, source_target_pairs={{0,2},{2,4},{4,6},{6,7},{7,5},{5,3},{3,1},{1,0},{8,10},{10,12},{12... | collective-permute-start | bytes 393224 | tf_op jit(solution)/shard_map/ppermute | solution.py:448
  11.0 0.0 collective-permute-done.5.refs_2_
  11.0 0.2 collective-permute-start.9
  11.2 2.9 %collective-permute-done.1.refs_0_ = bf16[64,1024]{1,0:T(8,128)(2,1)S(1)} collective-permute-done((bf16[64,1024]{1,0:T(8,128)(2,1)S(1)}, bf16[64,1024]{1,0:T(8,128)(2,1)S(1)}, u32[]{:S(2)}, u32[]{:S(2)}) %collective-permute-start.1) | collective-permute-done | bytes 131104 | tf_op jit(solution)/shard_map/ppermute | solution.py:448
  14.1 1.8 %collective-permute-start.2 = (bf16[64,1024]{1,0:T(8,128)(2,1)S(1)}, bf16[64,1024]{1,0:T(8,128)(2,1)S(1)}, u32[]{:S(2)}, u32[]{:S(2)}) collective-permute-start(bf16[64,1024]{1,0:T(8,128)(2,1)S(1)} %collective-permute-done.1.refs_0_), channel_id=1, source_target_pairs={{0,2},{2,4},{4,6},{6,7},{7,5},{5,3},{3,1},{1,0},{8,10},{10,12},{12... | collective-permute-start | bytes 393224 | tf_op jit(solution)/shard_map/ppermute | solution.py:448
  15.9 0.0 collective-permute-start.6
  15.9 0.5 %collective-permute-start.7 = (bf16[64,1024]{1,0:T(8,128)(2,1)S(1)}, bf16[64,1024]{1,0:T(8,128)(2,1)S(1)}, u32[]{:S(2)}, u32[]{:S(2)}) collective-permute-start(bf16[64,1024]{1,0:T(8,128)(2,1)S(1)} %collective-permute-done.refs_1_), channel_id=1, source_target_pairs={{0,8},{8,0},{1,9},{9,1},{2,10},{10,2},{3,11},{11,3},{4,12},{12,4},... | collective-permute-start | bytes 393224 | tf_op jit(solution)/shard_map/ppermute | solution.py:459
  16.4 0.0 collective-permute-start.8
  16.4 0.0 collective-permute-done.9.refs_1_
  16.4 0.2 collective-permute-start.10
  16.7 2.4 %collective-permute-done.2.refs_2_ = bf16[64,1024]{1,0:T(8,128)(2,1)S(1)} collective-permute-done((bf16[64,1024]{1,0:T(8,128)(2,1)S(1)}, bf16[64,1024]{1,0:T(8,128)(2,1)S(1)}, u32[]{:S(2)}, u32[]{:S(2)}) %collective-permute-start.2) | collective-permute-done | bytes 131104 | tf_op jit(solution)/shard_map/ppermute | solution.py:448
  19.1 1.8 %collective-permute-start.3 = (bf16[64,1024]{1,0:T(8,128)(2,1)S(1)}, bf16[64,1024]{1,0:T(8,128)(2,1)S(1)}, u32[]{:S(2)}, u32[]{:S(2)}) collective-permute-start(bf16[64,1024]{1,0:T(8,128)(2,1)S(1)} %collective-permute-done.2.refs_2_), channel_id=1, source_target_pairs={{0,2},{2,4},{4,6},{6,7},{7,5},{5,3},{3,1},{1,0},{8,10},{10,12},{12... | collective-permute-start | bytes 393224 | tf_op jit(solution)/shard_map/ppermute | solution.py:451
  20.9 0.0 collective-permute-done.6.refs_3_
  20.9 0.0 collective-permute-start.11
  20.9 0.0 collective-permute-done.7.refs_4_
  20.9 0.5 %collective-permute-start.12 = (bf16[64,1024]{1,0:T(8,128)(2,1)S(1)}, bf16[64,1024]{1,0:T(8,128)(2,1)S(1)}, u32[]{:S(2)}, u32[]{:S(2)}) collective-permute-start(bf16[64,1024]{1,0:T(8,128)(2,1)S(1)} %collective-permute-done.9.refs_1_), channel_id=1, source_target_pairs={{0,8},{8,0},{1,9},{9,1},{2,10},{10,2},{3,11},{11,3},{4,12},{12,4},... | collective-permute-start | bytes 393224 | tf_op jit(solution)/shard_map/ppermute | solution.py:459
  21.4 0.0 collective-permute-done.8.refs_5_
  21.4 0.1 collective-permute-start.13
  21.5 0.9 %collective-permute-done.10.refs_3_ = bf16[64,1024]{1,0:T(8,128)(2,1)S(1)} collective-permute-done((bf16[64,1024]{1,0:T(8,128)(2,1)S(1)}, bf16[64,1024]{1,0:T(8,128)(2,1)S(1)}, u32[]{:S(2)}, u32[]{:S(2)}) %collective-permute-start.10) | collective-permute-done | bytes 131104 | tf_op jit(solution)/shard_map/ppermute | solution.py:449
  22.3 0.0 collective-permute-start.14
  22.4 1.7 %collective-permute-done.3.refs_0_ = bf16[64,1024]{1,0:T(8,128)(2,1)S(1)} collective-permute-done((bf16[64,1024]{1,0:T(8,128)(2,1)S(1)}, bf16[64,1024]{1,0:T(8,128)(2,1)S(1)}, u32[]{:S(2)}, u32[]{:S(2)}) %collective-permute-start.3) | collective-permute-done | bytes 131104 | tf_op jit(solution)/shard_map/ppermute | solution.py:451
  24.1 0.0 collective-permute-start.4
  24.1 0.0 copy-start
  24.1 0.9 %copy-done = bf16[64,1024]{1,0:T(8,128)(2,1)S(1)} copy-done((bf16[64,1024]{1,0:T(8,128)(2,1)S(1)}, bf16[64,1024]{1,0:T(8,128)(2,1)}, u32[]{:S(2)}) %copy-start) | copy-done | bytes 131096
  25.0 1.0 %shard_map.74 = (bf16[384,1024]{1,0:T(8,128)(2,1)S(1)}, f32[256,256]{1,0:T(8,128)S(1)}, f32[512,256]{1,0:T(8,128)S(1)}, f32[768,256]{1,0:T(8,128)S(1)}, f32[1024,256]{1,0:T(8,128)S(1)}) custom-call(bf16[64,1024]{1,0:T(8,128)(2,1)S(1)} %copy-done, bf16[64,1024]{1,0:T(8,128)(2,1)S(1)} %collective-permute-done.refs_1_, ...), custom_call_target="tpu_custom_call" | custom-call | flops 805306368 | bytes 4718592 | tf_op jit(solution)/shard_map/pallas_call | solution.py:394
  26.0 0.0 collective-permute-done.11.refs_4_
  26.0 0.0 collective-permute-done.12.refs_5_
  26.0 0.0 collective-permute-done.13.refs_6_
  26.0 0.0 collective-permute-done.14.refs_7_
  26.0 1.3 %shard_map.75 = (bf16[512,1024]{1,0:T(8,128)(2,1)S(1)}, f32[256,256]{1,0:T(8,128)S(1)}, f32[512,256]{1,0:T(8,128)S(1)}, f32[768,256]{1,0:T(8,128)S(1)}, f32[1024,256]{1,0:T(8,128)S(1)}) custom-call(bf16[64,1024]{1,0:T(8,128)(2,1)S(1)} %collective-permute-done.1.refs_0_, ...), custom_call_target="tpu_custom_call", output_to_operand_aliasing={{1}: (8, {}), {2}: (9, {}), {3}: (10, {}), {4}: (11, {})} | custom-call | flops 1073741824 | bytes 5242880 | tf_op jit(solution)/shard_map/pallas_call | solution.py:394
  27.3 0.0 collective-permute-done.4.refs_1_
  27.3 12.6 %shard_map.76 = f32[512,128]{1,0:T(8,128)} custom-call(bf16[64,1024]{1,0:T(8,128)(2,1)S(1)} %collective-permute-done.3.refs_0_, bf16[64,1024]{1,0:T(8,128)(2,1)S(1)} %collective-permute-done.4.refs_1_, bf16[384,1024]{1,0:T(8,128)(2,1)S(1)} %get-tuple-element.15.refs_2_, bf16[512,1024]{1,0:T(8,128)(2,1)S(1)} %get-tuple-element.20.refs_3_, ...), custom_call_target="tpu_custom_call" | custom-call | tf_op jit(solution)/shard_map/pallas_call | solution.py:427
Async XLA Ops:
  2.4 6.8 %collective-permute-start = (bf16[64,1024]{1,0:T(8,128)(2,1)}, bf16[64,1024]{1,0:T(8,128)(2,1)S(1)}, u32[]{:S(2)}, u32[]{:S(2)}) collective-permute-start(bf16[64,1024]{1,0:T(8,128)(2,1)} %shard_map.73.refs_0_), channel_id=1, source_target_pairs={{0,2},{2,4},{4,6},{6,7},{7,5},{5,3},{3,1},{1,0},{8,10},{10,12},{12... | collective-permute-start | bytes 393224 | tf_op jit(solution)/shard_map/ppermute | solution.py:448
  5.5 5.5 %collective-permute-start.5 = (bf16[64,1024]{1,0:T(8,128)(2,1)}, bf16[64,1024]{1,0:T(8,128)(2,1)S(1)}, u32[]{:S(2)}, u32[]{:S(2)}) collective-permute-start(bf16[64,1024]{1,0:T(8,128)(2,1)} %shard_map.73.refs_0_), channel_id=1, source_target_pairs={{2,0},{4,2},{6,4},{7,6},{5,7},{3,5},{1,3},{0,1},{10,8},{12,10},{14... | collective-permute-start | bytes 393224 | tf_op jit(solution)/shard_map/ppermute | solution.py:449
  9.2 5.0 %collective-permute-start.1 = (bf16[64,1024]{1,0:T(8,128)(2,1)S(1)}, bf16[64,1024]{1,0:T(8,128)(2,1)S(1)}, u32[]{:S(2)}, u32[]{:S(2)}) collective-permute-start(bf16[64,1024]{1,0:T(8,128)(2,1)S(1)} %collective-permute-done.refs_1_), channel_id=1, source_target_pairs={{0,2},{2,4},{4,6},{6,7},{7,5},{5,3},{3,1},{1,0},{8,10},{10,12},{12... | collective-permute-start | bytes 393224 | tf_op jit(solution)/shard_map/ppermute | solution.py:448
  11.0 5.5 %collective-permute-start.9 = (bf16[64,1024]{1,0:T(8,128)(2,1)S(1)}, bf16[64,1024]{1,0:T(8,128)(2,1)S(1)}, u32[]{:S(2)}, u32[]{:S(2)}) collective-permute-start(bf16[64,1024]{1,0:T(8,128)(2,1)S(1)} %collective-permute-done.5.refs_2_), channel_id=1, source_target_pairs={{2,0},{4,2},{6,4},{7,6},{5,7},{3,5},{1,3},{0,1},{10,8},{12,10},{14... | collective-permute-start | bytes 393224 | tf_op jit(solution)/shard_map/ppermute | solution.py:449
  14.1 5.0 %collective-permute-start.2 = (bf16[64,1024]{1,0:T(8,128)(2,1)S(1)}, bf16[64,1024]{1,0:T(8,128)(2,1)S(1)}, u32[]{:S(2)}, u32[]{:S(2)}) collective-permute-start(bf16[64,1024]{1,0:T(8,128)(2,1)S(1)} %collective-permute-done.1.refs_0_), channel_id=1, source_target_pairs={{0,2},{2,4},{4,6},{6,7},{7,5},{5,3},{3,1},{1,0},{8,10},{10,12},{12... | collective-permute-start | bytes 393224 | tf_op jit(solution)/shard_map/ppermute | solution.py:448
  15.9 5.0 %collective-permute-start.6 = (bf16[64,1024]{1,0:T(8,128)(2,1)}, bf16[64,1024]{1,0:T(8,128)(2,1)S(1)}, u32[]{:S(2)}, u32[]{:S(2)}) collective-permute-start(bf16[64,1024]{1,0:T(8,128)(2,1)} %shard_map.73.refs_0_), channel_id=1, source_target_pairs={{0,8},{8,0},{1,9},{9,1},{2,10},{10,2},{3,11},{11,3},{4,12},{12,4},... | collective-permute-start | bytes 393224 | tf_op jit(solution)/shard_map/ppermute | solution.py:459
  15.9 5.0 %collective-permute-start.7 = (bf16[64,1024]{1,0:T(8,128)(2,1)S(1)}, bf16[64,1024]{1,0:T(8,128)(2,1)S(1)}, u32[]{:S(2)}, u32[]{:S(2)}) collective-permute-start(bf16[64,1024]{1,0:T(8,128)(2,1)S(1)} %collective-permute-done.refs_1_), channel_id=1, source_target_pairs={{0,8},{8,0},{1,9},{9,1},{2,10},{10,2},{3,11},{11,3},{4,12},{12,4},... | collective-permute-start | bytes 393224 | tf_op jit(solution)/shard_map/ppermute | solution.py:459
  16.4 5.0 %collective-permute-start.8 = (bf16[64,1024]{1,0:T(8,128)(2,1)S(1)}, bf16[64,1024]{1,0:T(8,128)(2,1)S(1)}, u32[]{:S(2)}, u32[]{:S(2)}) collective-permute-start(bf16[64,1024]{1,0:T(8,128)(2,1)S(1)} %collective-permute-done.5.refs_2_), channel_id=1, source_target_pairs={{0,8},{8,0},{1,9},{9,1},{2,10},{10,2},{3,11},{11,3},{4,12},{12,4},... | collective-permute-start | bytes 393224 | tf_op jit(solution)/shard_map/ppermute | solution.py:459
  16.4 5.9 %collective-permute-start.10 = (bf16[64,1024]{1,0:T(8,128)(2,1)S(1)}, bf16[64,1024]{1,0:T(8,128)(2,1)S(1)}, u32[]{:S(2)}, u32[]{:S(2)}) collective-permute-start(bf16[64,1024]{1,0:T(8,128)(2,1)S(1)} %collective-permute-done.9.refs_1_), channel_id=1, source_target_pairs={{2,0},{4,2},{6,4},{7,6},{5,7},{3,5},{1,3},{0,1},{10,8},{12,10},{14... | collective-permute-start | bytes 393224 | tf_op jit(solution)/shard_map/ppermute | solution.py:449
  19.1 5.0 %collective-permute-start.3 = (bf16[64,1024]{1,0:T(8,128)(2,1)S(1)}, bf16[64,1024]{1,0:T(8,128)(2,1)S(1)}, u32[]{:S(2)}, u32[]{:S(2)}) collective-permute-start(bf16[64,1024]{1,0:T(8,128)(2,1)S(1)} %collective-permute-done.2.refs_2_), channel_id=1, source_target_pairs={{0,2},{2,4},{4,6},{6,7},{7,5},{5,3},{3,1},{1,0},{8,10},{10,12},{12... | collective-permute-start | bytes 393224 | tf_op jit(solution)/shard_map/ppermute | solution.py:451
  20.9 5.1 %collective-permute-start.11 = (bf16[64,1024]{1,0:T(8,128)(2,1)S(1)}, bf16[64,1024]{1,0:T(8,128)(2,1)S(1)}, u32[]{:S(2)}, u32[]{:S(2)}) collective-permute-start(bf16[64,1024]{1,0:T(8,128)(2,1)S(1)} %collective-permute-done.1.refs_0_), channel_id=1, source_target_pairs={{0,8},{8,0},{1,9},{9,1},{2,10},{10,2},{3,11},{11,3},{4,12},{12,4},... | collective-permute-start | bytes 393224 | tf_op jit(solution)/shard_map/ppermute | solution.py:459
  20.9 5.1 %collective-permute-start.12 = (bf16[64,1024]{1,0:T(8,128)(2,1)S(1)}, bf16[64,1024]{1,0:T(8,128)(2,1)S(1)}, u32[]{:S(2)}, u32[]{:S(2)}) collective-permute-start(bf16[64,1024]{1,0:T(8,128)(2,1)S(1)} %collective-permute-done.9.refs_1_), channel_id=1, source_target_pairs={{0,8},{8,0},{1,9},{9,1},{2,10},{10,2},{3,11},{11,3},{4,12},{12,4},... | collective-permute-start | bytes 393224 | tf_op jit(solution)/shard_map/ppermute | solution.py:459
  21.4 4.6 %collective-permute-start.13 = (bf16[64,1024]{1,0:T(8,128)(2,1)S(1)}, bf16[64,1024]{1,0:T(8,128)(2,1)S(1)}, u32[]{:S(2)}, u32[]{:S(2)}) collective-permute-start(bf16[64,1024]{1,0:T(8,128)(2,1)S(1)} %collective-permute-done.2.refs_2_), channel_id=1, source_target_pairs={{0,8},{8,0},{1,9},{9,1},{2,10},{10,2},{3,11},{11,3},{4,12},{12,4},... | collective-permute-start | bytes 393224 | tf_op jit(solution)/shard_map/ppermute | solution.py:459
  22.3 3.7 %collective-permute-start.14 = (bf16[64,1024]{1,0:T(8,128)(2,1)S(1)}, bf16[64,1024]{1,0:T(8,128)(2,1)S(1)}, u32[]{:S(2)}, u32[]{:S(2)}) collective-permute-start(bf16[64,1024]{1,0:T(8,128)(2,1)S(1)} %collective-permute-done.10.refs_3_), channel_id=1, source_target_pairs={{0,8},{8,0},{1,9},{9,1},{2,10},{10,2},{3,11},{11,3},{4,12},{12,4},... | collective-permute-start | bytes 393224 | tf_op jit(solution)/shard_map/ppermute | solution.py:459
  24.1 3.3 %collective-permute-start.4 = (bf16[64,1024]{1,0:T(8,128)(2,1)S(1)}, bf16[64,1024]{1,0:T(8,128)(2,1)S(1)}, u32[]{:S(2)}, u32[]{:S(2)}) collective-permute-start(bf16[64,1024]{1,0:T(8,128)(2,1)S(1)} %collective-permute-done.3.refs_0_), channel_id=1, source_target_pairs={{0,8},{8,0},{1,9},{9,1},{2,10},{10,2},{3,11},{11,3},{4,12},{12,4},... | collective-permute-start | bytes 393224 | tf_op jit(solution)/shard_map/ppermute | solution.py:459
  24.1 0.9 %copy-start = (bf16[64,1024]{1,0:T(8,128)(2,1)S(1)}, bf16[64,1024]{1,0:T(8,128)(2,1)}, u32[]{:S(2)}) copy-start(bf16[64,1024]{1,0:T(8,128)(2,1)} %shard_map.73.refs_0_) | copy-start | bytes 393220

commit v6 on v5

--- a/solution.py
+++ b/solution.py
@@ -273,9 +273,9 @@
         offs = [
             joined(pair, pair, lambda block: jnp.where(eye, 0.0, block)) for pair in pairs
         ]
-        factors = root_factors(whole, offs)
         if finish is not None:
             finish()
+        factors = root_factors(whole, offs)
         keep = live[turn + 1]
         scales = {}
         if turn + 1 < ROUNDS:
@@ -284,11 +284,16 @@
                 slice(k[0] * width, (k[-1] + 1) * width) for k in kept
             ]
             fresh, row_scale, column_scale = {}, {}, {}
+            sides = [
+                off[span] + e[span] + mul(thin[span], half(off))
+                for off, span, (_, e, thin) in zip(offs, spans, factors)
+            ]
+            values = [
+                side[:, span] + e[span, span] + mul(half(side), thin[:, span])
+                for side, span, (_, e, thin) in zip(sides, spans, factors)
+            ]
             for i, pair in enumerate(pairs):
-                z, e, thin = factors[i]
-                span = spans[i]
-                part = offs[i][span] + e[span] + mul(thin[span], half(offs[i]))
-                value = part[:, span] + e[span, span] + mul(half(part), thin[:, span])
+                z, value = factors[i][0], values[i]
                 for k, at in enumerate(kept[i]):
                     cut = slice(k * width, (k + 1) * width)
                     block = value[cut, cut] + jnp.where(eye, 1.0, 0.0)

time: 40 us -> 39.6 us (0.990)
  Pallas kernels: 17.3 us -> 16.8 us
    pallas_call x1, Pallas kernels: 12.6 us -> 12.1 us  [all_rounds(): pl.pallas_call(functools.partial(rounds_kernel, count, len(last)), out_sh...]
where the time goes in v6:
time: 39.6 us; the launch traced here: 39.4 us
  Pallas kernels  16.8 us (42%)
  waiting for transfers between devices  11.6 us (29%)
  starting transfers between devices  10.1 us (26%)
  local copies, waits for them, and re-layouts  0.9 us (2%)
    pallas_call x1, Pallas kernels, all_rounds(): pl.pallas_call(functools.partial(rounds_kernel, count, len(last)), out_sh...  12.1 us
    ppermute x3, waiting for transfers between devices, ring_gather(): ahead = lax.ppermute(ahead, axis, onward)  9 us
    ppermute x3, starting transfers between devices, ring_gather(): ahead = lax.ppermute(ahead, axis, onward)  6.7 us
    pallas_call x1, Pallas kernels, sketch_local(): pl.pallas_call(sketch_kernel, out_shape=jax.ShapeDtypeStruct((KB, columns...  2.39 us
    pallas_call x2, Pallas kernels, add_gram(): pl.pallas_call(functools.partial(gram_kernel, count, len(blocks)), out_sh...  2.31 us
    ppermute x1, starting transfers between devices, ring_gather(): blocks.append(lax.ppermute(ahead, axis, onward))  1.8 us
    ppermute x1, waiting for transfers between devices, ring_gather(): blocks.append(lax.ppermute(ahead, axis, onward))  1.71 us
    ppermute x8, starting transfers between devices, gathered_rounds(): other.append(lax.ppermute(block, 'grp', [(0, 1), (1, 0)]))  1.1 us
  transfers between devices with their start and end apart: 15, of which 5 were waited for; matrix products, arithmetic and copies ran while one was open for 0% of the time, Pallas kernels for 6%

profile of v6, /device:TPU:0, one launch (start us, length us, event | category | flops | bytes accessed | tf_op | source)
XLA Modules:
  0.0 39.4 jit_solution(14330028346383110098)
XLA Ops:
  0.0 2.4 %shard_map.73.refs_0_ = bf16[64,1024]{1,0:T(8,128)(2,1)} custom-call(bf16[256,1024]{1,0:T(8,128)(2,1)} %refs_0_.1, f32[256]{0:T(256)} %refs_1_.1, bf16[1024]{0:T(1024)(128)(2,1)} %refs_2_.1, s32[2]{0:T(128)} %refs_3_.1, s32[256]{0:T(256)} %refs_4_.1, s32[256]{0:T(256)} %refs_5_.1, s32[8]{0:T(128)} %refs_6_.1), custom_call_target="tpu_custom_call" | custom-call | tf_op jit(solution)/shard_map/pallas_call | solution.py:71
  2.4 3.1 %collective-permute-start = (bf16[64,1024]{1,0:T(8,128)(2,1)}, bf16[64,1024]{1,0:T(8,128)(2,1)S(1)}, u32[]{:S(2)}, u32[]{:S(2)}) collective-permute-start(bf16[64,1024]{1,0:T(8,128)(2,1)} %shard_map.73.refs_0_), channel_id=1, source_target_pairs={{0,2},{2,4},{4,6},{6,7},{7,5},{5,3},{3,1},{1,0},{8,10},{10,12},{12... | collective-permute-start | bytes 393224 | tf_op jit(solution)/shard_map/ppermute | solution.py:453
  5.5 0.0 collective-permute-start.5
  5.5 3.6 %collective-permute-done.refs_1_ = bf16[64,1024]{1,0:T(8,128)(2,1)S(1)} collective-permute-done((bf16[64,1024]{1,0:T(8,128)(2,1)}, bf16[64,1024]{1,0:T(8,128)(2,1)S(1)}, u32[]{:S(2)}, u32[]{:S(2)}) %collective-permute-start) | collective-permute-done | bytes 131104 | tf_op jit(solution)/shard_map/ppermute | solution.py:453
  9.2 1.8 %collective-permute-start.1 = (bf16[64,1024]{1,0:T(8,128)(2,1)S(1)}, bf16[64,1024]{1,0:T(8,128)(2,1)S(1)}, u32[]{:S(2)}, u32[]{:S(2)}) collective-permute-start(bf16[64,1024]{1,0:T(8,128)(2,1)S(1)} %collective-permute-done.refs_1_), channel_id=1, source_target_pairs={{0,2},{2,4},{4,6},{6,7},{7,5},{5,3},{3,1},{1,0},{8,10},{10,12},{12... | collective-permute-start | bytes 393224 | tf_op jit(solution)/shard_map/ppermute | solution.py:453
  11.0 0.0 collective-permute-done.5.refs_2_
  11.0 0.2 collective-permute-start.9
  11.2 2.9 %collective-permute-done.1.refs_0_ = bf16[64,1024]{1,0:T(8,128)(2,1)S(1)} collective-permute-done((bf16[64,1024]{1,0:T(8,128)(2,1)S(1)}, bf16[64,1024]{1,0:T(8,128)(2,1)S(1)}, u32[]{:S(2)}, u32[]{:S(2)}) %collective-permute-start.1) | collective-permute-done | bytes 131104 | tf_op jit(solution)/shard_map/ppermute | solution.py:453
  14.1 1.8 %collective-permute-start.2 = (bf16[64,1024]{1,0:T(8,128)(2,1)S(1)}, bf16[64,1024]{1,0:T(8,128)(2,1)S(1)}, u32[]{:S(2)}, u32[]{:S(2)}) collective-permute-start(bf16[64,1024]{1,0:T(8,128)(2,1)S(1)} %collective-permute-done.1.refs_0_), channel_id=1, source_target_pairs={{0,2},{2,4},{4,6},{6,7},{7,5},{5,3},{3,1},{1,0},{8,10},{10,12},{12... | collective-permute-start | bytes 393224 | tf_op jit(solution)/shard_map/ppermute | solution.py:453
  15.9 0.0 collective-permute-start.6
  15.9 0.5 %collective-permute-start.7 = (bf16[64,1024]{1,0:T(8,128)(2,1)S(1)}, bf16[64,1024]{1,0:T(8,128)(2,1)S(1)}, u32[]{:S(2)}, u32[]{:S(2)}) collective-permute-start(bf16[64,1024]{1,0:T(8,128)(2,1)S(1)} %collective-permute-done.refs_1_), channel_id=1, source_target_pairs={{0,8},{8,0},{1,9},{9,1},{2,10},{10,2},{3,11},{11,3},{4,12},{12,4},... | collective-permute-start | bytes 393224 | tf_op jit(solution)/shard_map/ppermute | solution.py:464
  16.4 0.0 collective-permute-start.8
  16.4 0.0 collective-permute-done.9.refs_1_
  16.4 0.2 collective-permute-start.10
  16.7 2.4 %collective-permute-done.2.refs_2_ = bf16[64,1024]{1,0:T(8,128)(2,1)S(1)} collective-permute-done((bf16[64,1024]{1,0:T(8,128)(2,1)S(1)}, bf16[64,1024]{1,0:T(8,128)(2,1)S(1)}, u32[]{:S(2)}, u32[]{:S(2)}) %collective-permute-start.2) | collective-permute-done | bytes 131104 | tf_op jit(solution)/shard_map/ppermute | solution.py:453
  19.1 1.8 %collective-permute-start.3 = (bf16[64,1024]{1,0:T(8,128)(2,1)S(1)}, bf16[64,1024]{1,0:T(8,128)(2,1)S(1)}, u32[]{:S(2)}, u32[]{:S(2)}) collective-permute-start(bf16[64,1024]{1,0:T(8,128)(2,1)S(1)} %collective-permute-done.2.refs_2_), channel_id=1, source_target_pairs={{0,2},{2,4},{4,6},{6,7},{7,5},{5,3},{3,1},{1,0},{8,10},{10,12},{12... | collective-permute-start | bytes 393224 | tf_op jit(solution)/shard_map/ppermute | solution.py:456
  20.9 0.0 collective-permute-done.6.refs_3_
  20.9 0.0 collective-permute-start.11
  20.9 0.0 collective-permute-done.7.refs_4_
  20.9 0.5 %collective-permute-start.12 = (bf16[64,1024]{1,0:T(8,128)(2,1)S(1)}, bf16[64,1024]{1,0:T(8,128)(2,1)S(1)}, u32[]{:S(2)}, u32[]{:S(2)}) collective-permute-start(bf16[64,1024]{1,0:T(8,128)(2,1)S(1)} %collective-permute-done.9.refs_1_), channel_id=1, source_target_pairs={{0,8},{8,0},{1,9},{9,1},{2,10},{10,2},{3,11},{11,3},{4,12},{12,4},... | collective-permute-start | bytes 393224 | tf_op jit(solution)/shard_map/ppermute | solution.py:464
  21.4 0.0 collective-permute-done.8.refs_5_
  21.4 0.1 collective-permute-start.13
  21.5 0.9 %collective-permute-done.10.refs_3_ = bf16[64,1024]{1,0:T(8,128)(2,1)S(1)} collective-permute-done((bf16[64,1024]{1,0:T(8,128)(2,1)S(1)}, bf16[64,1024]{1,0:T(8,128)(2,1)S(1)}, u32[]{:S(2)}, u32[]{:S(2)}) %collective-permute-start.10) | collective-permute-done | bytes 131104 | tf_op jit(solution)/shard_map/ppermute | solution.py:454
  22.3 0.0 collective-permute-start.14
  22.4 1.7 %collective-permute-done.3.refs_0_ = bf16[64,1024]{1,0:T(8,128)(2,1)S(1)} collective-permute-done((bf16[64,1024]{1,0:T(8,128)(2,1)S(1)}, bf16[64,1024]{1,0:T(8,128)(2,1)S(1)}, u32[]{:S(2)}, u32[]{:S(2)}) %collective-permute-start.3) | collective-permute-done | bytes 131104 | tf_op jit(solution)/shard_map/ppermute | solution.py:456
  24.1 0.0 collective-permute-start.4
  24.1 0.0 copy-start
  24.1 0.9 %copy-done = bf16[64,1024]{1,0:T(8,128)(2,1)S(1)} copy-done((bf16[64,1024]{1,0:T(8,128)(2,1)S(1)}, bf16[64,1024]{1,0:T(8,128)(2,1)}, u32[]{:S(2)}) %copy-start) | copy-done | bytes 131096
  25.0 1.0 %shard_map.74 = (bf16[384,1024]{1,0:T(8,128)(2,1)S(1)}, f32[256,256]{1,0:T(8,128)S(1)}, f32[512,256]{1,0:T(8,128)S(1)}, f32[768,256]{1,0:T(8,128)S(1)}, f32[1024,256]{1,0:T(8,128)S(1)}) custom-call(bf16[64,1024]{1,0:T(8,128)(2,1)S(1)} %copy-done, bf16[64,1024]{1,0:T(8,128)(2,1)S(1)} %collective-permute-done.refs_1_, ...), custom_call_target="tpu_custom_call" | custom-call | flops 805306368 | bytes 4718592 | tf_op jit(solution)/shard_map/pallas_call | solution.py:399
  26.0 0.0 collective-permute-done.11.refs_4_
  26.0 0.0 collective-permute-done.12.refs_5_
  26.0 0.0 collective-permute-done.13.refs_6_
  26.0 0.0 collective-permute-done.14.refs_7_
  26.0 1.3 %shard_map.75 = (bf16[512,1024]{1,0:T(8,128)(2,1)S(1)}, f32[256,256]{1,0:T(8,128)S(1)}, f32[512,256]{1,0:T(8,128)S(1)}, f32[768,256]{1,0:T(8,128)S(1)}, f32[1024,256]{1,0:T(8,128)S(1)}) custom-call(bf16[64,1024]{1,0:T(8,128)(2,1)S(1)} %collective-permute-done.1.refs_0_, ...), custom_call_target="tpu_custom_call", output_to_operand_aliasing={{1}: (8, {}), {2}: (9, {}), {3}: (10, {}), {4}: (11, {})} | custom-call | flops 1073741824 | bytes 5242880 | tf_op jit(solution)/shard_map/pallas_call | solution.py:399
  27.3 0.0 collective-permute-done.4.refs_1_
  27.3 12.1 %shard_map.76 = f32[512,128]{1,0:T(8,128)} custom-call(bf16[64,1024]{1,0:T(8,128)(2,1)S(1)} %collective-permute-done.3.refs_0_, bf16[64,1024]{1,0:T(8,128)(2,1)S(1)} %collective-permute-done.4.refs_1_, bf16[384,1024]{1,0:T(8,128)(2,1)S(1)} %get-tuple-element.15.refs_2_, bf16[512,1024]{1,0:T(8,128)(2,1)S(1)} %get-tuple-element.20.refs_3_, ...), custom_call_target="tpu_custom_call" | custom-call | tf_op jit(solution)/shard_map/pallas_call | solution.py:432
Async XLA Ops:
  2.4 6.8 %collective-permute-start = (bf16[64,1024]{1,0:T(8,128)(2,1)}, bf16[64,1024]{1,0:T(8,128)(2,1)S(1)}, u32[]{:S(2)}, u32[]{:S(2)}) collective-permute-start(bf16[64,1024]{1,0:T(8,128)(2,1)} %shard_map.73.refs_0_), channel_id=1, source_target_pairs={{0,2},{2,4},{4,6},{6,7},{7,5},{5,3},{3,1},{1,0},{8,10},{10,12},{12... | collective-permute-start | bytes 393224 | tf_op jit(solution)/shard_map/ppermute | solution.py:453
  5.5 5.5 %collective-permute-start.5 = (bf16[64,1024]{1,0:T(8,128)(2,1)}, bf16[64,1024]{1,0:T(8,128)(2,1)S(1)}, u32[]{:S(2)}, u32[]{:S(2)}) collective-permute-start(bf16[64,1024]{1,0:T(8,128)(2,1)} %shard_map.73.refs_0_), channel_id=1, source_target_pairs={{2,0},{4,2},{6,4},{7,6},{5,7},{3,5},{1,3},{0,1},{10,8},{12,10},{14... | collective-permute-start | bytes 393224 | tf_op jit(solution)/shard_map/ppermute | solution.py:454
  9.2 5.0 %collective-permute-start.1 = (bf16[64,1024]{1,0:T(8,128)(2,1)S(1)}, bf16[64,1024]{1,0:T(8,128)(2,1)S(1)}, u32[]{:S(2)}, u32[]{:S(2)}) collective-permute-start(bf16[64,1024]{1,0:T(8,128)(2,1)S(1)} %collective-permute-done.refs_1_), channel_id=1, source_target_pairs={{0,2},{2,4},{4,6},{6,7},{7,5},{5,3},{3,1},{1,0},{8,10},{10,12},{12... | collective-permute-start | bytes 393224 | tf_op jit(solution)/shard_map/ppermute | solution.py:453
  11.0 5.5 %collective-permute-start.9 = (bf16[64,1024]{1,0:T(8,128)(2,1)S(1)}, bf16[64,1024]{1,0:T(8,128)(2,1)S(1)}, u32[]{:S(2)}, u32[]{:S(2)}) collective-permute-start(bf16[64,1024]{1,0:T(8,128)(2,1)S(1)} %collective-permute-done.5.refs_2_), channel_id=1, source_target_pairs={{2,0},{4,2},{6,4},{7,6},{5,7},{3,5},{1,3},{0,1},{10,8},{12,10},{14... | collective-permute-start | bytes 393224 | tf_op jit(solution)/shard_map/ppermute | solution.py:454
  14.1 5.0 %collective-permute-start.2 = (bf16[64,1024]{1,0:T(8,128)(2,1)S(1)}, bf16[64,1024]{1,0:T(8,128)(2,1)S(1)}, u32[]{:S(2)}, u32[]{:S(2)}) collective-permute-start(bf16[64,1024]{1,0:T(8,128)(2,1)S(1)} %collective-permute-done.1.refs_0_), channel_id=1, source_target_pairs={{0,2},{2,4},{4,6},{6,7},{7,5},{5,3},{3,1},{1,0},{8,10},{10,12},{12... | collective-permute-start | bytes 393224 | tf_op jit(solution)/shard_map/ppermute | solution.py:453
  15.9 5.0 %collective-permute-start.6 = (bf16[64,1024]{1,0:T(8,128)(2,1)}, bf16[64,1024]{1,0:T(8,128)(2,1)S(1)}, u32[]{:S(2)}, u32[]{:S(2)}) collective-permute-start(bf16[64,1024]{1,0:T(8,128)(2,1)} %shard_map.73.refs_0_), channel_id=1, source_target_pairs={{0,8},{8,0},{1,9},{9,1},{2,10},{10,2},{3,11},{11,3},{4,12},{12,4},... | collective-permute-start | bytes 393224 | tf_op jit(solution)/shard_map/ppermute | solution.py:464
  15.9 5.0 %collective-permute-start.7 = (bf16[64,1024]{1,0:T(8,128)(2,1)S(1)}, bf16[64,1024]{1,0:T(8,128)(2,1)S(1)}, u32[]{:S(2)}, u32[]{:S(2)}) collective-permute-start(bf16[64,1024]{1,0:T(8,128)(2,1)S(1)} %collective-permute-done.refs_1_), channel_id=1, source_target_pairs={{0,8},{8,0},{1,9},{9,1},{2,10},{10,2},{3,11},{11,3},{4,12},{12,4},... | collective-permute-start | bytes 393224 | tf_op jit(solution)/shard_map/ppermute | solution.py:464
  16.4 5.0 %collective-permute-start.8 = (bf16[64,1024]{1,0:T(8,128)(2,1)S(1)}, bf16[64,1024]{1,0:T(8,128)(2,1)S(1)}, u32[]{:S(2)}, u32[]{:S(2)}) collective-permute-start(bf16[64,1024]{1,0:T(8,128)(2,1)S(1)} %collective-permute-done.5.refs_2_), channel_id=1, source_target_pairs={{0,8},{8,0},{1,9},{9,1},{2,10},{10,2},{3,11},{11,3},{4,12},{12,4},... | collective-permute-start | bytes 393224 | tf_op jit(solution)/shard_map/ppermute | solution.py:464
  16.4 5.9 %collective-permute-start.10 = (bf16[64,1024]{1,0:T(8,128)(2,1)S(1)}, bf16[64,1024]{1,0:T(8,128)(2,1)S(1)}, u32[]{:S(2)}, u32[]{:S(2)}) collective-permute-start(bf16[64,1024]{1,0:T(8,128)(2,1)S(1)} %collective-permute-done.9.refs_1_), channel_id=1, source_target_pairs={{2,0},{4,2},{6,4},{7,6},{5,7},{3,5},{1,3},{0,1},{10,8},{12,10},{14... | collective-permute-start | bytes 393224 | tf_op jit(solution)/shard_map/ppermute | solution.py:454
  19.1 5.0 %collective-permute-start.3 = (bf16[64,1024]{1,0:T(8,128)(2,1)S(1)}, bf16[64,1024]{1,0:T(8,128)(2,1)S(1)}, u32[]{:S(2)}, u32[]{:S(2)}) collective-permute-start(bf16[64,1024]{1,0:T(8,128)(2,1)S(1)} %collective-permute-done.2.refs_2_), channel_id=1, source_target_pairs={{0,2},{2,4},{4,6},{6,7},{7,5},{5,3},{3,1},{1,0},{8,10},{10,12},{12... | collective-permute-start | bytes 393224 | tf_op jit(solution)/shard_map/ppermute | solution.py:456
  20.9 5.1 %collective-permute-start.11 = (bf16[64,1024]{1,0:T(8,128)(2,1)S(1)}, bf16[64,1024]{1,0:T(8,128)(2,1)S(1)}, u32[]{:S(2)}, u32[]{:S(2)}) collective-permute-start(bf16[64,1024]{1,0:T(8,128)(2,1)S(1)} %collective-permute-done.1.refs_0_), channel_id=1, source_target_pairs={{0,8},{8,0},{1,9},{9,1},{2,10},{10,2},{3,11},{11,3},{4,12},{12,4},... | collective-permute-start | bytes 393224 | tf_op jit(solution)/shard_map/ppermute | solution.py:464
  20.9 5.1 %collective-permute-start.12 = (bf16[64,1024]{1,0:T(8,128)(2,1)S(1)}, bf16[64,1024]{1,0:T(8,128)(2,1)S(1)}, u32[]{:S(2)}, u32[]{:S(2)}) collective-permute-start(bf16[64,1024]{1,0:T(8,128)(2,1)S(1)} %collective-permute-done.9.refs_1_), channel_id=1, source_target_pairs={{0,8},{8,0},{1,9},{9,1},{2,10},{10,2},{3,11},{11,3},{4,12},{12,4},... | collective-permute-start | bytes 393224 | tf_op jit(solution)/shard_map/ppermute | solution.py:464
  21.4 4.6 %collective-permute-start.13 = (bf16[64,1024]{1,0:T(8,128)(2,1)S(1)}, bf16[64,1024]{1,0:T(8,128)(2,1)S(1)}, u32[]{:S(2)}, u32[]{:S(2)}) collective-permute-start(bf16[64,1024]{1,0:T(8,128)(2,1)S(1)} %collective-permute-done.2.refs_2_), channel_id=1, source_target_pairs={{0,8},{8,0},{1,9},{9,1},{2,10},{10,2},{3,11},{11,3},{4,12},{12,4},... | collective-permute-start | bytes 393224 | tf_op jit(solution)/shard_map/ppermute | solution.py:464
  22.3 3.7 %collective-permute-start.14 = (bf16[64,1024]{1,0:T(8,128)(2,1)S(1)}, bf16[64,1024]{1,0:T(8,128)(2,1)S(1)}, u32[]{:S(2)}, u32[]{:S(2)}) collective-permute-start(bf16[64,1024]{1,0:T(8,128)(2,1)S(1)} %collective-permute-done.10.refs_3_), channel_id=1, source_target_pairs={{0,8},{8,0},{1,9},{9,1},{2,10},{10,2},{3,11},{11,3},{4,12},{12,4},... | collective-permute-start | bytes 393224 | tf_op jit(solution)/shard_map/ppermute | solution.py:464
  24.1 3.3 %collective-permute-start.4 = (bf16[64,1024]{1,0:T(8,128)(2,1)S(1)}, bf16[64,1024]{1,0:T(8,128)(2,1)S(1)}, u32[]{:S(2)}, u32[]{:S(2)}) collective-permute-start(bf16[64,1024]{1,0:T(8,128)(2,1)S(1)} %collective-permute-done.3.refs_0_), channel_id=1, source_target_pairs={{0,8},{8,0},{1,9},{9,1},{2,10},{10,2},{3,11},{11,3},{4,12},{12,4},... | collective-permute-start | bytes 393224 | tf_op jit(solution)/shard_map/ppermute | solution.py:464
  24.1 0.9 %copy-start = (bf16[64,1024]{1,0:T(8,128)(2,1)S(1)}, bf16[64,1024]{1,0:T(8,128)(2,1)}, u32[]{:S(2)}) copy-start(bf16[64,1024]{1,0:T(8,128)(2,1)} %shard_map.73.refs_0_) | copy-start | bytes 393220

commit v7 on v6

--- a/solution.py
+++ b/solution.py
@@ -232,7 +232,7 @@
         live[turn] = sorted({a for p in live[turn + 1] for a in (p, p ^ bit)})
 
     row_scale, column_scale, total, grams = {}, {}, {}, {}
-    for b in range(0, count, 2):
+    for b in reversed(range(0, count, 2)):
         tall = tall_refs[b // 2][...] + tall_gram(turned_ref, ordered_ref, b)
         for i in range(b + 2):
             for j in range(2):
@@ -316,17 +316,24 @@
                 later.append((j, [i for i in range(j) if i not in near]))
 
             def cross(work, joined, pairs, factors, kept, spans, fresh):
+                work = [(j, members) for j, members in work if members]
+                talls = []
                 for j, members in work:
-                    if not members:
-                        continue
-                    tops = []
-                    for i in members:
-                        source = joined(pairs[i], pairs[j])
-                        tops.append(
-                            source[spans[i]] + mul(factors[i][2][spans[i]], half(source))
+                    sources = [joined(pairs[i], pairs[j]) for i in members]
+                    talls.append(
+                        jnp.concatenate(
+                            [
+                                source[spans[i]] + mul(factors[i][2][spans[i]], half(source))
+                                for i, source in zip(members, sources)
+                            ],
+                            axis=0,
                         )
-                    tall = jnp.concatenate(tops, axis=0)
-                    tall = tall[:, spans[j]] + mul(half(tall), factors[j][2][:, spans[j]])
+                    )
+                talls = [
+                    tall[:, spans[j]] + mul(half(tall), factors[j][2][:, spans[j]])
+                    for (j, _), tall in zip(work, talls)
+                ]
+                for (j, members), tall in zip(work, talls):
                     start = 0
                     for i in members:
                         for at in kept[i]:

time: 39.6 us -> 39.6 us (level)
  no operation moved by 1% of the time
where the time goes in v7:
time: 39.6 us; the launch traced here: 39.5 us
  Pallas kernels  16.8 us (42%)
  waiting for transfers between devices  11.6 us (29%)
  starting transfers between devices  10.1 us (26%)
  local copies, waits for them, and re-layouts  0.9 us (2%)
    pallas_call x1, Pallas kernels, all_rounds(): pl.pallas_call(functools.partial(rounds_kernel, count, len(last)), out_sh...  12.1 us
    ppermute x3, waiting for transfers between devices, ring_gather(): ahead = lax.ppermute(ahead, axis, onward)  9 us
    ppermute x3, starting transfers between devices, ring_gather(): ahead = lax.ppermute(ahead, axis, onward)  6.7 us
    pallas_call x1, Pallas kernels, sketch_local(): pl.pallas_call(sketch_kernel, out_shape=jax.ShapeDtypeStruct((KB, columns...  2.39 us
    pallas_call x2, Pallas kernels, add_gram(): pl.pallas_call(functools.partial(gram_kernel, count, len(blocks)), out_sh...  2.31 us
    ppermute x1, starting transfers between devices, ring_gather(): blocks.append(lax.ppermute(ahead, axis, onward))  1.8 us
    ppermute x1, waiting for transfers between devices, ring_gather(): blocks.append(lax.ppermute(ahead, axis, onward))  1.71 us
    ppermute x8, starting transfers between devices, gathered_rounds(): other.append(lax.ppermute(block, 'grp', [(0, 1), (1, 0)]))  1.1 us
  transfers between devices with their start and end apart: 15, of which 5 were waited for; matrix products, arithmetic and copies ran while one was open for 0% of the time, Pallas kernels for 6%

profile of v7, /device:TPU:0, one launch (start us, length us, event | category | flops | bytes accessed | tf_op | source)
XLA Modules:
  0.0 39.5 jit_solution(4432422815339784555)
XLA Ops:
  0.0 2.4 %shard_map.73.refs_0_ = bf16[64,1024]{1,0:T(8,128)(2,1)} custom-call(bf16[256,1024]{1,0:T(8,128)(2,1)} %refs_0_.1, f32[256]{0:T(256)} %refs_1_.1, bf16[1024]{0:T(1024)(128)(2,1)} %refs_2_.1, s32[2]{0:T(128)} %refs_3_.1, s32[256]{0:T(256)} %refs_4_.1, s32[256]{0:T(256)} %refs_5_.1, s32[8]{0:T(128)} %refs_6_.1), custom_call_target="tpu_custom_call" | custom-call | tf_op jit(solution)/shard_map/pallas_call | solution.py:71
  2.4 3.1 %collective-permute-start = (bf16[64,1024]{1,0:T(8,128)(2,1)}, bf16[64,1024]{1,0:T(8,128)(2,1)S(1)}, u32[]{:S(2)}, u32[]{:S(2)}) collective-permute-start(bf16[64,1024]{1,0:T(8,128)(2,1)} %shard_map.73.refs_0_), channel_id=1, source_target_pairs={{0,2},{2,4},{4,6},{6,7},{7,5},{5,3},{3,1},{1,0},{8,10},{10,12},{12... | collective-permute-start | bytes 393224 | tf_op jit(solution)/shard_map/ppermute | solution.py:460
  5.5 0.0 collective-permute-start.5
  5.5 3.6 %collective-permute-done.refs_1_ = bf16[64,1024]{1,0:T(8,128)(2,1)S(1)} collective-permute-done((bf16[64,1024]{1,0:T(8,128)(2,1)}, bf16[64,1024]{1,0:T(8,128)(2,1)S(1)}, u32[]{:S(2)}, u32[]{:S(2)}) %collective-permute-start) | collective-permute-done | bytes 131104 | tf_op jit(solution)/shard_map/ppermute | solution.py:460
  9.2 1.8 %collective-permute-start.1 = (bf16[64,1024]{1,0:T(8,128)(2,1)S(1)}, bf16[64,1024]{1,0:T(8,128)(2,1)S(1)}, u32[]{:S(2)}, u32[]{:S(2)}) collective-permute-start(bf16[64,1024]{1,0:T(8,128)(2,1)S(1)} %collective-permute-done.refs_1_), channel_id=1, source_target_pairs={{0,2},{2,4},{4,6},{6,7},{7,5},{5,3},{3,1},{1,0},{8,10},{10,12},{12... | collective-permute-start | bytes 393224 | tf_op jit(solution)/shard_map/ppermute | solution.py:460
  11.0 0.0 collective-permute-done.5.refs_2_
  11.0 0.2 collective-permute-start.9
  11.2 2.9 %collective-permute-done.1.refs_0_ = bf16[64,1024]{1,0:T(8,128)(2,1)S(1)} collective-permute-done((bf16[64,1024]{1,0:T(8,128)(2,1)S(1)}, bf16[64,1024]{1,0:T(8,128)(2,1)S(1)}, u32[]{:S(2)}, u32[]{:S(2)}) %collective-permute-start.1) | collective-permute-done | bytes 131104 | tf_op jit(solution)/shard_map/ppermute | solution.py:460
  14.1 1.8 %collective-permute-start.2 = (bf16[64,1024]{1,0:T(8,128)(2,1)S(1)}, bf16[64,1024]{1,0:T(8,128)(2,1)S(1)}, u32[]{:S(2)}, u32[]{:S(2)}) collective-permute-start(bf16[64,1024]{1,0:T(8,128)(2,1)S(1)} %collective-permute-done.1.refs_0_), channel_id=1, source_target_pairs={{0,2},{2,4},{4,6},{6,7},{7,5},{5,3},{3,1},{1,0},{8,10},{10,12},{12... | collective-permute-start | bytes 393224 | tf_op jit(solution)/shard_map/ppermute | solution.py:460
  15.9 0.0 collective-permute-start.6
  15.9 0.5 %collective-permute-start.7 = (bf16[64,1024]{1,0:T(8,128)(2,1)S(1)}, bf16[64,1024]{1,0:T(8,128)(2,1)S(1)}, u32[]{:S(2)}, u32[]{:S(2)}) collective-permute-start(bf16[64,1024]{1,0:T(8,128)(2,1)S(1)} %collective-permute-done.refs_1_), channel_id=1, source_target_pairs={{0,8},{8,0},{1,9},{9,1},{2,10},{10,2},{3,11},{11,3},{4,12},{12,4},... | collective-permute-start | bytes 393224 | tf_op jit(solution)/shard_map/ppermute | solution.py:471
  16.4 0.0 collective-permute-start.8
  16.4 0.0 collective-permute-done.9.refs_1_
  16.4 0.2 collective-permute-start.10
  16.7 2.4 %collective-permute-done.2.refs_2_ = bf16[64,1024]{1,0:T(8,128)(2,1)S(1)} collective-permute-done((bf16[64,1024]{1,0:T(8,128)(2,1)S(1)}, bf16[64,1024]{1,0:T(8,128)(2,1)S(1)}, u32[]{:S(2)}, u32[]{:S(2)}) %collective-permute-start.2) | collective-permute-done | bytes 131104 | tf_op jit(solution)/shard_map/ppermute | solution.py:460
  19.1 1.8 %collective-permute-start.3 = (bf16[64,1024]{1,0:T(8,128)(2,1)S(1)}, bf16[64,1024]{1,0:T(8,128)(2,1)S(1)}, u32[]{:S(2)}, u32[]{:S(2)}) collective-permute-start(bf16[64,1024]{1,0:T(8,128)(2,1)S(1)} %collective-permute-done.2.refs_2_), channel_id=1, source_target_pairs={{0,2},{2,4},{4,6},{6,7},{7,5},{5,3},{3,1},{1,0},{8,10},{10,12},{12... | collective-permute-start | bytes 393224 | tf_op jit(solution)/shard_map/ppermute | solution.py:463
  20.9 0.0 collective-permute-done.6.refs_3_
  20.9 0.0 collective-permute-start.11
  20.9 0.0 collective-permute-done.7.refs_4_
  20.9 0.5 %collective-permute-start.12 = (bf16[64,1024]{1,0:T(8,128)(2,1)S(1)}, bf16[64,1024]{1,0:T(8,128)(2,1)S(1)}, u32[]{:S(2)}, u32[]{:S(2)}) collective-permute-start(bf16[64,1024]{1,0:T(8,128)(2,1)S(1)} %collective-permute-done.9.refs_1_), channel_id=1, source_target_pairs={{0,8},{8,0},{1,9},{9,1},{2,10},{10,2},{3,11},{11,3},{4,12},{12,4},... | collective-permute-start | bytes 393224 | tf_op jit(solution)/shard_map/ppermute | solution.py:471
  21.4 0.0 collective-permute-done.8.refs_5_
  21.4 0.1 collective-permute-start.13
  21.5 0.9 %collective-permute-done.10.refs_3_ = bf16[64,1024]{1,0:T(8,128)(2,1)S(1)} collective-permute-done((bf16[64,1024]{1,0:T(8,128)(2,1)S(1)}, bf16[64,1024]{1,0:T(8,128)(2,1)S(1)}, u32[]{:S(2)}, u32[]{:S(2)}) %collective-permute-start.10) | collective-permute-done | bytes 131104 | tf_op jit(solution)/shard_map/ppermute | solution.py:461
  22.3 0.0 collective-permute-start.14
  22.4 1.7 %collective-permute-done.3.refs_0_ = bf16[64,1024]{1,0:T(8,128)(2,1)S(1)} collective-permute-done((bf16[64,1024]{1,0:T(8,128)(2,1)S(1)}, bf16[64,1024]{1,0:T(8,128)(2,1)S(1)}, u32[]{:S(2)}, u32[]{:S(2)}) %collective-permute-start.3) | collective-permute-done | bytes 131104 | tf_op jit(solution)/shard_map/ppermute | solution.py:463
  24.1 0.0 collective-permute-start.4
  24.1 0.0 copy-start
  24.1 0.9 %copy-done = bf16[64,1024]{1,0:T(8,128)(2,1)S(1)} copy-done((bf16[64,1024]{1,0:T(8,128)(2,1)S(1)}, bf16[64,1024]{1,0:T(8,128)(2,1)}, u32[]{:S(2)}) %copy-start) | copy-done | bytes 131096
  25.0 1.0 %shard_map.74 = (bf16[384,1024]{1,0:T(8,128)(2,1)S(1)}, f32[256,256]{1,0:T(8,128)S(1)}, f32[512,256]{1,0:T(8,128)S(1)}, f32[768,256]{1,0:T(8,128)S(1)}, f32[1024,256]{1,0:T(8,128)S(1)}) custom-call(bf16[64,1024]{1,0:T(8,128)(2,1)S(1)} %copy-done, bf16[64,1024]{1,0:T(8,128)(2,1)S(1)} %collective-permute-done.refs_1_, ...), custom_call_target="tpu_custom_call" | custom-call | flops 805306368 | bytes 4718592 | tf_op jit(solution)/shard_map/pallas_call | solution.py:406
  26.0 0.0 collective-permute-done.11.refs_4_
  26.0 0.0 collective-permute-done.12.refs_5_
  26.0 0.0 collective-permute-done.13.refs_6_
  26.0 0.0 collective-permute-done.14.refs_7_
  26.0 1.3 %shard_map.75 = (bf16[512,1024]{1,0:T(8,128)(2,1)S(1)}, f32[256,256]{1,0:T(8,128)S(1)}, f32[512,256]{1,0:T(8,128)S(1)}, f32[768,256]{1,0:T(8,128)S(1)}, f32[1024,256]{1,0:T(8,128)S(1)}) custom-call(bf16[64,1024]{1,0:T(8,128)(2,1)S(1)} %collective-permute-done.1.refs_0_, ...), custom_call_target="tpu_custom_call", output_to_operand_aliasing={{1}: (8, {}), {2}: (9, {}), {3}: (10, {}), {4}: (11, {})} | custom-call | flops 1073741824 | bytes 5242880 | tf_op jit(solution)/shard_map/pallas_call | solution.py:406
  27.3 0.0 collective-permute-done.4.refs_1_
  27.3 12.1 %shard_map.76 = f32[512,128]{1,0:T(8,128)} custom-call(bf16[64,1024]{1,0:T(8,128)(2,1)S(1)} %collective-permute-done.3.refs_0_, bf16[64,1024]{1,0:T(8,128)(2,1)S(1)} %collective-permute-done.4.refs_1_, bf16[384,1024]{1,0:T(8,128)(2,1)S(1)} %get-tuple-element.15.refs_2_, bf16[512,1024]{1,0:T(8,128)(2,1)S(1)} %get-tuple-element.20.refs_3_, ...), custom_call_target="tpu_custom_call" | custom-call | tf_op jit(solution)/shard_map/pallas_call | solution.py:439
Async XLA Ops:
  2.4 6.8 %collective-permute-start = (bf16[64,1024]{1,0:T(8,128)(2,1)}, bf16[64,1024]{1,0:T(8,128)(2,1)S(1)}, u32[]{:S(2)}, u32[]{:S(2)}) collective-permute-start(bf16[64,1024]{1,0:T(8,128)(2,1)} %shard_map.73.refs_0_), channel_id=1, source_target_pairs={{0,2},{2,4},{4,6},{6,7},{7,5},{5,3},{3,1},{1,0},{8,10},{10,12},{12... | collective-permute-start | bytes 393224 | tf_op jit(solution)/shard_map/ppermute | solution.py:460
  5.5 5.5 %collective-permute-start.5 = (bf16[64,1024]{1,0:T(8,128)(2,1)}, bf16[64,1024]{1,0:T(8,128)(2,1)S(1)}, u32[]{:S(2)}, u32[]{:S(2)}) collective-permute-start(bf16[64,1024]{1,0:T(8,128)(2,1)} %shard_map.73.refs_0_), channel_id=1, source_target_pairs={{2,0},{4,2},{6,4},{7,6},{5,7},{3,5},{1,3},{0,1},{10,8},{12,10},{14... | collective-permute-start | bytes 393224 | tf_op jit(solution)/shard_map/ppermute | solution.py:461
  9.2 5.0 %collective-permute-start.1 = (bf16[64,1024]{1,0:T(8,128)(2,1)S(1)}, bf16[64,1024]{1,0:T(8,128)(2,1)S(1)}, u32[]{:S(2)}, u32[]{:S(2)}) collective-permute-start(bf16[64,1024]{1,0:T(8,128)(2,1)S(1)} %collective-permute-done.refs_1_), channel_id=1, source_target_pairs={{0,2},{2,4},{4,6},{6,7},{7,5},{5,3},{3,1},{1,0},{8,10},{10,12},{12... | collective-permute-start | bytes 393224 | tf_op jit(solution)/shard_map/ppermute | solution.py:460
  11.0 5.5 %collective-permute-start.9 = (bf16[64,1024]{1,0:T(8,128)(2,1)S(1)}, bf16[64,1024]{1,0:T(8,128)(2,1)S(1)}, u32[]{:S(2)}, u32[]{:S(2)}) collective-permute-start(bf16[64,1024]{1,0:T(8,128)(2,1)S(1)} %collective-permute-done.5.refs_2_), channel_id=1, source_target_pairs={{2,0},{4,2},{6,4},{7,6},{5,7},{3,5},{1,3},{0,1},{10,8},{12,10},{14... | collective-permute-start | bytes 393224 | tf_op jit(solution)/shard_map/ppermute | solution.py:461
  14.1 5.0 %collective-permute-start.2 = (bf16[64,1024]{1,0:T(8,128)(2,1)S(1)}, bf16[64,1024]{1,0:T(8,128)(2,1)S(1)}, u32[]{:S(2)}, u32[]{:S(2)}) collective-permute-start(bf16[64,1024]{1,0:T(8,128)(2,1)S(1)} %collective-permute-done.1.refs_0_), channel_id=1, source_target_pairs={{0,2},{2,4},{4,6},{6,7},{7,5},{5,3},{3,1},{1,0},{8,10},{10,12},{12... | collective-permute-start | bytes 393224 | tf_op jit(solution)/shard_map/ppermute | solution.py:460
  15.9 5.0 %collective-permute-start.6 = (bf16[64,1024]{1,0:T(8,128)(2,1)}, bf16[64,1024]{1,0:T(8,128)(2,1)S(1)}, u32[]{:S(2)}, u32[]{:S(2)}) collective-permute-start(bf16[64,1024]{1,0:T(8,128)(2,1)} %shard_map.73.refs_0_), channel_id=1, source_target_pairs={{0,8},{8,0},{1,9},{9,1},{2,10},{10,2},{3,11},{11,3},{4,12},{12,4},... | collective-permute-start | bytes 393224 | tf_op jit(solution)/shard_map/ppermute | solution.py:471
  15.9 5.0 %collective-permute-start.7 = (bf16[64,1024]{1,0:T(8,128)(2,1)S(1)}, bf16[64,1024]{1,0:T(8,128)(2,1)S(1)}, u32[]{:S(2)}, u32[]{:S(2)}) collective-permute-start(bf16[64,1024]{1,0:T(8,128)(2,1)S(1)} %collective-permute-done.refs_1_), channel_id=1, source_target_pairs={{0,8},{8,0},{1,9},{9,1},{2,10},{10,2},{3,11},{11,3},{4,12},{12,4},... | collective-permute-start | bytes 393224 | tf_op jit(solution)/shard_map/ppermute | solution.py:471
  16.4 5.0 %collective-permute-start.8 = (bf16[64,1024]{1,0:T(8,128)(2,1)S(1)}, bf16[64,1024]{1,0:T(8,128)(2,1)S(1)}, u32[]{:S(2)}, u32[]{:S(2)}) collective-permute-start(bf16[64,1024]{1,0:T(8,128)(2,1)S(1)} %collective-permute-done.5.refs_2_), channel_id=1, source_target_pairs={{0,8},{8,0},{1,9},{9,1},{2,10},{10,2},{3,11},{11,3},{4,12},{12,4},... | collective-permute-start | bytes 393224 | tf_op jit(solution)/shard_map/ppermute | solution.py:471
  16.4 5.9 %collective-permute-start.10 = (bf16[64,1024]{1,0:T(8,128)(2,1)S(1)}, bf16[64,1024]{1,0:T(8,128)(2,1)S(1)}, u32[]{:S(2)}, u32[]{:S(2)}) collective-permute-start(bf16[64,1024]{1,0:T(8,128)(2,1)S(1)} %collective-permute-done.9.refs_1_), channel_id=1, source_target_pairs={{2,0},{4,2},{6,4},{7,6},{5,7},{3,5},{1,3},{0,1},{10,8},{12,10},{14... | collective-permute-start | bytes 393224 | tf_op jit(solution)/shard_map/ppermute | solution.py:461
  19.1 5.0 %collective-permute-start.3 = (bf16[64,1024]{1,0:T(8,128)(2,1)S(1)}, bf16[64,1024]{1,0:T(8,128)(2,1)S(1)}, u32[]{:S(2)}, u32[]{:S(2)}) collective-permute-start(bf16[64,1024]{1,0:T(8,128)(2,1)S(1)} %collective-permute-done.2.refs_2_), channel_id=1, source_target_pairs={{0,2},{2,4},{4,6},{6,7},{7,5},{5,3},{3,1},{1,0},{8,10},{10,12},{12... | collective-permute-start | bytes 393224 | tf_op jit(solution)/shard_map/ppermute | solution.py:463
  20.9 5.1 %collective-permute-start.11 = (bf16[64,1024]{1,0:T(8,128)(2,1)S(1)}, bf16[64,1024]{1,0:T(8,128)(2,1)S(1)}, u32[]{:S(2)}, u32[]{:S(2)}) collective-permute-start(bf16[64,1024]{1,0:T(8,128)(2,1)S(1)} %collective-permute-done.1.refs_0_), channel_id=1, source_target_pairs={{0,8},{8,0},{1,9},{9,1},{2,10},{10,2},{3,11},{11,3},{4,12},{12,4},... | collective-permute-start | bytes 393224 | tf_op jit(solution)/shard_map/ppermute | solution.py:471
  20.9 5.1 %collective-permute-start.12 = (bf16[64,1024]{1,0:T(8,128)(2,1)S(1)}, bf16[64,1024]{1,0:T(8,128)(2,1)S(1)}, u32[]{:S(2)}, u32[]{:S(2)}) collective-permute-start(bf16[64,1024]{1,0:T(8,128)(2,1)S(1)} %collective-permute-done.9.refs_1_), channel_id=1, source_target_pairs={{0,8},{8,0},{1,9},{9,1},{2,10},{10,2},{3,11},{11,3},{4,12},{12,4},... | collective-permute-start | bytes 393224 | tf_op jit(solution)/shard_map/ppermute | solution.py:471
  21.4 4.6 %collective-permute-start.13 = (bf16[64,1024]{1,0:T(8,128)(2,1)S(1)}, bf16[64,1024]{1,0:T(8,128)(2,1)S(1)}, u32[]{:S(2)}, u32[]{:S(2)}) collective-permute-start(bf16[64,1024]{1,0:T(8,128)(2,1)S(1)} %collective-permute-done.2.refs_2_), channel_id=1, source_target_pairs={{0,8},{8,0},{1,9},{9,1},{2,10},{10,2},{3,11},{11,3},{4,12},{12,4},... | collective-permute-start | bytes 393224 | tf_op jit(solution)/shard_map/ppermute | solution.py:471
  22.3 3.7 %collective-permute-start.14 = (bf16[64,1024]{1,0:T(8,128)(2,1)S(1)}, bf16[64,1024]{1,0:T(8,128)(2,1)S(1)}, u32[]{:S(2)}, u32[]{:S(2)}) collective-permute-start(bf16[64,1024]{1,0:T(8,128)(2,1)S(1)} %collective-permute-done.10.refs_3_), channel_id=1, source_target_pairs={{0,8},{8,0},{1,9},{9,1},{2,10},{10,2},{3,11},{11,3},{4,12},{12,4},... | collective-permute-start | bytes 393224 | tf_op jit(solution)/shard_map/ppermute | solution.py:471
  24.1 3.3 %collective-permute-start.4 = (bf16[64,1024]{1,0:T(8,128)(2,1)S(1)}, bf16[64,1024]{1,0:T(8,128)(2,1)S(1)}, u32[]{:S(2)}, u32[]{:S(2)}) collective-permute-start(bf16[64,1024]{1,0:T(8,128)(2,1)S(1)} %collective-permute-done.3.refs_0_), channel_id=1, source_target_pairs={{0,8},{8,0},{1,9},{9,1},{2,10},{10,2},{3,11},{11,3},{4,12},{12,4},... | collective-permute-start | bytes 393224 | tf_op jit(solution)/shard_map/ppermute | solution.py:471
  24.1 0.9 %copy-start = (bf16[64,1024]{1,0:T(8,128)(2,1)S(1)}, bf16[64,1024]{1,0:T(8,128)(2,1)}, u32[]{:S(2)}) copy-start(bf16[64,1024]{1,0:T(8,128)(2,1)} %shard_map.73.refs_0_) | copy-start | bytes 393220
